TPU v7x, 32 devices: a whole 2x2x4 slice. The times are simulated.
32 devices in a mesh: seq: 16 (over z, y, x), fsdp: 2 (over core).
Axes of the slice: x: 2, y: 2, z: 4, core: 2. Of those that a mesh axis runs over, the one named last changes fastest.
Arguments:
- query: bfloat16 [3072, 4096], P('seq', 'fsdp'), may hold values from -6 to 6
- key: bfloat16 [3072, 4096], P('seq', 'fsdp'), may hold values from -6 to 6
- value: bfloat16 [3072, 4096], P('seq', 'fsdp'), may hold values from -6 to 6
- grad_out: bfloat16 [3072, 4096], P('seq', 'fsdp'), may hold values from -6 to 6
- short_filter: float32 [3, 7, 4096], P(None, None, 'fsdp'), may hold values from -2 to 2
- medium_filter: float32 [256, 128], P('fsdp'), may hold values from -0.5 to 0.5
Outputs:
- grad_query: bfloat16 [3072, 4096], P('seq', 'fsdp')
- grad_key: bfloat16 [3072, 4096], P('seq', 'fsdp')
- grad_value: bfloat16 [3072, 4096], P('seq', 'fsdp')
- grad_short: float32 [3, 7, 4096], P(None, None, 'fsdp')
- grad_medium: float32 [256, 128], P('fsdp')
All inputs are finite; a program needn't handle non-finite values.
Results may differ from a plain program's by a relative error of at most 0.0075.
Values may be sent and summed in bfloat16 or wider, within the bound.
No kernel may reach another device: no remote copies, remote signals or barrier semaphores. Data moves between devices by JAX's collectives and lax.ppermute only.
A program may use at most 64 MiB of HBM per device.

v0:
```python
import jax
import jax.numpy as jnp
from jax import lax
from jax.sharding import PartitionSpec as P


def from_behind(value, axis, steps):
    count = lax.axis_size(axis)
    initial, last = (max(0, -steps), min(count, count - steps))
    return lax.ppermute(value, axis, [(source, source + steps) for source in range(initial, last)])


def depthwise(signal_in, kernel):
    result = lax.conv_general_dilated(
        signal_in[None],
        kernel[:, None, :],
        (1,),
        "VALID",
        dimension_numbers=("NWC", "WIO", "NWC"),
        feature_group_count=signal_in.shape[1],
        preferred_element_type=jnp.float32,
    )
    return result[0]


def short_causal(extended, weights):
    length = weights.shape[0]
    count = extended.shape[0] - length + 1
    total = jnp.zeros((count, extended.shape[1]), jnp.float32)
    for index in range(length):
        offset = length - 1 - index
        total = total + weights[index] * extended[offset : offset + count].astype(jnp.float32)
    return total


def short_anticausal(extended, weights):
    length = weights.shape[0]
    count = extended.shape[0] - length + 1
    total = jnp.zeros((count, extended.shape[1]), jnp.float32)
    for index in range(length):
        total = total + weights[index] * extended[index : index + count].astype(jnp.float32)
    return total


def short_gradient(gradient, extended, length):
    count = gradient.shape[0]
    grad_f = gradient.astype(jnp.float32)
    rows_list = []
    for index in range(length):
        offset = length - 1 - index
        rows_list.append(
            jnp.sum(grad_f * extended[offset : offset + count].astype(jnp.float32), axis=0)
        )
    return jnp.stack(rows_list)


def shards(query, key, value, grad_out, short_filter, medium_filter):
    positions = query.shape[0]
    channels = query.shape[1]
    length_short = short_filter.shape[1]
    length_long = medium_filter.shape[1]
    edge_short = length_short - 1
    edge_long = length_long - 1
    gathered = lax.all_gather(medium_filter.astype(jnp.bfloat16), "fsdp", axis=0, tiled=True)
    groups = gathered.shape[0]
    taps_long = jnp.tile(gathered.T, (1, channels // groups))
    prior_query, prior_key, prior_value = from_behind(
        (
            query[positions - edge_short :],
            key[positions - edge_short :],
            value[positions - edge_short :],
        ),
        "seq",
        1,
    )
    query_ext = jnp.concatenate([prior_query, query], axis=0)
    key_ext = jnp.concatenate([prior_key, key], axis=0)
    value_ext = jnp.concatenate([prior_value, value], axis=0)
    query_short = short_causal(query_ext, short_filter[0])
    key_wide = short_causal(key_ext, short_filter[1])
    value_wide = short_causal(value_ext, short_filter[2])
    gated = (key_wide * value_wide).astype(jnp.bfloat16)
    prior_gated = from_behind(gated[positions - edge_long :], "seq", 1)
    gated_ext = jnp.concatenate([prior_gated, gated], axis=0)
    flipped_taps = jnp.flip(taps_long, 0)
    signal_long = depthwise(gated_ext, flipped_taps)
    grad_f = grad_out.astype(jnp.float32)
    grad_gated_in = (grad_f * query_short).astype(jnp.bfloat16)
    grad_qshort = (grad_f * signal_long).astype(jnp.bfloat16)
    padding = jnp.zeros((edge_long, channels), jnp.bfloat16)
    inner = depthwise(jnp.concatenate([grad_gated_in, padding], axis=0), taps_long)
    key_head = (inner[:edge_short] * value_wide[:edge_short]).astype(jnp.bfloat16)
    value_head = (inner[:edge_short] * key_wide[:edge_short]).astype(jnp.bfloat16)
    next_gated, next_query, next_key, next_value = from_behind(
        (grad_gated_in[:edge_long], grad_qshort[:edge_short], key_head, value_head), "seq", -1
    )
    lags = depthwise(gated_ext, grad_gated_in)
    medium_local = jnp.flip(lags, 0).reshape(length_long, channels // groups, groups).sum(axis=1).T
    query_grad_part = short_gradient(grad_qshort, query_ext, length_short)
    edge_part = depthwise(jnp.concatenate([padding, next_gated], axis=0), taps_long)
    grad_gated = inner.at[positions - edge_long :].add(edge_part)
    grad_kshort = jnp.concatenate(
        [key_head, (grad_gated[edge_short:] * value_wide[edge_short:]).astype(jnp.bfloat16)], axis=0
    )
    grad_vshort = jnp.concatenate(
        [value_head, (grad_gated[edge_short:] * key_wide[edge_short:]).astype(jnp.bfloat16)], axis=0
    )
    grad_query = short_anticausal(
        jnp.concatenate([grad_qshort, next_query], axis=0), short_filter[0]
    ).astype(jnp.bfloat16)
    grad_key = short_anticausal(
        jnp.concatenate([grad_kshort, next_key], axis=0), short_filter[1]
    ).astype(jnp.bfloat16)
    grad_value = short_anticausal(
        jnp.concatenate([grad_vshort, next_value], axis=0), short_filter[2]
    ).astype(jnp.bfloat16)
    short_local = jnp.stack(
        [
            query_grad_part,
            short_gradient(grad_kshort, key_ext, length_short),
            short_gradient(grad_vshort, value_ext, length_short),
        ]
    )
    medium_part = lax.psum_scatter(
        medium_local.astype(jnp.bfloat16), "fsdp", scatter_dimension=0, tiled=True
    ).astype(jnp.float32)
    grad_short, grad_medium = lax.psum((short_local, medium_part), "seq")
    return (grad_query, grad_key, grad_value, grad_short, grad_medium)


def solution(mesh):
    in_specs = (
        P("seq", "fsdp"),
        P("seq", "fsdp"),
        P("seq", "fsdp"),
        P("seq", "fsdp"),
        P(None, None, "fsdp"),
        P("fsdp", None),
    )
    out_specs = (
        P("seq", "fsdp"),
        P("seq", "fsdp"),
        P("seq", "fsdp"),
        P(None, None, "fsdp"),
        P("fsdp", None),
    )
    return jax.shard_map(shards, mesh=mesh, in_specs=in_specs, out_specs=out_specs, check_vma=False)
```

profile of v0, /device:TPU:0, one launch (start us, length us, event | category | flops | bytes accessed | tf_op | source)
XLA Modules:
  0.0 362.2 jit_solution(3751491505622646079)
XLA Ops:
  8.8 4.9 %collective-permute-start.1 = (bf16[6,2048]{1,0:T(8,128)(2,1)S(1)}, bf16[6,2048]{1,0:T(8,128)(2,1)S(1)}, u32[]{:S(2)}, u32[]{:S(2)}) collective-permute-start(bf16[6,2048]{1,0:T(8,128)(2,1)S(1)} %slice.333), channel_id=1, source_target_pairs={{0,2},{2,4},{4,6},{6,8},{8,10},{10,12},{12,14},{14,16},{16,18},{18... | collective-permute-start | bytes 73736 | tf_op jit(solution)/shard_map/ppermute | solution.py:10
  14.5 3.4 collective-permute-start
  17.9 1.7 fusion.98
  19.8 8.4 %multiply_convert_fusion = (bf16[192,2048]{1,0:T(8,128)(2,1)S(1)}, f32[192,2048]{1,0:T(8,128)}, f32[192,2048]{1,0:T(8,128)}) fusion(bf16[192,2048]{1,0:T(8,128)(2,1)} %param.10, bf16[6,2048]{1,0:T(8,128)(2,1)S(1)} %collective-permute-done.1, f32[2048]{0:T(1024)S(1)} %bitcast.109, f32[2048]{0:T(1024)S(1)} %bitcast.111, f32[2048]{0:T(1024)S(1)} %bitcast.113, ...), kind=kLoop, calls=%fused_computation.143 | loop fusion | flops 30670848 | bytes 5668864 | tf_op jit(solution)/shard_map/convert_element_type | solution.py:82
  29.3 3.9 %collective-permute-start.2 = (bf16[127,2048]{1,0:T(8,128)(2,1)}, bf16[127,2048]{1,0:T(8,128)(2,1)S(1)}, u32[]{:S(2)}, u32[]{:S(2)}) collective-permute-start(bf16[127,2048]{1,0:T(8,128)(2,1)} %slice.405), channel_id=1, source_target_pairs={{0,2},{2,4},{4,6},{6,8},{8,10},{10,12},{12,14},{14,16},{16,18},{18... | collective-permute-start | bytes 1560584 | tf_op jit(solution)/shard_map/ppermute | solution.py:10
  33.2 4.3 %collective-permute-start.4 = (bf16[6,2048]{1,0:T(8,128)(2,1)S(1)}, bf16[6,2048]{1,0:T(8,128)(2,1)S(1)}, u32[]{:S(2)}, u32[]{:S(2)}) collective-permute-start(bf16[6,2048]{1,0:T(8,128)(2,1)S(1)} %slice.359), channel_id=1, source_target_pairs={{0,2},{2,4},{4,6},{6,8},{8,10},{10,12},{12,14},{14,16},{16,18},{18... | collective-permute-start | bytes 73736 | tf_op jit(solution)/shard_map/ppermute | solution.py:10
  37.5 1.9 all_gather.3
  39.7 5.1 %rev.8 = bf16[128,2048]{1,0:T(8,128)(2,1)} reverse(bf16[128,2048]{1,0:T(8,128)(2,1)S(1)} %copy.52), dimensions={0} | reverse | bytes 1048576 | tf_op jit(solution)/shard_map/jit(_flip)/rev | solution.py:85
  45.9 23.0 %fusion.5 = f32[1,192,2048]{2,0,1:T(1,128)S(1)} fusion(bf16[1,319,2048]{2,1,0:T(8,128)(2,1)S(1)} %maximum_bitcast_fusion, bf16[128,1,2048]{2,0,1:T(8,128)(2,1)S(1)} %bitcast.89), kind=kOutput, calls=%fused_computation.30 | convolution fusion | flops 100663296 | bytes 3403776 | tf_op jit(solution)/shard_map/conv_general_dilated | solution.py:14
  68.9 2.3 fusion.40
  71.2 1.3 collective-permute-start.3
  72.5 0.9 fusion.99
  73.4 2.1 copy.43
  77.0 4.0 %fusion.8 = (bf16[192,2048]{1,0:T(8,128)(2,1)S(1)}, bf16[192,2048]{1,0:T(8,128)(2,1)}) fusion(bf16[192,2048]{1,0:T(8,128)(2,1)S(1)} %copy-done.4, bf16[192,2048]{1,0:T(8,128)(2,1)S(1)} %copy-done.3, bf16[6,2048]{1,0:T(8,128)(2,1)S(1)} %collective-permute-done.4, f32[2048]{0:T(1024)S(1)} %bitcast.129, f32[2048]{0:T(1024)S(1)} %bitcast.128, ...), kind=kLoop, calls=%fused_computation.76 | loop fusion | flops 31457280 | bytes 4038656 | tf_op jit(solution)/shard_map/convert_element_type | solution.py:88
  81.8 1.2 pad_bitcast_fusion
  83.0 21.3 %fusion.3 = f32[1,128,2048]{2,0,1:T(1,128)S(1)} fusion(bf16[1,319,2048]{2,1,0:T(8,128)(2,1)S(1)} %copy-done.6, bf16[192,1,2048]{2,0,1:T(8,128)(2,1)S(1)} %bitcast.83), kind=kOutput, calls=%fused_computation.28 | convolution fusion | flops 100663296 | bytes 3141632 | tf_op jit(solution)/shard_map/conv_general_dilated | solution.py:14
  106.6 1.4 collective-permute-start.5
  108.0 22.6 %fusion = f32[1,192,2048]{2,0,1:T(1,128)S(1)} fusion(bf16[128,1,2048]{2,1,0:T(2,128)(2,1)} %copy.43, bf16[1,319,2048]{2,1,0:T(8,128)(2,1)} %pad_bitcast_fusion), kind=kOutput, calls=%fused_computation.24 | convolution fusion | flops 100663296 | bytes 3403776 | tf_op jit(solution)/shard_map/conv_general_dilated | solution.py:14
  131.5 1.8 copy.81
  133.2 1.3 collective-permute-start.7
  134.5 1.3 collective-permute-start.6
  136.7 84.0 %all-reduce.6 = f32[128,128]{0,1:T(8,128)S(1)} all-reduce(bf16[128,128]{0,1:T(8,128)(2,1)S(1)} %copy.51), channel_id=1, replica_groups=mesh['seq'=16,'fsdp'=2] {'seq'}, use_global_device_ids=true, to_apply=%region_24.25 | all-reduce | flops 16384 | bytes 98304 | tf_op jit(solution)/shard_map/psum | solution.py:127
  221.5 1.2 pad_bitcast_fusion.1
  222.7 16.4 %convolution_add_fusion = f32[1,127,2048]{2,0,1:T(1,128)S(1)} fusion(bf16[128,1,2048]{2,1,0:T(2,128)(2,1)} %copy.43, bf16[1,254,2048]{2,1,0:T(8,128)(2,1)S(1)} %pad_bitcast_fusion.1, f32[1,192,2048]{2,0,1:T(1,128)S(1)} %fusion), kind=kOutput, calls=%fused_computation.26 | convolution fusion | flops 66844672 | bytes 3645440 | tf_op jit(solution)/shard_map/conv_general_dilated | solution.py:14
  239.4 3.5 scatter-add.4
  242.9 2.5 fusion.69
  245.5 1.8 fusion.67
  247.4 1.8 fusion.53
  250.3 2.3 fusion.61
  253.5 2.3 fusion.47
  255.8 97.4 %all-reduce.5.cloned.1.call-done = f32[3,7,2048]{2,1,0:T(8,128)} async-done(((f32[3,7,2048]{2,1,0:T(8,128)}), f32[3,7,2048]{2,1,0:T(8,128)}) %all-reduce.5.cloned.1.call-update) | async-done | bytes 172048 | tf_op jit(solution)/shard_map/psum | solution.py:127
  353.2 1.6 copy.88
  (123 shorter events, 13.2 us)
Async XLA Ops:
  8.0 127.9 %reduce-scatter.4.cloned.1.call-start = ((), (), s32[]{:S(2)}) async-start(), calls=%async_computation.2 | async-start | bytes 98304
  8.8 10.9 %collective-permute-start.1 = (bf16[6,2048]{1,0:T(8,128)(2,1)S(1)}, bf16[6,2048]{1,0:T(8,128)(2,1)S(1)}, u32[]{:S(2)}, u32[]{:S(2)}) collective-permute-start(bf16[6,2048]{1,0:T(8,128)(2,1)S(1)} %slice.333), channel_id=1, source_target_pairs={{0,2},{2,4},{4,6},{6,8},{8,10},{10,12},{12,14},{14,16},{16,18},{18... | collective-permute-start | bytes 73736 | tf_op jit(solution)/shard_map/ppermute | solution.py:10
  14.5 5.3 %collective-permute-start = (bf16[6,2048]{1,0:T(8,128)(2,1)S(1)}, bf16[6,2048]{1,0:T(8,128)(2,1)S(1)}, u32[]{:S(2)}, u32[]{:S(2)}) collective-permute-start(bf16[6,2048]{1,0:T(8,128)(2,1)S(1)} %slice.319), channel_id=1, source_target_pairs={{0,2},{2,4},{4,6},{6,8},{8,10},{10,12},{12,14},{14,16},{16,18},{18... | collective-permute-start | bytes 73736 | tf_op jit(solution)/shard_map/ppermute | solution.py:10
  19.6 8.6 %copy-start.13 = (f32[1,1,2048]{2,1,0:T(1,128)}, f32[1,1,2048]{2,1,0:T(1,128)S(1)}, u32[]{:S(2)}) copy-start(f32[1,1,2048]{2,1,0:T(1,128)S(1)} %get-tuple-element.76) | copy-start | bytes 24580
  19.6 8.6 %copy-start.15 = (f32[1,1,2048]{2,1,0:T(1,128)}, f32[1,1,2048]{2,1,0:T(1,128)S(1)}, u32[]{:S(2)}) copy-start(f32[1,1,2048]{2,1,0:T(1,128)S(1)} %get-tuple-element.77) | copy-start | bytes 24580
  19.6 8.6 %copy-start.17 = (f32[1,1,2048]{2,1,0:T(1,128)}, f32[1,1,2048]{2,1,0:T(1,128)S(1)}, u32[]{:S(2)}) copy-start(f32[1,1,2048]{2,1,0:T(1,128)S(1)} %get-tuple-element.78) | copy-start | bytes 24580
  19.6 8.6 %copy-start.19 = (f32[1,1,2048]{2,1,0:T(1,128)}, f32[1,1,2048]{2,1,0:T(1,128)S(1)}, u32[]{:S(2)}) copy-start(f32[1,1,2048]{2,1,0:T(1,128)S(1)} %get-tuple-element.79) | copy-start | bytes 24580
  19.6 8.6 %copy-start.21 = (f32[1,1,2048]{2,1,0:T(1,128)}, f32[1,1,2048]{2,1,0:T(1,128)S(1)}, u32[]{:S(2)}) copy-start(f32[1,1,2048]{2,1,0:T(1,128)S(1)} %get-tuple-element.80) | copy-start | bytes 24580
  19.6 8.6 %copy-start.23 = (f32[1,1,2048]{2,1,0:T(1,128)}, f32[1,1,2048]{2,1,0:T(1,128)S(1)}, u32[]{:S(2)}) copy-start(f32[1,1,2048]{2,1,0:T(1,128)S(1)} %get-tuple-element.81) | copy-start | bytes 24580
  19.6 8.6 %copy-start.25 = (f32[1,1,2048]{2,1,0:T(1,128)}, f32[1,1,2048]{2,1,0:T(1,128)S(1)}, u32[]{:S(2)}) copy-start(f32[1,1,2048]{2,1,0:T(1,128)S(1)} %get-tuple-element.82) | copy-start | bytes 24580
  19.7 8.6 %copy-start.27 = (f32[1,1,2048]{2,1,0:T(1,128)}, f32[1,1,2048]{2,1,0:T(1,128)S(1)}, u32[]{:S(2)}) copy-start(f32[1,1,2048]{2,1,0:T(1,128)S(1)} %get-tuple-element.69) | copy-start | bytes 24580
  19.7 8.6 %copy-start.29 = (f32[1,1,2048]{2,1,0:T(1,128)}, f32[1,1,2048]{2,1,0:T(1,128)S(1)}, u32[]{:S(2)}) copy-start(f32[1,1,2048]{2,1,0:T(1,128)S(1)} %get-tuple-element.70) | copy-start | bytes 24580
  19.7 8.6 %copy-start.31 = (f32[1,1,2048]{2,1,0:T(1,128)}, f32[1,1,2048]{2,1,0:T(1,128)S(1)}, u32[]{:S(2)}) copy-start(f32[1,1,2048]{2,1,0:T(1,128)S(1)} %get-tuple-element.71) | copy-start | bytes 24580
  19.7 8.6 %copy-start.33 = (f32[1,1,2048]{2,1,0:T(1,128)}, f32[1,1,2048]{2,1,0:T(1,128)S(1)}, u32[]{:S(2)}) copy-start(f32[1,1,2048]{2,1,0:T(1,128)S(1)} %get-tuple-element.72) | copy-start | bytes 24580
  19.7 8.6 %copy-start.35 = (f32[1,1,2048]{2,1,0:T(1,128)}, f32[1,1,2048]{2,1,0:T(1,128)S(1)}, u32[]{:S(2)}) copy-start(f32[1,1,2048]{2,1,0:T(1,128)S(1)} %get-tuple-element.73) | copy-start | bytes 24580
  19.7 8.6 %copy-start.37 = (f32[1,1,2048]{2,1,0:T(1,128)}, f32[1,1,2048]{2,1,0:T(1,128)S(1)}, u32[]{:S(2)}) copy-start(f32[1,1,2048]{2,1,0:T(1,128)S(1)} %get-tuple-element.74) | copy-start | bytes 24580
  19.7 8.6 %copy-start.39 = (f32[1,1,2048]{2,1,0:T(1,128)}, f32[1,1,2048]{2,1,0:T(1,128)S(1)}, u32[]{:S(2)}) copy-start(f32[1,1,2048]{2,1,0:T(1,128)S(1)} %get-tuple-element.75) | copy-start | bytes 24580
  19.7 8.6 %copy-start.11 = (bf16[6,2048]{1,0:T(8,128)(2,1)}, bf16[6,2048]{1,0:T(8,128)(2,1)S(1)}, u32[]{:S(2)}) copy-start(bf16[6,2048]{1,0:T(8,128)(2,1)S(1)} %collective-permute-done.1) | copy-start | bytes 73732
  19.8 8.6 %copy-start.9 = (bf16[6,2048]{1,0:T(8,128)(2,1)}, bf16[6,2048]{1,0:T(8,128)(2,1)S(1)}, u32[]{:S(2)}) copy-start(bf16[6,2048]{1,0:T(8,128)(2,1)S(1)} %collective-permute-done) | copy-start | bytes 73732
  19.8 13.4 %copy-start.3 = (bf16[192,2048]{1,0:T(8,128)(2,1)S(1)}, bf16[192,2048]{1,0:T(8,128)(2,1)}, u32[]{:S(2)}) copy-start(bf16[192,2048]{1,0:T(8,128)(2,1)} %param.8) | copy-start | bytes 2359300
  19.8 17.7 %copy-start.41 = (f32[128,128]{1,0:T(8,128)S(1)}, f32[128,128]{1,0:T(8,128)}, u32[]{:S(2)}) copy-start(f32[128,128]{1,0:T(8,128)} %param.13) | copy-start | bytes 196612
  29.3 15.5 %collective-permute-start.2 = (bf16[127,2048]{1,0:T(8,128)(2,1)}, bf16[127,2048]{1,0:T(8,128)(2,1)S(1)}, u32[]{:S(2)}, u32[]{:S(2)}) collective-permute-start(bf16[127,2048]{1,0:T(8,128)(2,1)} %slice.405), channel_id=1, source_target_pairs={{0,2},{2,4},{4,6},{6,8},{8,10},{10,12},{12,14},{14,16},{16,18},{18... | collective-permute-start | bytes 1560584 | tf_op jit(solution)/shard_map/ppermute | solution.py:10
  33.2 35.6 %collective-permute-start.4 = (bf16[6,2048]{1,0:T(8,128)(2,1)S(1)}, bf16[6,2048]{1,0:T(8,128)(2,1)S(1)}, u32[]{:S(2)}, u32[]{:S(2)}) collective-permute-start(bf16[6,2048]{1,0:T(8,128)(2,1)S(1)} %slice.359), channel_id=1, source_target_pairs={{0,2},{2,4},{4,6},{6,8},{8,10},{10,12},{12,14},{14,16},{16,18},{18... | collective-permute-start | bytes 73736 | tf_op jit(solution)/shard_map/ppermute | solution.py:10
  45.0 23.8 %copy-start.5 = (bf16[1,319,2048]{2,1,0:T(8,128)(2,1)}, bf16[1,319,2048]{2,1,0:T(8,128)(2,1)S(1)}, u32[]{:S(2)}) copy-start(bf16[1,319,2048]{2,1,0:T(8,128)(2,1)S(1)} %maximum_bitcast_fusion) | copy-start | bytes 3919876
  45.9 23.0 %copy-start.4 = (bf16[192,2048]{1,0:T(8,128)(2,1)S(1)}, bf16[192,2048]{1,0:T(8,128)(2,1)}, u32[]{:S(2)}) copy-start(bf16[192,2048]{1,0:T(8,128)(2,1)} %param.11) | copy-start | bytes 2359300
  71.2 5.8 %collective-permute-start.3 = (bf16[6,2048]{1,0:T(8,128)(2,1)S(1)}, bf16[6,2048]{1,0:T(8,128)(2,1)S(1)}, u32[]{:S(2)}, u32[]{:S(2)}) collective-permute-start(bf16[6,2048]{1,0:T(8,128)(2,1)S(1)} %slice.406), channel_id=1, source_target_pairs={{2,0},{4,2},{6,4},{8,6},{10,8},{12,10},{14,12},{16,14},{18,16},{20... | collective-permute-start | bytes 73736 | tf_op jit(solution)/shard_map/ppermute | solution.py:10
  106.5 24.1 %copy-start = (f32[192,2048]{1,0:T(8,128)S(1)}, f32[192,2048]{1,0:T(8,128)}, u32[]{:S(2)}) copy-start(f32[192,2048]{1,0:T(8,128)} %get-tuple-element.50) | copy-start | bytes 4718596
  106.5 246.6 %all-reduce.5.cloned.1.call-start = ((), (), s32[]{:S(2)}) async-start(), calls=%async_computation.1 | async-start | bytes 393216 | tf_op jit(solution)/shard_map/psum | solution.py:127
  106.6 114.9 %collective-permute-start.5 = (bf16[127,2048]{1,0:T(8,128)(2,1)}, bf16[127,2048]{1,0:T(8,128)(2,1)}, u32[]{:S(2)}, u32[]{:S(2)}) collective-permute-start(bf16[127,2048]{1,0:T(8,128)(2,1)} %slice.430), channel_id=1, source_target_pairs={{2,0},{4,2},{6,4},{8,6},{10,8},{12,10},{14,12},{16,14},{18,16},{20... | collective-permute-start | bytes 1560584 | tf_op jit(solution)/shard_map/ppermute | solution.py:10
  133.2 116.8 %collective-permute-start.7 = (bf16[6,2048]{1,0:T(8,128)(2,1)S(1)}, bf16[6,2048]{1,0:T(8,128)(2,1)S(1)}, u32[]{:S(2)}, u32[]{:S(2)}) collective-permute-start(bf16[6,2048]{1,0:T(8,128)(2,1)S(1)} %get-tuple-element.87), channel_id=1, source_target_pairs={{2,0},{4,2},{6,4},{8,6},{10,8},{12,10},{14,12},{16,14},{18,16},{20... | collective-permute-start | bytes 73736 | tf_op jit(solution)/shard_map/ppermute | solution.py:10
  134.5 118.2 %collective-permute-start.6 = (bf16[6,2048]{1,0:T(8,128)(2,1)S(1)}, bf16[6,2048]{1,0:T(8,128)(2,1)S(1)}, u32[]{:S(2)}, u32[]{:S(2)}) collective-permute-start(bf16[6,2048]{1,0:T(8,128)(2,1)S(1)} %get-tuple-element.88), channel_id=1, source_target_pairs={{2,0},{4,2},{6,4},{8,6},{10,8},{12,10},{14,12},{16,14},{18,16},{20... | collective-permute-start | bytes 73736 | tf_op jit(solution)/shard_map/ppermute | solution.py:10
  245.5 3.9 %copy-start.8 = (f32[7,2048]{1,0:T(8,128)S(1)}, f32[7,2048]{1,0:T(8,128)}, u32[]{:S(2)}) copy-start(f32[7,2048]{1,0:T(8,128)} %stack.91) | copy-start | bytes 172036
  (20 other events, 25.1 us)
Sparse Core Ops, SparseCore 0:
  106.6 10.6 reduce-scatter.3
Sparse Core Ops, SparseCore 1:
  250.1 103.0 all-reduce.4
where the time goes:
time: 363 us; the launch traced here: 362 us
  waiting for transfers between devices  98.3 us (27%)
  blocking collectives  85.9 us (24%)
  matrix products  83.3 us (23%)
  local copies, waits for them, and re-layouts  29 us (8%)
  other arithmetic  27.8 us (8%)
  starting transfers between devices  21.8 us (6%)
  between operations  16.3 us (4%)
    psum x1, waiting for transfers between devices, shards(): grad_short, grad_medium = lax.psum((short_local, medium_part), 'seq')  97.4 us
    psum x1, blocking collectives, shards(): grad_short, grad_medium = lax.psum((short_local, medium_part), 'seq')  84 us
    conv_general_dilated x4, matrix products, depthwise(): lax.conv_general_dilated(signal_in[None], kernel[:, None, :], (1,), 'VALI...  83.3 us
    ppermute x8, starting transfers between devices, from_behind(): lax.ppermute(value, axis, [(source, source + steps) for source in range(i...  21.7 us
    convert_element_type x1, other arithmetic, shards(): gated = (key_wide * value_wide).astype(jnp.bfloat16)  8.42 us
    unnamed x92, local copies, waits for them, and re-layouts  8.22 us
  transfers between devices with their start and end apart: 10, of which 2 were waited for; matrix products, arithmetic and copies ran while one was open for 26% of the time, Pallas kernels for 0%

commit v1 on v0

v1 whole, which is shorter than its diff:
```python
import numpy as np
import jax
import jax.numpy as jnp
from jax import lax
from jax.experimental import pallas as pl
from jax.experimental.pallas import tpu as pltpu
from jax.sharding import PartitionSpec as P

HALO = 8
BLOCK = 128
WINDOW = 2 * BLOCK
F32 = jnp.float32
BF16 = jnp.bfloat16


def split_terms(matrix):
    high = matrix.astype(BF16)
    low = (matrix - high.astype(np.float32)).astype(BF16)
    return np.asarray(high), np.asarray(low)


def transforms():
    time = np.arange(WINDOW)
    freq = np.arange(BLOCK)
    angle = 2 * np.pi * ((freq[:, None] * time[None, :]) % WINDOW) / WINDOW
    cosine, sine = np.cos(angle), np.sin(angle)
    nyquist = np.where(time % 2 == 0, 1.0, -1.0)
    forward = np.concatenate([cosine, -sine]).astype(np.float64)
    forward[BLOCK] = nyquist
    scale = np.full(WINDOW, 2.0 / WINDOW)
    scale[0] = scale[BLOCK] = 1.0 / WINDOW
    inverse = forward.T * scale[None, :]
    f_high, f_low = split_terms(forward.astype(np.float32))
    i_high, i_low = split_terms(inverse.astype(np.float32))
    whole = np.concatenate([f_high, f_low], axis=1)
    half = np.concatenate([f_high[:, :BLOCK], f_low[:, :BLOCK]], axis=1)
    back = np.concatenate([i_high, i_high, i_low], axis=1)
    return whole, half, back[:BLOCK], back[BLOCK:]


def dot(left, right):
    return jnp.dot(left, right, preferred_element_type=F32)


def to_spectrum(matrix, rows):
    return dot(matrix, jnp.concatenate([rows, rows], axis=0))


def from_spectrum(matrix, real, imag):
    whole = jnp.concatenate([real, imag], axis=0)
    high = whole.astype(BF16)
    low = (whole - high.astype(F32)).astype(BF16)
    return dot(matrix, jnp.concatenate([high, low, high], axis=0))


def times(spec, taps):
    xr, xi = spec[:BLOCK], spec[BLOCK:]
    return xr * taps[0] - xi * taps[1], xr * taps[1] + xi * taps[2]


def times_conj(spec, taps):
    xr, xi = spec[:BLOCK], spec[BLOCK:]
    return xr * taps[0] + xi * taps[1], xi * taps[2] - xr * taps[1]


def rounded(value):
    return value.astype(BF16).astype(F32)


def lanes_of(width):
    return [slice(at, at + 128) for at in range(0, width, 128)]


def causal(ref, weights, index, count, lanes):
    total = None
    for j in range(weights.shape[1]):
        term = weights[index, j : j + 1, lanes] * ref[pl.ds(HALO - j, count), lanes]
        total = term if total is None else total + term
    return total


def anticausal(ref, weights, index, count, lanes):
    total = None
    for j in range(weights.shape[1]):
        term = weights[index, j : j + 1, lanes] * ref[pl.ds(j, count), lanes]
        total = term if total is None else total + term
    return total


def lag_sums(gradient, ref, taps, lanes):
    count = gradient.shape[0]
    rows = []
    for j in range(taps):
        prod = gradient * ref[pl.ds(HALO - j, count), lanes]
        rows.append(jnp.sum(prod, axis=0, keepdims=True))
    rows.append(jnp.zeros_like(rows[0]))
    return jnp.concatenate(rows, axis=0)


def first_kernel(q, k, v, g, w, tails, heads, ahead, xq):
    rows = q.shape[0]
    low = rows - 2 * HALO
    tails[...] = jnp.concatenate(
        [x[low:, :].astype(F32)[HALO:] for x in (q, k, v)], axis=0
    ).astype(BF16)
    heads[...] = jnp.concatenate(
        [x[: 2 * HALO, :].astype(F32)[:HALO] for x in (q, k, v, g)], axis=0
    ).astype(BF16)
    need = BLOCK + 2 * HALO
    xq[...] = q[:need, :].astype(F32)
    grad = g[:need, :].astype(F32)[HALO : HALO + BLOCK]
    for lanes in lanes_of(q.shape[1]):
        ahead[:, lanes] = (grad[:, lanes] * causal(xq, w, 0, BLOCK, lanes)).astype(BF16)


def second_kernel(
    q, k, v, g, tails, heads, w, taps, half, whole, low, high,
    gated_out, ggi_out, ks_out, vs_out, inner_out, behind_out, spec_out,
    xq, xk, xv, tap_spec,
):
    rows, width = q.shape
    ext = rows + HALO

    @pl.when(pl.program_id(0) == 0)
    def _():
        both = jnp.concatenate([taps[...], taps[...]], axis=1)
        spec = lax.dot_general(half[...], both, (((1,), (1,)), ((), ())), preferred_element_type=F32)
        real, imag = spec[:BLOCK], spec[BLOCK:]
        first = lax.broadcasted_iota(jnp.int32, real.shape, 0) == 0
        tap_spec[0] = real
        tap_spec[1] = jnp.where(first, 0.0, imag)
        tap_spec[2] = jnp.where(first, imag, real)
        spec_out[...] = tap_spec[...]

    tail = tails[...].astype(F32)
    head = heads[...].astype(F32)
    for at, (ref, x) in enumerate(((xq, q), (xk, k), (xv, v))):
        ref[:HALO] = tail[at * HALO : (at + 1) * HALO]
        ref[HALO : HALO + rows] = x[...].astype(F32)
        ref[HALO + rows :] = head[at * HALO : (at + 1) * HALO]
    grad = jnp.concatenate([g[...].astype(F32), head[3 * HALO :]], axis=0)
    gated = []
    for lanes in lanes_of(width):
        ks = causal(xk, w, 1, ext, lanes)
        vs = causal(xv, w, 2, ext, lanes)
        ks_out[:ext, lanes] = ks
        vs_out[:ext, lanes] = vs
        gated.append(ks * vs)
        qs = causal(xq, w, 0, ext, lanes)
        ggi_out[:, lanes] = grad[:, lanes] * qs
    gated = jnp.concatenate(gated, axis=1)
    pad = jnp.zeros((WINDOW - ext, width), F32)
    window = jnp.concatenate([gated, pad], axis=0).astype(BF16)
    gated_out[...] = window[: gated_out.shape[0]]
    behind_out[...] = window[rows - BLOCK : rows]
    first = to_spectrum(half[...], window[:BLOCK])
    inner_out[:BLOCK] = from_spectrum(low[...], *times(first, tap_spec))
    second = to_spectrum(whole[...], window)
    inner_out[BLOCK:] = from_spectrum(high[: ext - BLOCK, :], *times(second, tap_spec))


def third_kernel(
    k, v, tails, gated, ggi, ahead, ks, vs, w, spec, half, whole, low,
    gk_out, gv_out, sums_out, medium_out,
    xk, xv, yk, yv, acc,
):
    rows, width = k.shape
    ext = rows + HALO
    step = pl.program_id(0)

    @pl.when(step == 0)
    def _():
        acc[...] = jnp.zeros_like(acc)

    tail = tails[...].astype(F32)
    for at, (ref, x) in enumerate(((xk, k), (xv, v))):
        ref[:HALO] = tail[(at + 1) * HALO : (at + 2) * HALO]
        ref[HALO:] = x[...].astype(F32)
    pad = jnp.zeros((3 * BLOCK - ext - BLOCK, width), F32)
    ggi_ext = jnp.concatenate([ggi[...], ahead[...].astype(F32), pad], axis=0).astype(BF16)
    own = gated[: WINDOW - BLOCK + 0, :]
    rest = jnp.concatenate(
        [gated[BLOCK:rows, :], jnp.zeros((WINDOW - rows, width), BF16)], axis=0
    )
    parts = []
    for at, mine in ((0, own), (1, rest)):
        win = to_spectrum(whole[...], ggi_ext[at * BLOCK : at * BLOCK + WINDOW])
        gs = to_spectrum(half[...], mine)
        acc[0] += gs[:BLOCK] * win[:BLOCK]
        acc[1] += gs[BLOCK:] * win[BLOCK:]
        acc[2] += gs[:BLOCK] * win[BLOCK:] - gs[BLOCK:] * win[:BLOCK]
        count = min(BLOCK, ext - at * BLOCK)
        parts.append(from_spectrum(low[:count, :], *times_conj(win, spec)))
    gg = jnp.concatenate(parts, axis=0)
    yk[:ext] = rounded(gg * vs[:ext, :])
    yv[:ext] = rounded(gg * ks[:ext, :])
    for lanes in lanes_of(width):
        gk_out[:, lanes] = anticausal(yk, w, 1, rows, lanes).astype(BF16)
        gv_out[:, lanes] = anticausal(yv, w, 2, rows, lanes).astype(BF16)
        sums_out[:HALO, lanes] = lag_sums(yk[:rows, lanes], xk, w.shape[1], lanes)
        sums_out[HALO:, lanes] = lag_sums(yv[:rows, lanes], xv, w.shape[1], lanes)

    @pl.when(step == pl.num_programs(0) - 1)
    def _():
        first = lax.broadcasted_iota(jnp.int32, (BLOCK, width), 0) == 0
        real = acc[0] + jnp.where(first, 0.0, acc[1])
        imag = jnp.where(first, acc[1], acc[2])
        medium_out[...] = from_spectrum(low[...], real, imag).T


def fourth_kernel(
    q, g, tails, heads, inner, behind, w, spec, half, high,
    gq_out, sums_out,
    xq, yq,
):
    rows, width = q.shape
    ext = rows + HALO
    xq[:HALO] = tails[...].astype(F32)[:HALO]
    xq[HALO:] = q[...].astype(F32)
    edge = from_spectrum(high[...], *times(to_spectrum(half[...], behind[...]), spec))
    yq[:BLOCK] = rounded(g[:BLOCK, :].astype(F32) * (inner[:BLOCK, :] + edge))
    yq[BLOCK:rows] = rounded(g[BLOCK:, :].astype(F32) * inner[BLOCK:rows, :])
    yq[rows:ext] = rounded(heads[...].astype(F32)[3 * HALO :] * inner[rows:ext, :])
    for lanes in lanes_of(width):
        gq_out[:, lanes] = anticausal(yq, w, 0, rows, lanes).astype(BF16)
        sums_out[:, lanes] = lag_sums(yq[:rows, lanes], xq, w.shape[1], lanes)


def shift(value, axis, steps):
    count = lax.axis_size(axis)
    initial, last = (max(0, -steps), min(count, count - steps))
    return lax.ppermute(value, axis, [(s, s + steps) for s in range(initial, last)])


def gather_rows(value, axis):
    count, rows = lax.axis_size(axis), value.shape[0]
    me = lax.axis_index(axis)
    result = jnp.zeros((count * rows, value.shape[1]), value.dtype)
    result = lax.dynamic_update_slice(result, value, (me * rows, 0))
    for step in range(1, count):
        other = lax.ppermute(value, axis, [(s, (s + step) % count) for s in range(count)])
        result = lax.dynamic_update_slice(result, other, ((me - step) % count * rows, 0))
    return result


def scatter_sum(value, axis):
    count = lax.axis_size(axis)
    rows = value.shape[0] // count
    me = lax.axis_index(axis)
    total = lax.dynamic_slice(value, (me * rows, 0), (rows, value.shape[1]))
    for step in range(1, count):
        part = lax.dynamic_slice(value, ((me + step) % count * rows, 0), (rows, value.shape[1]))
        total = total + lax.ppermute(
            part.astype(BF16), axis, [(s, (s + step) % count) for s in range(count)]
        ).astype(F32)
    return total


def sum_over(value, axis):
    count = lax.axis_size(axis)
    if count & (count - 1):
        return lax.psum(value, axis)
    distance = 1
    while distance < count:
        other = lax.ppermute(value.astype(BF16), axis, [(s, s ^ distance) for s in range(count)])
        value = value + other.astype(F32)
        distance *= 2
    return value


def shards(query, key, value, grad_out, short_filter, medium_filter):
    rows, channels = query.shape
    groups = medium_filter.shape[0] * lax.axis_size("fsdp")
    width, tiles = groups, channels // groups
    ext = rows + HALO
    pad_rows = rows + 2 * HALO
    taps_short = short_filter.shape[1]
    whole, half, low, high = (jnp.asarray(m) for m in transforms())

    def col(count):
        return pl.BlockSpec((count, width), lambda i: (0, i))

    def fixed(shape):
        return pl.BlockSpec(shape, lambda i: (0,) * len(shape))

    weights = pl.BlockSpec((3, taps_short, width), lambda i: (0, 0, i))

    def out(count, dtype):
        return jax.ShapeDtypeStruct((count, channels), dtype)

    params = pltpu.CompilerParams(vmem_limit_bytes=48 * 1024 * 1024)

    def cost(flops, moved):
        return pl.CostEstimate(flops=int(flops), bytes_accessed=int(moved), transcendentals=0)

    tails, heads, ahead = pl.pallas_call(
        first_kernel,
        grid=(tiles,),
        in_specs=[col(rows)] * 4 + [weights],
        out_specs=[col(3 * HALO), col(4 * HALO), col(BLOCK)],
        out_shape=[out(3 * HALO, BF16), out(4 * HALO, BF16), out(BLOCK, BF16)],
        scratch_shapes=[pltpu.VMEM((BLOCK + 2 * HALO, width), F32)],
        compiler_params=params,
        name="first",
    )(query, key, value, grad_out, short_filter)
    taps = gather_rows(medium_filter.astype(BF16), "fsdp")
    tails = shift(tails, "seq", 1)
    heads = shift(heads, "seq", -1)
    ahead = shift(ahead, "seq", -1)

    gated, ggi, ks, vs, inner, behind, spec = pl.pallas_call(
        second_kernel,
        grid=(tiles,),
        in_specs=[col(rows)] * 4
        + [col(3 * HALO), col(4 * HALO), weights, fixed(taps.shape)]
        + [fixed(m.shape) for m in (half, whole, low, high)],
        out_specs=[col(pad_rows), col(ext), col(ext), col(ext), col(ext), col(BLOCK), fixed((3, BLOCK, width))],
        out_shape=[
            out(pad_rows, BF16), out(ext, F32), out(ext, F32), out(ext, F32), out(ext, F32),
            out(BLOCK, BF16), jax.ShapeDtypeStruct((3, BLOCK, width), F32),
        ],
        scratch_shapes=[pltpu.VMEM((rows + 2 * HALO, width), F32)] * 3
        + [pltpu.VMEM((3, BLOCK, width), F32)],
        compiler_params=params,
        cost_estimate=cost(2e9, 12e6),
        name="second",
    )(query, key, value, grad_out, tails, heads, short_filter, taps, half, whole, low, high)
    behind = shift(behind, "seq", 1)

    grad_key, grad_value, sums_kv, medium = pl.pallas_call(
        third_kernel,
        grid=(tiles,),
        in_specs=[col(rows)] * 2
        + [col(3 * HALO), col(pad_rows), col(ext), col(BLOCK), col(ext), col(ext), weights]
        + [fixed((3, BLOCK, width))]
        + [fixed(m.shape) for m in (half, whole, low)],
        out_specs=[col(rows), col(rows), col(2 * HALO), fixed((width, BLOCK))],
        out_shape=[out(rows, BF16), out(rows, BF16), out(2 * HALO, F32), jax.ShapeDtypeStruct((width, BLOCK), F32)],
        scratch_shapes=[pltpu.VMEM((rows + HALO, width), F32)] * 4
        + [pltpu.VMEM((3, BLOCK, width), F32)],
        compiler_params=params,
        cost_estimate=cost(4e9, 12e6),
        name="third",
    )(key, value, tails, gated, ggi, ahead, ks, vs, short_filter, spec, half, whole, low)

    grad_query, sums_q = pl.pallas_call(
        fourth_kernel,
        grid=(tiles,),
        in_specs=[col(rows)] * 2
        + [col(3 * HALO), col(4 * HALO), col(ext), col(BLOCK), weights]
        + [fixed((3, BLOCK, width))]
        + [fixed(m.shape) for m in (half, high)],
        out_specs=[col(rows), col(HALO)],
        out_shape=[out(rows, BF16), out(HALO, F32)],
        scratch_shapes=[pltpu.VMEM((rows + HALO, width), F32)] * 2,
        compiler_params=params,
        cost_estimate=cost(1e9, 6e6),
        name="fourth",
    )(query, grad_out, tails, heads, inner, behind, short_filter, spec, half, high)

    medium = scatter_sum(medium, "fsdp")
    per = channels // BLOCK
    count = medium.shape[0] // per
    packed = jnp.concatenate([medium[i * count : (i + 1) * count] for i in range(per)], axis=1)
    late = sum_over(jnp.concatenate([sums_kv, packed], axis=0), "seq")
    sums_q = sum_over(sums_q, "seq")
    packed = late[2 * HALO :]
    grad_medium = jnp.concatenate([packed[:, i * BLOCK : (i + 1) * BLOCK] for i in range(per)], axis=0)
    grad_short = jnp.stack([sums_q[:taps_short], late[:taps_short], late[HALO : HALO + taps_short]])
    return grad_query, grad_key, grad_value, grad_short, grad_medium


def solution(mesh):
    in_specs = (
        P("seq", "fsdp"),
        P("seq", "fsdp"),
        P("seq", "fsdp"),
        P("seq", "fsdp"),
        P(None, None, "fsdp"),
        P("fsdp", None),
    )
    out_specs = (
        P("seq", "fsdp"),
        P("seq", "fsdp"),
        P("seq", "fsdp"),
        P(None, None, "fsdp"),
        P("fsdp", None),
    )
    return jax.shard_map(shards, mesh=mesh, in_specs=in_specs, out_specs=out_specs, check_vma=False)
```

time: 363 us -> 115 us (0.32)
  blocking collectives: 85.9 us -> 0 us
  matrix products: 83.3 us -> 0 us
  waiting for transfers between devices: 98.3 us -> 29.5 us
  Pallas kernels: 0 us -> 38.3 us
  other arithmetic: 27.8 us -> 2.41 us
  local copies, waits for them, and re-layouts: 29 us -> 13.1 us
  between operations: 16.3 us -> 1.11 us
  starting transfers between devices: 21.8 us -> 29.8 us
    psum x1 -> x0, waiting for transfers between devices: 97.4 us -> none  [shards(): grad_short, grad_medium = lax.psum((short_local, medium_part), 'seq')]
    psum x1 -> x0, blocking collectives: 84 us -> none  [shards(): grad_short, grad_medium = lax.psum((short_local, medium_part), 'seq')]
    conv_general_dilated x4 -> x0, matrix products: 83.3 us -> none  [depthwise(): lax.conv_general_dilated(signal_in[None], kernel[:, None, :], (1,), 'VALI...]
    pallas_call x0 -> x4, Pallas kernels: none -> 38.3 us  [the longest x1 14.4 us: shards(): pl.pallas_call(third_kernel, grid=(tiles,), in_specs=[col(rows)] * 2 + [c...]
    ppermute x8 -> x14, waiting for transfers between devices: 0.8 us -> 29.5 us  [the longest x4 21.8 us: shift(): lax.ppermute(value, axis, [(s, s + steps) for s in range(initial, last)])]
    convert_element_type x7 -> x8, other arithmetic: 20.4 us -> 0.16 us  [sum_over(): value.astype(BF16)]
    ppermute x8 -> x14, starting transfers between devices: 21.7 us -> 29.8 us  [the longest x8 15.9 us: sum_over(): lax.ppermute(value.astype(BF16), axis, [(s, s ^ distance) for s in range(...]
    reduce_sum x4 -> x0, other arithmetic: 6.1 us -> none  [the longest x3 5.83 us: short_gradient(): jnp.sum(grad_f * extended[offset:offset + count].astype(jnp.float32), axi...]
  transfers between devices with their start and end apart: 10 -> 14, of which waited for: 2 -> 8; matrix products, arithmetic and copies ran while one was open for 26% -> 3% of each run, Pallas kernels for 0% -> 11%
where the time goes in v1:
time: 115 us; the launch traced here: 114 us
  Pallas kernels  38.3 us (33%)
  starting transfers between devices  29.8 us (26%)
  waiting for transfers between devices  29.5 us (26%)
  local copies, waits for them, and re-layouts  13.1 us (11%)
  other arithmetic  2.41 us (2%)
    ppermute x4, waiting for transfers between devices, shift(): lax.ppermute(value, axis, [(s, s + steps) for s in range(initial, last)])  21.8 us
    ppermute x8, starting transfers between devices, sum_over(): lax.ppermute(value.astype(BF16), axis, [(s, s ^ distance) for s in range(...  15.9 us
    pallas_call x1, Pallas kernels, shards(): pl.pallas_call(third_kernel, grid=(tiles,), in_specs=[col(rows)] * 2 + [c...  14.4 us
    ppermute x4, starting transfers between devices, shift(): lax.ppermute(value, axis, [(s, s + steps) for s in range(initial, last)])  13.2 us
    pallas_call x1, Pallas kernels, shards(): pl.pallas_call(second_kernel, grid=(tiles,), in_specs=[col(rows)] * 4 + [...  12 us
    unnamed x74, local copies, waits for them, and re-layouts  11.1 us
    pallas_call x1, Pallas kernels, shards(): pl.pallas_call(fourth_kernel, grid=(tiles,), in_specs=[col(rows)] * 2 + [...  8.32 us
    ppermute x8, waiting for transfers between devices, sum_over(): lax.ppermute(value.astype(BF16), axis, [(s, s ^ distance) for s in range(...  7.68 us
  transfers between devices with their start and end apart: 14, of which 8 were waited for; matrix products, arithmetic and copies ran while one was open for 3% of the time, Pallas kernels for 11%

profile of v1, /device:TPU:0, one launch (start us, length us, event | category | flops | bytes accessed | tf_op | source)
XLA Modules:
  0.0 114.2 jit_solution(11797806969684816636)
XLA Ops:
  0.6 1.1 copy-done
  1.8 1.1 copy-done.2
  2.9 0.9 copy-done.5
  3.8 1.1 copy-done.7
  5.0 1.1 copy-done.9
  6.1 3.6 %first.1 = (bf16[24,2048]{1,0:T(8,128)(2,1)S(1)}, bf16[32,2048]{1,0:T(8,128)(2,1)S(1)}, bf16[128,2048]{1,0:T(8,128)(2,1)}) custom-call(bf16[192,2048]{1,0:T(8,128)(2,1)S(1)} %copy-done, bf16[192,2048]{1,0:T(8,128)(2,1)S(1)} %copy-done.7, bf16[192,2048]{1,0:T(8,128)(2,1)S(1)} %copy-done.9, bf16[192,2048]{1,0:T(8,128)(2,1)S(1)} %copy-done.2, ...), custom_call_target="tpu_custom_call" | custom-call | tf_op jit(solution)/shard_map/first/pallas_call | solution.py:296
  11.0 1.3 %collective-permute-start.4 = (bf16[128,2048]{1,0:T(8,128)(2,1)}, bf16[128,2048]{1,0:T(8,128)(2,1)}, u32[]{:S(2)}, u32[]{:S(2)}) collective-permute-start(bf16[128,2048]{1,0:T(8,128)(2,1)} %get-tuple-element.29), channel_id=1, source_target_pairs={{2,0},{4,2},{6,4},{8,6},{10,8},{12,10},{14,12},{16,14},{18,16},{20... | collective-permute-start | bytes 1572872 | tf_op jit(solution)/shard_map/ppermute | solution.py:232
  12.9 1.5 %constant_dynamic-update-slice_fusion.33 = (bf16[256,128]{1,0:T(8,128)(2,1)}, bf16[128,128]{1,0:T(8,128)(2,1)}) fusion(bf16[256,128]{1,0:T(8,128)(2,1)} %broadcast_in_dim.3, s32[]{:T(128)S(6)} %select_n.21, f32[128,128]{1,0:T(8,128)} %param.15), kind=kLoop, calls=%fused_computation.53 | loop fusion | flops 16384 | bytes 131076 | tf_op jit(solution)/shard_map/dynamic_update_slice | solution.py:239
  14.9 1.3 %collective-permute-start.1 = (bf16[32,2048]{1,0:T(8,128)(2,1)}, bf16[32,2048]{1,0:T(8,128)(2,1)}, u32[]{:S(2)}, u32[]{:S(2)}) collective-permute-start(bf16[32,2048]{1,0:T(8,128)(2,1)} %copy-done.14), channel_id=1, source_target_pairs={{2,0},{4,2},{6,4},{8,6},{10,8},{12,10},{14,12},{16,14},{18,16},{20... | collective-permute-start | bytes 393224 | tf_op jit(solution)/shard_map/ppermute | solution.py:232
  16.2 6.3 %collective-permute-start = (bf16[24,2048]{1,0:T(8,128)(2,1)}, bf16[24,2048]{1,0:T(8,128)(2,1)}, u32[]{:S(2)}, u32[]{:S(2)}) collective-permute-start(bf16[24,2048]{1,0:T(8,128)(2,1)} %copy-done.15), channel_id=1, source_target_pairs={{0,2},{2,4},{4,6},{6,8},{8,10},{10,12},{12,14},{14,16},{16,18},{18... | collective-permute-start | bytes 294920 | tf_op jit(solution)/shard_map/ppermute | solution.py:232
  22.5 1.4 %constant_dynamic-update-slice_fusion.32.taps = bf16[256,128]{1,0:T(8,128)(2,1)} fusion(bf16[256,128]{1,0:T(8,128)(2,1)} %get-tuple-element.39, bf16[128,128]{1,0:T(8,128)(2,1)} %collective-permute-done.2, s32[]{:T(128)S(6)} %select_n.23), kind=kLoop, calls=%fused_computation.52 | loop fusion | bytes 65540 | tf_op jit(solution)/shard_map/dynamic_update_slice | solution.py:242
  23.8 10.3 %collective-permute-done.tails = bf16[24,2048]{1,0:T(8,128)(2,1)} collective-permute-done((bf16[24,2048]{1,0:T(8,128)(2,1)}, bf16[24,2048]{1,0:T(8,128)(2,1)}, u32[]{:S(2)}, u32[]{:S(2)}) %collective-permute-start) | collective-permute-done | bytes 98336 | tf_op jit(solution)/shard_map/ppermute | solution.py:232
  34.2 0.9 copy-done.12
  35.1 0.9 copy-done.16
  36.0 0.9 copy-done.18
  37.0 12.0 %second.1 = (bf16[208,2048]{1,0:T(8,128)(2,1)S(1)}, f32[200,2048]{1,0:T(8,128)}, f32[200,2048]{1,0:T(8,128)}, f32[200,2048]{1,0:T(8,128)}, f32[200,2048]{1,0:T(8...) custom-call(bf16[192,2048]{1,0:T(8,128)(2,1)S(1)} %copy-done.1, bf16[192,2048]{1,0:T(8,128)(2,1)S(1)} %copy-done.8, ...), custom_call_target="tpu_custom_call" | custom-call | flops 2000000000 | bytes 12000000 | tf_op jit(solution)/shard_map/second/pallas_call | solution.py:311
  49.0 1.4 %copy-done.20 = f32[200,2048]{1,0:T(8,128)S(1)} copy-done((f32[200,2048]{1,0:T(8,128)S(1)}, f32[200,2048]{1,0:T(8,128)}, u32[]{:S(2)}) %copy-start.20) | copy-done | bytes 1638424
  50.5 14.4 %third.1 = (bf16[192,2048]{1,0:T(8,128)(2,1)}, bf16[192,2048]{1,0:T(8,128)(2,1)}, f32[16,2048]{1,0:T(8,128)S(1)}, f32[256,128]{1,0:T(8,128)S(1)}) custom-call(bf16[192,2048]{1,0:T(8,128)(2,1)S(1)} %copy-done.8, bf16[192,2048]{1,0:T(8,128)(2,1)S(1)} %copy-done.10, bf16[24,2048]{1,0:T(8,128)(2,1)} %collective-permute-done.tails, ...), custom_call_target="tpu_custom_call" | custom-call | flops 4000000000 | bytes 12000000 | tf_op jit(solution)/shard_map/third/pallas_call | solution.py:330
  65.0 4.4 %collective-permute-start.3 = (bf16[128,2048]{1,0:T(8,128)(2,1)S(1)}, bf16[128,2048]{1,0:T(8,128)(2,1)S(1)}, u32[]{:S(2)}, u32[]{:S(2)}) collective-permute-start(bf16[128,2048]{1,0:T(8,128)(2,1)S(1)} %get-tuple-element.24), channel_id=1, source_target_pairs={{0,2},{2,4},{4,6},{6,8},{8,10},{10,12},{12,14},{14,16},{16,18},{18... | collective-permute-start | bytes 1572872 | tf_op jit(solution)/shard_map/ppermute | solution.py:232
  69.6 11.5 %collective-permute-done.3.behind = bf16[128,2048]{1,0:T(8,128)(2,1)S(1)} collective-permute-done((bf16[128,2048]{1,0:T(8,128)(2,1)S(1)}, bf16[128,2048]{1,0:T(8,128)(2,1)S(1)}, u32[]{:S(2)}, u32[]{:S(2)}) %collective-permute-start.3) | collective-permute-done | bytes 524320 | tf_op jit(solution)/shard_map/ppermute | solution.py:232
  81.1 8.3 %fourth.1 = (bf16[192,2048]{1,0:T(8,128)(2,1)}, f32[8,2048]{1,0:T(8,128)S(1)}) custom-call(bf16[192,2048]{1,0:T(8,128)(2,1)S(1)} %copy-done.1, bf16[192,2048]{1,0:T(8,128)(2,1)S(1)} %copy-done.3, bf16[24,2048]{1,0:T(8,128)(2,1)} %collective-permute-done.tails, bf16[32,2048]{1,0:T(8,128)(2,1)} %collective-permute-done.1.heads, f32[200,2048]{1,0:T(8,128)S(1)} %copy-done.4, ...), custom_call_target="tpu_custom_call" | custom-call | flops 1000000000 | bytes 6000000 | tf_op jit(solution)/shard_map/fourth/pallas_call | solution.py:346
  89.5 2.5 %collective-permute-start.5 = (bf16[8,2048]{1,0:T(8,128)(2,1)S(1)}, bf16[8,2048]{1,0:T(8,128)(2,1)S(1)}, u32[]{:S(2)}, u32[]{:S(2)}) collective-permute-start(bf16[8,2048]{1,0:T(8,128)(2,1)S(1)} %convert_element_type.58), channel_id=1, source_target_pairs={{0,2},{2,0},{4,6},{6,4},{8,10},{10,8},{12,14},{14,12},{16,18},{18,... | collective-permute-start | bytes 98312 | tf_op jit(solution)/shard_map/ppermute | solution.py:265
  92.1 1.8 %collective-permute-done.5 = bf16[8,2048]{1,0:T(8,128)(2,1)S(1)} collective-permute-done((bf16[8,2048]{1,0:T(8,128)(2,1)S(1)}, bf16[8,2048]{1,0:T(8,128)(2,1)S(1)}, u32[]{:S(2)}, u32[]{:S(2)}) %collective-permute-start.5) | collective-permute-done | bytes 32800 | tf_op jit(solution)/shard_map/ppermute | solution.py:265
  93.9 2.1 %collective-permute-start.6 = (bf16[8,2048]{1,0:T(8,128)(2,1)S(1)}, bf16[8,2048]{1,0:T(8,128)(2,1)S(1)}, u32[]{:S(2)}, u32[]{:S(2)}) collective-permute-start(bf16[8,2048]{1,0:T(8,128)(2,1)S(1)} %fusion.4), channel_id=1, source_target_pairs={{0,4},{2,6},{4,0},{6,2},{8,12},{10,14},{12,8},{14,10},{16,20},{18,... | collective-permute-start | bytes 98312 | tf_op jit(solution)/shard_map/ppermute | solution.py:265
  96.0 0.7 collective-permute-done.10
  97.1 1.2 %collective-permute-done.6 = bf16[8,2048]{1,0:T(8,128)(2,1)S(1)} collective-permute-done((bf16[8,2048]{1,0:T(8,128)(2,1)S(1)}, bf16[8,2048]{1,0:T(8,128)(2,1)S(1)}, u32[]{:S(2)}, u32[]{:S(2)}) %collective-permute-start.6) | collective-permute-done | bytes 32800 | tf_op jit(solution)/shard_map/ppermute | solution.py:265
  98.3 2.8 %collective-permute-start.7 = (bf16[8,2048]{1,0:T(8,128)(2,1)S(1)}, bf16[8,2048]{1,0:T(8,128)(2,1)S(1)}, u32[]{:S(2)}, u32[]{:S(2)}) collective-permute-start(bf16[8,2048]{1,0:T(8,128)(2,1)S(1)} %fusion.5), channel_id=1, source_target_pairs={{0,8},{2,10},{4,12},{6,14},{8,0},{10,2},{12,4},{14,6},{16,24},{18,... | collective-permute-start | bytes 98312 | tf_op jit(solution)/shard_map/ppermute | solution.py:265
  101.5 1.6 %collective-permute-start.12 = (bf16[24,2048]{1,0:T(8,128)(2,1)S(1)}, bf16[24,2048]{1,0:T(8,128)(2,1)S(1)}, u32[]{:S(2)}, u32[]{:S(2)}) collective-permute-start(bf16[24,2048]{1,0:T(8,128)(2,1)S(1)} %fusion.1), channel_id=1, source_target_pairs={{0,8},{2,10},{4,12},{6,14},{8,0},{10,2},{12,4},{14,6},{16,24},{18,... | collective-permute-start | bytes 294920 | tf_op jit(solution)/shard_map/ppermute | solution.py:265
  103.2 3.2 %collective-permute-start.8 = (bf16[8,2048]{1,0:T(8,128)(2,1)S(1)}, bf16[8,2048]{1,0:T(8,128)(2,1)S(1)}, u32[]{:S(2)}, u32[]{:S(2)}) collective-permute-start(bf16[8,2048]{1,0:T(8,128)(2,1)S(1)} %get-tuple-element.37), channel_id=1, source_target_pairs={{0,16},{2,18},{4,20},{6,22},{8,24},{10,26},{12,28},{14,30},{16,0},... | collective-permute-start | bytes 98312 | tf_op jit(solution)/shard_map/ppermute | solution.py:265
  106.4 3.2 %collective-permute-start.13 = (bf16[24,2048]{1,0:T(8,128)(2,1)S(1)}, bf16[24,2048]{1,0:T(8,128)(2,1)S(1)}, u32[]{:S(2)}, u32[]{:S(2)}) collective-permute-start(bf16[24,2048]{1,0:T(8,128)(2,1)S(1)} %fusion.2), channel_id=1, source_target_pairs={{0,16},{2,18},{4,20},{6,22},{8,24},{10,26},{12,28},{14,30},{16,0},... | collective-permute-start | bytes 294920 | tf_op jit(solution)/shard_map/ppermute | solution.py:265
  109.6 3.6 %collective-permute-done.13 = bf16[24,2048]{1,0:T(8,128)(2,1)S(1)} collective-permute-done((bf16[24,2048]{1,0:T(8,128)(2,1)S(1)}, bf16[24,2048]{1,0:T(8,128)(2,1)S(1)}, u32[]{:S(2)}, u32[]{:S(2)}) %collective-permute-start.13) | collective-permute-done | bytes 98336 | tf_op jit(solution)/shard_map/ppermute | solution.py:265
  113.5 0.7 pad_maximum_fusion.1
  (93 shorter events, 3.8 us)
Async XLA Ops:
  0.6 1.1 copy-start
  1.8 1.1 copy-start.2
  2.9 0.9 copy-start.5
  3.8 1.1 copy-start.7
  5.0 1.1 copy-start.9
  6.1 28.0 %copy-start.1 = (bf16[192,2048]{1,0:T(8,128)(2,1)S(1)}, bf16[192,2048]{1,0:T(8,128)(2,1)}, u32[]{:S(2)}) copy-start(bf16[192,2048]{1,0:T(8,128)(2,1)} %q.5) | copy-start | bytes 2359300
  6.1 28.0 %copy-start.3 = (bf16[192,2048]{1,0:T(8,128)(2,1)S(1)}, bf16[192,2048]{1,0:T(8,128)(2,1)}, u32[]{:S(2)}) copy-start(bf16[192,2048]{1,0:T(8,128)(2,1)} %g.5) | copy-start | bytes 2359300
  6.1 28.0 %copy-start.6 = (f32[3,7,2048]{2,1,0:T(8,128)S(1)}, f32[3,7,2048]{2,1,0:T(8,128)}, u32[]{:S(2)}) copy-start(f32[3,7,2048]{2,1,0:T(8,128)} %w.7) | copy-start | bytes 516100
  6.1 28.0 %copy-start.8 = (bf16[192,2048]{1,0:T(8,128)(2,1)S(1)}, bf16[192,2048]{1,0:T(8,128)(2,1)}, u32[]{:S(2)}) copy-start(bf16[192,2048]{1,0:T(8,128)(2,1)} %k.5) | copy-start | bytes 2359300
  6.1 28.0 %copy-start.10 = (bf16[192,2048]{1,0:T(8,128)(2,1)S(1)}, bf16[192,2048]{1,0:T(8,128)(2,1)}, u32[]{:S(2)}) copy-start(bf16[192,2048]{1,0:T(8,128)(2,1)} %v.5) | copy-start | bytes 2359300
  6.1 28.0 %copy-start.11 = (bf16[128,768]{1,0:T(8,128)(2,1)S(1)}, bf16[128,768]{1,0:T(8,128)(2,1)}, u32[]{:S(2)}) copy-start(bf16[128,768]{1,0:T(8,128)(2,1)} %constant.42.clone.high) | copy-start | bytes 589828
  11.0 38.0 %collective-permute-start.4 = (bf16[128,2048]{1,0:T(8,128)(2,1)}, bf16[128,2048]{1,0:T(8,128)(2,1)}, u32[]{:S(2)}, u32[]{:S(2)}) collective-permute-start(bf16[128,2048]{1,0:T(8,128)(2,1)} %get-tuple-element.29), channel_id=1, source_target_pairs={{2,0},{4,2},{6,4},{8,6},{10,8},{12,10},{14,12},{16,14},{18,16},{20... | collective-permute-start | bytes 1572872 | tf_op jit(solution)/shard_map/ppermute | solution.py:232
  14.4 8.1 %collective-permute-start.2 = (bf16[128,128]{1,0:T(8,128)(2,1)}, bf16[128,128]{1,0:T(8,128)(2,1)}, u32[]{:S(2)}, u32[]{:S(2)}) collective-permute-start(bf16[128,128]{1,0:T(8,128)(2,1)} %get-tuple-element.40), channel_id=1, source_target_pairs={{0,1},{1,0},{2,3},{3,2},{4,5},{5,4},{6,7},{7,6},{8,9},{9,8},{10,11... | collective-permute-start | bytes 98312 | tf_op jit(solution)/shard_map/ppermute | solution.py:241
  14.9 19.2 %collective-permute-start.1 = (bf16[32,2048]{1,0:T(8,128)(2,1)}, bf16[32,2048]{1,0:T(8,128)(2,1)}, u32[]{:S(2)}, u32[]{:S(2)}) collective-permute-start(bf16[32,2048]{1,0:T(8,128)(2,1)} %copy-done.14), channel_id=1, source_target_pairs={{2,0},{4,2},{6,4},{8,6},{10,8},{12,10},{14,12},{16,14},{18,16},{20... | collective-permute-start | bytes 393224 | tf_op jit(solution)/shard_map/ppermute | solution.py:232
  16.2 17.9 %collective-permute-start = (bf16[24,2048]{1,0:T(8,128)(2,1)}, bf16[24,2048]{1,0:T(8,128)(2,1)}, u32[]{:S(2)}, u32[]{:S(2)}) collective-permute-start(bf16[24,2048]{1,0:T(8,128)(2,1)} %copy-done.15), channel_id=1, source_target_pairs={{0,2},{2,4},{4,6},{6,8},{8,10},{10,12},{12,14},{14,16},{16,18},{18... | collective-permute-start | bytes 294920 | tf_op jit(solution)/shard_map/ppermute | solution.py:232
  35.1 0.9 copy-start.16
  36.0 0.9 copy-start.18
  36.9 12.0 %copy-start.13 = (bf16[256,256]{1,0:T(8,128)(2,1)S(1)}, bf16[256,256]{1,0:T(8,128)(2,1)}, u32[]{:S(2)}) copy-start(bf16[256,256]{1,0:T(8,128)(2,1)} %constant.40.clone.half) | copy-start | bytes 393220
  37.0 12.0 %copy-start.17 = (bf16[256,512]{1,0:T(8,128)(2,1)S(1)}, bf16[256,512]{1,0:T(8,128)(2,1)}, u32[]{:S(2)}) copy-start(bf16[256,512]{1,0:T(8,128)(2,1)} %constant.39.clone.whole) | copy-start | bytes 786436
  37.0 12.1 %copy-start.19 = (bf16[128,768]{1,0:T(8,128)(2,1)S(1)}, bf16[128,768]{1,0:T(8,128)(2,1)}, u32[]{:S(2)}) copy-start(bf16[128,768]{1,0:T(8,128)(2,1)} %constant.41.clone.low) | copy-start | bytes 589828
  49.0 1.4 %copy-start.20 = (f32[200,2048]{1,0:T(8,128)S(1)}, f32[200,2048]{1,0:T(8,128)}, u32[]{:S(2)}) copy-start(f32[200,2048]{1,0:T(8,128)} %get-tuple-element.28.ggi) | copy-start | bytes 4915204
  50.4 30.7 %copy-start.4 = (f32[200,2048]{1,0:T(8,128)S(1)}, f32[200,2048]{1,0:T(8,128)}, u32[]{:S(2)}) copy-start(f32[200,2048]{1,0:T(8,128)} %get-tuple-element.23.inner) | copy-start | bytes 4915204
  64.9 4.6 %collective-permute-start.9 = (bf16[128,128]{1,0:T(8,128)(2,1)S(1)}, bf16[128,128]{1,0:T(8,128)(2,1)S(1)}, u32[]{:S(2)}, u32[]{:S(2)}) collective-permute-start(bf16[128,128]{1,0:T(8,128)(2,1)S(1)} %dynamic-slice_convert_fusion), channel_id=1, source_target_pairs={{0,1},{1,0},{2,3},{3,2},{4,5},{5,4},{6,7},{7,6},{8,9},{9,8},{10,11... | collective-permute-start | bytes 98312 | tf_op jit(solution)/shard_map/ppermute | solution.py:253
  65.0 16.1 %collective-permute-start.3 = (bf16[128,2048]{1,0:T(8,128)(2,1)S(1)}, bf16[128,2048]{1,0:T(8,128)(2,1)S(1)}, u32[]{:S(2)}, u32[]{:S(2)}) collective-permute-start(bf16[128,2048]{1,0:T(8,128)(2,1)S(1)} %get-tuple-element.24), channel_id=1, source_target_pairs={{0,2},{2,4},{4,6},{6,8},{8,10},{10,12},{12,14},{14,16},{16,18},{18... | collective-permute-start | bytes 1572872 | tf_op jit(solution)/shard_map/ppermute | solution.py:232
  89.5 4.4 %collective-permute-start.5 = (bf16[8,2048]{1,0:T(8,128)(2,1)S(1)}, bf16[8,2048]{1,0:T(8,128)(2,1)S(1)}, u32[]{:S(2)}, u32[]{:S(2)}) collective-permute-start(bf16[8,2048]{1,0:T(8,128)(2,1)S(1)} %convert_element_type.58), channel_id=1, source_target_pairs={{0,2},{2,0},{4,6},{6,4},{8,10},{10,8},{12,14},{14,12},{16,18},{18,... | collective-permute-start | bytes 98312 | tf_op jit(solution)/shard_map/ppermute | solution.py:265
  92.0 4.7 %collective-permute-start.10 = (bf16[24,2048]{1,0:T(8,128)(2,1)S(1)}, bf16[24,2048]{1,0:T(8,128)(2,1)S(1)}, u32[]{:S(2)}, u32[]{:S(2)}) collective-permute-start(bf16[24,2048]{1,0:T(8,128)(2,1)S(1)} %fusion), channel_id=1, source_target_pairs={{0,2},{2,0},{4,6},{6,4},{8,10},{10,8},{12,14},{14,12},{16,18},{18,... | collective-permute-start | bytes 294920 | tf_op jit(solution)/shard_map/ppermute | solution.py:265
  93.9 4.3 %collective-permute-start.6 = (bf16[8,2048]{1,0:T(8,128)(2,1)S(1)}, bf16[8,2048]{1,0:T(8,128)(2,1)S(1)}, u32[]{:S(2)}, u32[]{:S(2)}) collective-permute-start(bf16[8,2048]{1,0:T(8,128)(2,1)S(1)} %fusion.4), channel_id=1, source_target_pairs={{0,4},{2,6},{4,0},{6,2},{8,12},{10,14},{12,8},{14,10},{16,20},{18,... | collective-permute-start | bytes 98312 | tf_op jit(solution)/shard_map/ppermute | solution.py:265
  96.7 4.7 %collective-permute-start.11 = (bf16[24,2048]{1,0:T(8,128)(2,1)S(1)}, bf16[24,2048]{1,0:T(8,128)(2,1)S(1)}, u32[]{:S(2)}, u32[]{:S(2)}) collective-permute-start(bf16[24,2048]{1,0:T(8,128)(2,1)S(1)} %fusion.6), channel_id=1, source_target_pairs={{0,4},{2,6},{4,0},{6,2},{8,12},{10,14},{12,8},{14,10},{16,20},{18,... | collective-permute-start | bytes 294920 | tf_op jit(solution)/shard_map/ppermute | solution.py:265
  98.3 4.9 %collective-permute-start.7 = (bf16[8,2048]{1,0:T(8,128)(2,1)S(1)}, bf16[8,2048]{1,0:T(8,128)(2,1)S(1)}, u32[]{:S(2)}, u32[]{:S(2)}) collective-permute-start(bf16[8,2048]{1,0:T(8,128)(2,1)S(1)} %fusion.5), channel_id=1, source_target_pairs={{0,8},{2,10},{4,12},{6,14},{8,0},{10,2},{12,4},{14,6},{16,24},{18,... | collective-permute-start | bytes 98312 | tf_op jit(solution)/shard_map/ppermute | solution.py:265
  101.5 4.9 %collective-permute-start.12 = (bf16[24,2048]{1,0:T(8,128)(2,1)S(1)}, bf16[24,2048]{1,0:T(8,128)(2,1)S(1)}, u32[]{:S(2)}, u32[]{:S(2)}) collective-permute-start(bf16[24,2048]{1,0:T(8,128)(2,1)S(1)} %fusion.1), channel_id=1, source_target_pairs={{0,8},{2,10},{4,12},{6,14},{8,0},{10,2},{12,4},{14,6},{16,24},{18,... | collective-permute-start | bytes 294920 | tf_op jit(solution)/shard_map/ppermute | solution.py:265
  103.2 6.4 %collective-permute-start.8 = (bf16[8,2048]{1,0:T(8,128)(2,1)S(1)}, bf16[8,2048]{1,0:T(8,128)(2,1)S(1)}, u32[]{:S(2)}, u32[]{:S(2)}) collective-permute-start(bf16[8,2048]{1,0:T(8,128)(2,1)S(1)} %get-tuple-element.37), channel_id=1, source_target_pairs={{0,16},{2,18},{4,20},{6,22},{8,24},{10,26},{12,28},{14,30},{16,0},... | collective-permute-start | bytes 98312 | tf_op jit(solution)/shard_map/ppermute | solution.py:265
  106.4 6.8 %collective-permute-start.13 = (bf16[24,2048]{1,0:T(8,128)(2,1)S(1)}, bf16[24,2048]{1,0:T(8,128)(2,1)S(1)}, u32[]{:S(2)}, u32[]{:S(2)}) collective-permute-start(bf16[24,2048]{1,0:T(8,128)(2,1)S(1)} %fusion.2), channel_id=1, source_target_pairs={{0,16},{2,18},{4,20},{6,22},{8,24},{10,26},{12,28},{14,30},{16,0},... | collective-permute-start | bytes 294920 | tf_op jit(solution)/shard_map/ppermute | solution.py:265
  (4 other events, 2.9 us)

commit v2 on v1

v2 whole, which is shorter than its diff:
```python
import numpy as np
import jax
import jax.numpy as jnp
from jax import lax
from jax.experimental import pallas as pl
from jax.experimental.pallas import tpu as pltpu
from jax.sharding import PartitionSpec as P


HALO = 8
BLOCK = 128
WINDOW = 2 * BLOCK
F32 = jnp.float32
BF16 = jnp.bfloat16


def split_terms(matrix):
    high = matrix.astype(BF16)
    low = (matrix - high.astype(np.float32)).astype(BF16)
    return np.asarray(high), np.asarray(low)


def transforms():
    time = np.arange(WINDOW)
    freq = np.arange(BLOCK)
    angle = 2 * np.pi * ((freq[:, None] * time[None, :]) % WINDOW) / WINDOW
    cosine, sine = np.cos(angle), np.sin(angle)
    nyquist = np.where(time % 2 == 0, 1.0, -1.0)
    forward = np.concatenate([cosine, -sine]).astype(np.float64)
    forward[BLOCK] = nyquist
    scale = np.full(WINDOW, 2.0 / WINDOW)
    scale[0] = scale[BLOCK] = 1.0 / WINDOW
    inverse = forward.T * scale[None, :]
    f_high, f_low = split_terms(forward.astype(np.float32))
    i_high, i_low = split_terms(inverse.astype(np.float32))
    whole = np.concatenate([f_high, f_low], axis=1)
    half = np.concatenate([f_high[:, :BLOCK], f_low[:, :BLOCK]], axis=1)
    back = np.concatenate([i_high, i_low], axis=1)
    return whole, half, back[:BLOCK], back[BLOCK:]


def dot(left, right):
    return jnp.dot(left, right, preferred_element_type=F32)


def to_spectrum(matrix, rows):
    return dot(matrix, jnp.concatenate([rows, rows], axis=0))


def from_spectrum(matrix, real, imag):
    whole = jnp.concatenate([real, imag], axis=0).astype(BF16)
    return to_spectrum(matrix, whole)


def times(spec, taps):
    xr, xi = spec[:BLOCK], spec[BLOCK:]
    return xr * taps[0] - xi * taps[1], xr * taps[1] + xi * taps[2]


def times_conj(spec, taps):
    xr, xi = spec[:BLOCK], spec[BLOCK:]
    return xr * taps[0] + xi * taps[1], xi * taps[2] - xr * taps[1]


def rounded(value):
    return value.astype(BF16).astype(F32)


LANES = 128
CHUNK = 64


def halves(width):
    return [(at // LANES, slice(at, at + LANES)) for at in range(0, width, LANES)]


def pieces(count):
    return [(at, min(CHUNK, count - at)) for at in range(0, count, CHUNK)]


def put(ref, at, value):
    for h, lanes in halves(value.shape[1]):
        ref[h, at : at + value.shape[0]] = value[:, lanes]


def causal(ref, h, at, count, weights):
    total = None
    for j, weight in enumerate(weights):
        term = weight * ref[h, at - j : at - j + count]
        total = term if total is None else total + term
    return total


def anticausal(ref, h, at, count, weights):
    total = None
    for j, weight in enumerate(weights):
        term = weight * ref[h, at + j : at + j + count]
        total = term if total is None else total + term
    return total


def taps_of(w, index, lanes):
    return [w[index, j : j + 1, lanes] for j in range(w.shape[1])]


def lag_sums(grad, g_at, x, x_at, h, count, taps):
    totals = [None] * taps
    for at, size in pieces(count):
        mine = grad[h, g_at + at : g_at + at + size]
        for j in range(taps):
            prod = mine * x[h, x_at + at - j : x_at + at - j + size]
            part = jnp.sum(prod.reshape(size // 8, 8, LANES), axis=0)
            totals[j] = part if totals[j] is None else totals[j] + part
    rows = [jnp.sum(t, axis=0, keepdims=True) for t in totals]
    return jnp.concatenate(rows + [jnp.zeros_like(rows[0])], axis=0)


def first_kernel(q, g, q_tail, k_tail, v_tail, k_head, v_head, w, tails, ahead, xq):
    tails[...] = jnp.concatenate(
        [x[...].astype(F32)[HALO:] for x in (q_tail, k_tail, v_tail)], axis=0
    ).astype(BF16)
    put(xq, 0, q[...].astype(F32))
    grad = g[...].astype(F32)
    heads = [x[: 2 * HALO, :].astype(F32)[:HALO] for x in (q, k_head, v_head, g)]
    ahead[: 4 * HALO] = jnp.concatenate(heads, axis=0).astype(BF16)
    for h, lanes in halves(q.shape[1]):
        weights = taps_of(w, 0, lanes)
        for at, size in pieces(BLOCK):
            qs = causal(xq, h, HALO + at, size, weights)
            ahead[4 * HALO + at : 4 * HALO + at + size, lanes] = (
                grad[HALO + at : HALO + at + size, lanes] * qs
            ).astype(BF16)


def second_kernel(
    q, k, v, g, tails, w, taps, half, low,
    gated_out, ggi_out, ks_out, vs_out, inner_out, behind_out, spec_out,
    xq, xk, xv, tap_spec,
):
    rows, width = q.shape

    @pl.when(pl.program_id(0) == 0)
    def _():
        both = jnp.concatenate([taps[...], taps[...]], axis=1)
        spec = lax.dot_general(half[...], both, (((1,), (1,)), ((), ())), preferred_element_type=F32)
        real, imag = spec[:BLOCK], spec[BLOCK:]
        first = lax.broadcasted_iota(jnp.int32, real.shape, 0) == 0
        tap_spec[0] = real
        tap_spec[1] = jnp.where(first, 0.0, imag)
        tap_spec[2] = jnp.where(first, imag, real)
        spec_out[...] = tap_spec[...]

    tail = tails[...].astype(F32)
    for at, (ref, x) in enumerate(((xq, q), (xk, k), (xv, v))):
        put(ref, 0, tail[at * HALO : (at + 1) * HALO])
        put(ref, HALO, x[...].astype(F32))
    for h, lanes in halves(width):
        wq, wk, wv = (taps_of(w, i, lanes) for i in range(3))
        for at, size in pieces(rows):
            span = slice(at, at + size)
            ks = causal(xk, h, HALO + at, size, wk)
            vs = causal(xv, h, HALO + at, size, wv)
            ks_out[span, lanes] = ks
            vs_out[span, lanes] = vs
            gated_out[span, lanes] = (ks * vs).astype(BF16)
            qs = causal(xq, h, HALO + at, size, wq)
            ggi_out[span, lanes] = (g[span, lanes].astype(F32) * qs).astype(BF16)
    behind_out[...] = gated_out[rows - BLOCK :, :]
    first = to_spectrum(half[...], gated_out[:BLOCK, :])
    inner_out[...] = from_spectrum(low[...], *times(first, tap_spec))


def third_kernel(
    q, k, v, g, tails, ahead, gated, ggi, ks, vs, w, spec, half, whole, low, high,
    gk_out, gv_out, gq_out, next_out, sums_out, medium_out,
    xq, xk, xv, yq, yk, yv, acc,
):
    rows, width = k.shape
    rest = rows - BLOCK
    step = pl.program_id(0)
    count = w.shape[1]

    @pl.when(step == 0)
    def _():
        acc[...] = jnp.zeros_like(acc)

    tail = tails[...].astype(F32)
    head = ahead[: 4 * HALO, :].astype(F32)
    for at, (ref, x) in enumerate(((xq, q), (xk, k), (xv, v))):
        put(ref, 0, tail[at * HALO : (at + 1) * HALO])
        put(ref, HALO, x[...].astype(F32))
        put(ref, HALO + rows, head[at * HALO : (at + 1) * HALO])
    gated_new, ggi_new, ks_new, vs_new = [], [], [], []
    for h, lanes in halves(width):
        kn, vn, qn = (
            causal(ref, h, HALO + rows, HALO, taps_of(w, i, lanes))
            for ref, i in ((xk, 1), (xv, 2), (xq, 0))
        )
        ks_new.append(kn)
        vs_new.append(vn)
        gated_new.append(kn * vn)
        ggi_new.append(head[3 * HALO :, lanes] * qn)
    ks_new, vs_new, gated_new, ggi_new = (
        jnp.concatenate(x, axis=1) for x in (ks_new, vs_new, gated_new, ggi_new)
    )
    blank = jnp.zeros((WINDOW - rows - HALO, width), F32)
    rest_new = jnp.concatenate([gated_new, blank], axis=0).astype(BF16)
    window = jnp.concatenate([gated[...], rest_new], axis=0)
    sig = from_spectrum(high[: rest + HALO, :], *times(to_spectrum(whole[...], window), spec))
    put(yq, 0, rounded(g[BLOCK:, :].astype(F32) * sig[:rest]))
    put(yq, rest, rounded(head[3 * HALO :] * sig[rest:]))
    for h, lanes in halves(width):
        next_out[:, lanes] = yq[h, :HALO]

    fill = 3 * BLOCK - rows - HALO - BLOCK
    later = jnp.concatenate(
        [ggi_new, ahead[4 * HALO :, :].astype(F32), jnp.zeros((fill, width), F32)], axis=0
    ).astype(BF16)
    ggi_ext = jnp.concatenate([ggi[...], later], axis=0)
    own = jnp.concatenate([gated[...], jnp.zeros((WINDOW - rows, width), BF16)], axis=0)
    for at in range(2):
        win = to_spectrum(whole[...], ggi_ext[at * BLOCK : at * BLOCK + WINDOW])
        gs = to_spectrum(half[...], own[at * BLOCK : (at + 1) * BLOCK])
        acc[0] += gs[:BLOCK] * win[:BLOCK]
        acc[1] += gs[BLOCK:] * win[BLOCK:]
        acc[2] += gs[:BLOCK] * win[BLOCK:] - gs[BLOCK:] * win[:BLOCK]
        prod = times_conj(win, spec)
        if at == 0:
            gg = from_spectrum(low[...], *prod)
            put(yk, 0, rounded(gg * vs[:BLOCK, :]))
            put(yv, 0, rounded(gg * ks[:BLOCK, :]))
        else:
            gg = from_spectrum(low[: rest + HALO, :], *prod)
            put(yk, BLOCK, rounded(gg[:rest] * vs[BLOCK:, :]))
            put(yv, BLOCK, rounded(gg[:rest] * ks[BLOCK:, :]))
            put(yk, rows, rounded(gg[rest:] * vs_new))
            put(yv, rows, rounded(gg[rest:] * ks_new))
    for h, lanes in halves(width):
        for i, ref, out in ((1, yk, gk_out), (2, yv, gv_out)):
            weights = taps_of(w, i, lanes)
            for at, size in pieces(rows):
                out[at : at + size, lanes] = anticausal(ref, h, at, size, weights).astype(BF16)
        gq_out[:, lanes] = anticausal(yq, h, 0, rest, taps_of(w, 0, lanes)).astype(BF16)
        sums_out[:HALO, lanes] = lag_sums(yk, 0, xk, HALO, h, rows, count)
        sums_out[HALO : 2 * HALO, lanes] = lag_sums(yv, 0, xv, HALO, h, rows, count)
        sums_out[2 * HALO :, lanes] = lag_sums(yq, 0, xq, HALO + BLOCK, h, rest, count)

    @pl.when(step == pl.num_programs(0) - 1)
    def _():
        first = lax.broadcasted_iota(jnp.int32, (BLOCK, width), 0) == 0
        real = acc[0] + jnp.where(first, 0.0, acc[1])
        imag = jnp.where(first, acc[1], acc[2])
        medium_out[...] = from_spectrum(low[...], real, imag).T


def fourth_kernel(
    q, g, tails, inner, behind, following, sums, w, spec, half, high, gq_in,
    gq_out, sums_out,
    xq, yq,
):
    width = q.shape[1]
    put(xq, 0, tails[...].astype(F32)[:HALO])
    put(xq, HALO, q[...].astype(F32))
    edge = from_spectrum(high[...], *times(to_spectrum(half[...], behind[...]), spec))
    put(yq, 0, rounded(g[...].astype(F32) * (inner[...] + edge)))
    put(yq, BLOCK, following[...])
    for h, lanes in halves(width):
        weights = taps_of(w, 0, lanes)
        for at, size in pieces(BLOCK):
            gq_out[at : at + size, lanes] = anticausal(yq, h, at, size, weights).astype(BF16)
        sums_out[:, lanes] = sums[:, lanes] + lag_sums(yq, 0, xq, HALO, h, BLOCK, w.shape[1])


def shift(value, axis, steps):
    count = lax.axis_size(axis)
    initial, last = (max(0, -steps), min(count, count - steps))
    return lax.ppermute(value, axis, [(s, s + steps) for s in range(initial, last)])


def gather_rows(value, axis):
    count, rows = lax.axis_size(axis), value.shape[0]
    me = lax.axis_index(axis)
    result = jnp.zeros((count * rows, value.shape[1]), value.dtype)
    result = lax.dynamic_update_slice(result, value, (me * rows, 0))
    for step in range(1, count):
        other = lax.ppermute(value, axis, [(s, (s + step) % count) for s in range(count)])
        result = lax.dynamic_update_slice(result, other, ((me - step) % count * rows, 0))
    return result


def scatter_sum(value, axis):
    count = lax.axis_size(axis)
    rows = value.shape[0] // count
    me = lax.axis_index(axis)
    total = lax.dynamic_slice(value, (me * rows, 0), (rows, value.shape[1]))
    for step in range(1, count):
        part = lax.dynamic_slice(value, ((me + step) % count * rows, 0), (rows, value.shape[1]))
        total = total + lax.ppermute(
            part.astype(BF16), axis, [(s, (s + step) % count) for s in range(count)]
        ).astype(F32)
    return total


def sum_over(value, axis):
    count = lax.axis_size(axis)
    if count & (count - 1):
        return lax.psum(value, axis)
    distance = 1
    while distance < count:
        other = lax.ppermute(value.astype(BF16), axis, [(s, s ^ distance) for s in range(count)])
        value = value + other.astype(F32)
        distance *= 2
    return value


def shards(query, key, value, grad_out, short_filter, medium_filter):
    rows, channels = query.shape
    groups = medium_filter.shape[0] * lax.axis_size("fsdp")
    width, tiles = groups, channels // groups
    rest = rows - BLOCK
    taps_short = short_filter.shape[1]
    whole, half, low, high = (jnp.asarray(m) for m in transforms())

    def col(count, at=0, wide=width):
        return pl.BlockSpec((count, wide), lambda i: (at, i))

    def fixed(shape):
        return pl.BlockSpec(shape, lambda i: (0,) * len(shape))

    def filters(wide=width):
        return pl.BlockSpec((3, taps_short, wide), lambda i: (0, 0, i))

    def out(count, dtype):
        return jax.ShapeDtypeStruct((count, channels), dtype)

    def scratch(count, wide=width):
        return pltpu.VMEM((wide // LANES, count, LANES), F32)

    def cost(flops, moved):
        return pl.CostEstimate(flops=int(flops), bytes_accessed=int(moved), transcendentals=0)

    wide = 2 * width
    last = rows // (2 * HALO) - 1
    tails, ahead = pl.pallas_call(
        first_kernel,
        grid=(channels // wide,),
        in_specs=[col(BLOCK + 2 * HALO, 0, wide)] * 2
        + [col(2 * HALO, last, wide)] * 3
        + [col(2 * HALO, 0, wide)] * 2
        + [filters(wide)],
        out_specs=[col(3 * HALO, 0, wide), col(BLOCK + 4 * HALO, 0, wide)],
        out_shape=[out(3 * HALO, BF16), out(BLOCK + 4 * HALO, BF16)],
        scratch_shapes=[scratch(BLOCK + 2 * HALO, wide)],
        name="first",
    )(query, grad_out, query, key, value, key, value, short_filter)
    tails = shift(tails, "seq", 1)
    ahead = shift(ahead, "seq", -1)
    taps = gather_rows(medium_filter.astype(BF16), "fsdp")

    gated, ggi, ks, vs, inner, behind, spec = pl.pallas_call(
        second_kernel,
        grid=(tiles,),
        in_specs=[col(rows)] * 4
        + [col(3 * HALO), filters(), fixed(taps.shape), fixed(half.shape), fixed(low.shape)],
        out_specs=[col(rows)] * 4 + [col(BLOCK), col(BLOCK), fixed((3, BLOCK, width))],
        out_shape=[
            out(rows, BF16), out(rows, BF16), out(rows, F32), out(rows, F32),
            out(BLOCK, F32), out(BLOCK, BF16), jax.ShapeDtypeStruct((3, BLOCK, width), F32),
        ],
        scratch_shapes=[scratch(rows + HALO)] * 3 + [pltpu.VMEM((3, BLOCK, width), F32)],
        cost_estimate=cost(4e9, 20e6),
        name="second",
    )(query, key, value, grad_out, tails, short_filter, taps, half, low)
    behind = shift(behind, "seq", 1)

    grad_key, grad_value, grad_query, following, sums, medium = pl.pallas_call(
        third_kernel,
        grid=(tiles,),
        in_specs=[col(rows)] * 4
        + [col(3 * HALO), col(BLOCK + 4 * HALO)]
        + [col(rows)] * 4
        + [filters(), fixed((3, BLOCK, width))]
        + [fixed(m.shape) for m in (half, whole, low, high)],
        out_specs=[
            col(rows), col(rows), col(rest, BLOCK // rest), col(HALO), col(3 * HALO),
            fixed((width, BLOCK)),
        ],
        out_shape=[
            out(rows, BF16), out(rows, BF16), out(rows, BF16), out(HALO, F32),
            out(3 * HALO, F32), jax.ShapeDtypeStruct((width, BLOCK), F32),
        ],
        scratch_shapes=[scratch(rows + 2 * HALO)] * 3
        + [scratch(rest + 2 * HALO)]
        + [scratch(rows + 2 * HALO)] * 2
        + [pltpu.VMEM((3, BLOCK, width), F32)],
        cost_estimate=cost(8e9, 30e6),
        name="third",
    )(query, key, value, grad_out, tails, ahead, gated, ggi, ks, vs, short_filter, spec,
      half, whole, low, high)

    grad_query, sums_q = pl.pallas_call(
        fourth_kernel,
        grid=(tiles,),
        in_specs=[col(BLOCK)] * 2
        + [col(3 * HALO), col(BLOCK), col(BLOCK), col(HALO), col(HALO, 2), filters()]
        + [fixed((3, BLOCK, width)), fixed(half.shape), fixed(high.shape)]
        + [pl.BlockSpec(memory_space=pl.ANY)],
        out_specs=[col(BLOCK), col(HALO)],
        out_shape=[out(rows, BF16), out(HALO, F32)],
        scratch_shapes=[scratch(BLOCK + HALO)] * 2,
        input_output_aliases={11: 0},
        cost_estimate=cost(2e9, 8e6),
        name="fourth",
    )(query, grad_out, tails, inner, behind, following, sums, short_filter, spec, half, high,
      grad_query)

    medium = scatter_sum(medium, "fsdp")
    per = channels // BLOCK
    count = medium.shape[0] // per
    packed = jnp.concatenate([medium[i * count : (i + 1) * count] for i in range(per)], axis=1)
    early = jnp.concatenate([sums[: 2 * HALO], packed], axis=0)
    early = sum_over(early, "seq")
    sums_q = sum_over(sums_q, "seq")
    packed = early[2 * HALO :]
    grad_medium = jnp.concatenate([packed[:, i * BLOCK : (i + 1) * BLOCK] for i in range(per)], axis=0)
    grad_short = jnp.stack([sums_q[:taps_short], early[:taps_short], early[HALO : HALO + taps_short]])
    return grad_query, grad_key, grad_value, grad_short, grad_medium


def solution(mesh):
    in_specs = (
        P("seq", "fsdp"),
        P("seq", "fsdp"),
        P("seq", "fsdp"),
        P("seq", "fsdp"),
        P(None, None, "fsdp"),
        P("fsdp", None),
    )
    out_specs = (
        P("seq", "fsdp"),
        P("seq", "fsdp"),
        P("seq", "fsdp"),
        P(None, None, "fsdp"),
        P("fsdp", None),
    )
    return jax.shard_map(shards, mesh=mesh, in_specs=in_specs, out_specs=out_specs, check_vma=False)
```

time: 115 us -> 94.3 us (0.82)
  local copies, waits for them, and re-layouts: 13.1 us -> 3.31 us
  starting transfers between devices: 29.8 us -> 20.7 us
  Pallas kernels: 38.3 us -> 36.6 us
  waiting for transfers between devices: 29.5 us -> 28.1 us
    unnamed x74 -> x48, local copies, waits for them, and re-layouts: 11.1 us -> 2.41 us
    ppermute x8, starting transfers between devices: 15.9 us -> 9.49 us  [sum_over(): lax.ppermute(value.astype(BF16), axis, [(s, s ^ distance) for s in range(...]
    ppermute x4 -> x3, waiting for transfers between devices: 21.8 us -> 16.1 us  [shift(): lax.ppermute(value, axis, [(s, s + steps) for s in range(initial, last)])]
    ppermute x8, waiting for transfers between devices: 7.68 us -> 12 us  [sum_over(): lax.ppermute(value.astype(BF16), axis, [(s, s ^ distance) for s in range(...]
    ppermute x4 -> x3, starting transfers between devices: 13.2 us -> 10.6 us  [shift(): lax.ppermute(value, axis, [(s, s + steps) for s in range(initial, last)])]
    pallas_call x1, Pallas kernels: 12 us -> 9.41 us  [shards(): pl.pallas_call(second_kernel, grid=(tiles,), in_specs=[col(rows)] * 4 + [...]
    convert_element_type x8, other arithmetic: 0.16 us -> 2.73 us  [sum_over(): value.astype(BF16)]
    dynamic_update_slice x1, other arithmetic: 1.47 us -> 0.03 us  [gather_rows(): result = lax.dynamic_update_slice(result, value, (me * rows, 0))]
  transfers between devices with their start and end apart: 14 -> 13, of which waited for: 8 -> 7; matrix products, arithmetic and copies ran while one was open for 3% -> 4% of each run, Pallas kernels for 11% -> 35%
where the time goes in v2:
time: 94.3 us; the launch traced here: 93.4 us
  Pallas kernels  36.6 us (39%)
  waiting for transfers between devices  28.1 us (30%)
  starting transfers between devices  20.7 us (22%)
  other arithmetic  3.53 us (4%)
  local copies, waits for them, and re-layouts  3.31 us (4%)
  between operations  1.13 us (1%)
    ppermute x3, waiting for transfers between devices, shift(): lax.ppermute(value, axis, [(s, s + steps) for s in range(initial, last)])  16.1 us
    pallas_call x1, Pallas kernels, shards(): pl.pallas_call(third_kernel, grid=(tiles,), in_specs=[col(rows)] * 4 + [c...  15.4 us
    ppermute x8, waiting for transfers between devices, sum_over(): lax.ppermute(value.astype(BF16), axis, [(s, s ^ distance) for s in range(...  12 us
    ppermute x3, starting transfers between devices, shift(): lax.ppermute(value, axis, [(s, s + steps) for s in range(initial, last)])  10.6 us
    ppermute x8, starting transfers between devices, sum_over(): lax.ppermute(value.astype(BF16), axis, [(s, s ^ distance) for s in range(...  9.49 us
    pallas_call x1, Pallas kernels, shards(): pl.pallas_call(second_kernel, grid=(tiles,), in_specs=[col(rows)] * 4 + [...  9.41 us
    pallas_call x1, Pallas kernels, shards(): pl.pallas_call(fourth_kernel, grid=(tiles,), in_specs=[col(BLOCK)] * 2 +...  8.07 us
    pallas_call x1, Pallas kernels, shards(): pl.pallas_call(first_kernel, grid=(channels // wide,), in_specs=[col(BLOC...  3.79 us
  transfers between devices with their start and end apart: 13, of which 7 were waited for; matrix products, arithmetic and copies ran while one was open for 4% of the time, Pallas kernels for 35%

profile of v2, /device:TPU:0, one launch (start us, length us, event | category | flops | bytes accessed | tf_op | source)
XLA Modules:
  0.0 93.4 jit_solution(6238327419949395168)
XLA Ops:
  0.6 3.8 %first.1 = (bf16[24,2048]{1,0:T(8,128)(2,1)}, bf16[160,2048]{1,0:T(8,128)(2,1)}) custom-call(bf16[192,2048]{1,0:T(8,128)(2,1)} %q.7, bf16[192,2048]{1,0:T(8,128)(2,1)} %g.7, bf16[192,2048]{1,0:T(8,128)(2,1)} %q.7, bf16[192,2048]{1,0:T(8,128)(2,1)} %k.3, bf16[192,2048]{1,0:T(8,128)(2,1)} %v.3, bf16[192,2048]{1,0:T(8,128)(2,1)} %k.3, bf16[192,2048]{1,0:T(8,128)(2,1)} %v.3, ...), custom_call_target="tpu_custom_call" | custom-call | tf_op jit(solution)/shard_map/first/pallas_call | solution.py:344
  4.4 1.3 %collective-permute-start.3 = (bf16[160,2048]{1,0:T(8,128)(2,1)}, bf16[160,2048]{1,0:T(8,128)(2,1)S(1)}, u32[]{:S(2)}, u32[]{:S(2)}) collective-permute-start(bf16[160,2048]{1,0:T(8,128)(2,1)} %get-tuple-element.25), channel_id=1, source_target_pairs={{2,0},{4,2},{6,4},{8,6},{10,8},{12,10},{14,12},{16,14},{18,16},{20... | collective-permute-start | bytes 1966088 | tf_op jit(solution)/shard_map/ppermute | solution.py:277
  5.8 0.6 collective-permute-start.1
  6.3 5.0 %collective-permute-start = (bf16[24,2048]{1,0:T(8,128)(2,1)}, bf16[24,2048]{1,0:T(8,128)(2,1)S(1)}, u32[]{:S(2)}, u32[]{:S(2)}) collective-permute-start(bf16[24,2048]{1,0:T(8,128)(2,1)} %get-tuple-element.22), channel_id=1, source_target_pairs={{0,2},{2,4},{4,6},{6,8},{8,10},{10,12},{12,14},{14,16},{16,18},{18... | collective-permute-start | bytes 294920 | tf_op jit(solution)/shard_map/ppermute | solution.py:277
  11.5 16.1 %collective-permute-done.tails = bf16[24,2048]{1,0:T(8,128)(2,1)S(1)} collective-permute-done((bf16[24,2048]{1,0:T(8,128)(2,1)}, bf16[24,2048]{1,0:T(8,128)(2,1)S(1)}, u32[]{:S(2)}, u32[]{:S(2)}) %collective-permute-start) | collective-permute-done | bytes 98336 | tf_op jit(solution)/shard_map/ppermute | solution.py:277
  27.6 0.6 copy-done.8
  28.2 9.4 %second.1 = (bf16[192,2048]{1,0:T(8,128)(2,1)}, bf16[192,2048]{1,0:T(8,128)(2,1)}, f32[192,2048]{1,0:T(8,128)}, f32[192,2048]{1,0:T(8,128)}, f32[128,2048]{1,0:T...) custom-call(bf16[192,2048]{1,0:T(8,128)(2,1)} %q.7, bf16[192,2048]{1,0:T(8,128)(2,1)} %k.3, ...), custom_call_target="tpu_custom_call" | custom-call | flops 4000000000 | bytes 20000000 | tf_op jit(solution)/shard_map/second/pallas_call | solution.py:360
  37.6 4.3 %collective-permute-start.2 = (bf16[128,2048]{1,0:T(8,128)(2,1)}, bf16[128,2048]{1,0:T(8,128)(2,1)S(1)}, u32[]{:S(2)}, u32[]{:S(2)}) collective-permute-start(bf16[128,2048]{1,0:T(8,128)(2,1)} %get-tuple-element.24), channel_id=1, source_target_pairs={{0,2},{2,4},{4,6},{6,8},{8,10},{10,12},{12,14},{14,16},{16,18},{18... | collective-permute-start | bytes 1572872 | tf_op jit(solution)/shard_map/ppermute | solution.py:277
  42.0 0.8 copy-done.6
  42.8 15.4 %third.1 = (bf16[192,2048]{1,0:T(8,128)(2,1)}, bf16[192,2048]{1,0:T(8,128)(2,1)}, bf16[192,2048]{1,0:T(8,128)(2,1)}, f32[8,2048]{1,0:T(8,128)}, f32[24,2048]{1,0:T(8,128)}, /*index=5*/f32[256,128]{1,0:T(8,128)}) custom-call(bf16[192,2048]{1,0:T(8,128)(2,1)} %q.7, bf16[192,2048]{1,0:T(8,128)(2,1)} %k.3, bf16[192,2048]{1,0:T(8,128)(2,1)} %v.3, ...), custom_call_target="tpu_custom_call" | custom-call | flops 8000000000 | bytes 30000000 | tf_op jit(solution)/shard_map/third/pallas_call | solution.py:376
  58.2 0.9 dynamic-slice_convert_fusion
  59.0 0.8 copy-done.7
  59.9 8.1 %fourth.1 = (bf16[192,2048]{1,0:T(8,128)(2,1)}, f32[8,2048]{1,0:T(8,128)}) custom-call(bf16[192,2048]{1,0:T(8,128)(2,1)} %q.7, bf16[192,2048]{1,0:T(8,128)(2,1)} %g.7, bf16[24,2048]{1,0:T(8,128)(2,1)} %copy-done.8, f32[128,2048]{1,0:T(8,128)} %get-tuple-element.23.inner, bf16[128,2048]{1,0:T(8,128)(2,1)} %copy-done.7, ...), custom_call_target="tpu_custom_call", output_to_operand_aliasing={{0}: (11, {})} | custom-call | flops 2000000000 | bytes 8000000 | tf_op jit(solution)/shard_map/fourth/pallas_call | solution.py:401
  68.0 0.9 convert_element_type.58
  68.9 0.0 collective-permute-start.4
  69.1 2.0 %collective-permute-start.9 = (bf16[24,2048]{1,0:T(8,128)(2,1)S(1)}, bf16[24,2048]{1,0:T(8,128)(2,1)S(1)}, u32[]{:S(2)}, u32[]{:S(2)}) collective-permute-start(bf16[24,2048]{1,0:T(8,128)(2,1)S(1)} %fusion), channel_id=1, source_target_pairs={{0,2},{2,0},{4,6},{6,4},{8,10},{10,8},{12,14},{14,12},{16,18},{18,... | collective-permute-start | bytes 294920 | tf_op jit(solution)/shard_map/ppermute | solution.py:310
  71.2 2.0 %collective-permute-done.4 = bf16[8,2048]{1,0:T(8,128)(2,1)S(1)} collective-permute-done((bf16[8,2048]{1,0:T(8,128)(2,1)S(1)}, bf16[8,2048]{1,0:T(8,128)(2,1)S(1)}, u32[]{:S(2)}, u32[]{:S(2)}) %collective-permute-start.4) | collective-permute-done | bytes 32800 | tf_op jit(solution)/shard_map/ppermute | solution.py:310
  73.1 0.9 fusion.4
  74.0 0.1 collective-permute-start.5
  74.0 0.7 collective-permute-done.9
  74.8 1.5 %collective-permute-start.10 = (bf16[24,2048]{1,0:T(8,128)(2,1)S(1)}, bf16[24,2048]{1,0:T(8,128)(2,1)S(1)}, u32[]{:S(2)}, u32[]{:S(2)}) collective-permute-start(bf16[24,2048]{1,0:T(8,128)(2,1)S(1)} %fusion.6), channel_id=1, source_target_pairs={{0,4},{2,6},{4,0},{6,2},{8,12},{10,14},{12,8},{14,10},{16,20},{18,... | collective-permute-start | bytes 294920 | tf_op jit(solution)/shard_map/ppermute | solution.py:310
  76.2 2.1 %collective-permute-done.5 = bf16[8,2048]{1,0:T(8,128)(2,1)S(1)} collective-permute-done((bf16[8,2048]{1,0:T(8,128)(2,1)S(1)}, bf16[8,2048]{1,0:T(8,128)(2,1)S(1)}, u32[]{:S(2)}, u32[]{:S(2)}) %collective-permute-start.5) | collective-permute-done | bytes 32800 | tf_op jit(solution)/shard_map/ppermute | solution.py:310
  78.3 0.9 fusion.5
  79.1 1.6 %collective-permute-start.6 = (bf16[8,2048]{1,0:T(8,128)(2,1)S(1)}, bf16[8,2048]{1,0:T(8,128)(2,1)S(1)}, u32[]{:S(2)}, u32[]{:S(2)}) collective-permute-start(bf16[8,2048]{1,0:T(8,128)(2,1)S(1)} %fusion.5), channel_id=1, source_target_pairs={{0,8},{2,10},{4,12},{6,14},{8,0},{10,2},{12,4},{14,6},{16,24},{18,... | collective-permute-start | bytes 98312 | tf_op jit(solution)/shard_map/ppermute | solution.py:310
  80.8 0.5 collective-permute-start.11
  81.3 1.8 %collective-permute-done.6 = bf16[8,2048]{1,0:T(8,128)(2,1)S(1)} collective-permute-done((bf16[8,2048]{1,0:T(8,128)(2,1)S(1)}, bf16[8,2048]{1,0:T(8,128)(2,1)S(1)}, u32[]{:S(2)}, u32[]{:S(2)}) %collective-permute-start.6) | collective-permute-done | bytes 32800 | tf_op jit(solution)/shard_map/ppermute | solution.py:310
  83.2 2.6 %collective-permute-start.7 = (bf16[8,2048]{1,0:T(8,128)(2,1)S(1)}, bf16[8,2048]{1,0:T(8,128)(2,1)S(1)}, u32[]{:S(2)}, u32[]{:S(2)}) collective-permute-start(bf16[8,2048]{1,0:T(8,128)(2,1)S(1)} %get-tuple-element.39), channel_id=1, source_target_pairs={{0,16},{2,18},{4,20},{6,22},{8,24},{10,26},{12,28},{14,30},{16,0},... | collective-permute-start | bytes 98312 | tf_op jit(solution)/shard_map/ppermute | solution.py:310
  85.8 1.1 %collective-permute-start.12 = (bf16[24,2048]{1,0:T(8,128)(2,1)S(1)}, bf16[24,2048]{1,0:T(8,128)(2,1)S(1)}, u32[]{:S(2)}, u32[]{:S(2)}) collective-permute-start(bf16[24,2048]{1,0:T(8,128)(2,1)S(1)} %fusion.2), channel_id=1, source_target_pairs={{0,16},{2,18},{4,20},{6,22},{8,24},{10,26},{12,28},{14,30},{16,0},... | collective-permute-start | bytes 294920 | tf_op jit(solution)/shard_map/ppermute | solution.py:310
  86.9 1.4 %collective-permute-done.7 = bf16[8,2048]{1,0:T(8,128)(2,1)S(1)} collective-permute-done((bf16[8,2048]{1,0:T(8,128)(2,1)S(1)}, bf16[8,2048]{1,0:T(8,128)(2,1)S(1)}, u32[]{:S(2)}, u32[]{:S(2)}) %collective-permute-start.7) | collective-permute-done | bytes 32800 | tf_op jit(solution)/shard_map/ppermute | solution.py:310
  88.3 4.1 %collective-permute-done.12 = bf16[24,2048]{1,0:T(8,128)(2,1)S(1)} collective-permute-done((bf16[24,2048]{1,0:T(8,128)(2,1)S(1)}, bf16[24,2048]{1,0:T(8,128)(2,1)S(1)}, u32[]{:S(2)}, u32[]{:S(2)}) %collective-permute-start.12) | collective-permute-done | bytes 98336 | tf_op jit(solution)/shard_map/ppermute | solution.py:310
  92.4 0.1 convert_add_fusion
  92.7 0.7 pad_maximum_fusion.1
  (66 shorter events, 0.4 us)
Async XLA Ops:
  0.6 5.1 %copy-start.3 = (f32[128,128]{1,0:T(8,128)S(1)}, f32[128,128]{1,0:T(8,128)}, u32[]{:S(2)}) copy-start(f32[128,128]{1,0:T(8,128)} %param.15) | copy-start | bytes 196612
  4.4 37.5 %collective-permute-start.3 = (bf16[160,2048]{1,0:T(8,128)(2,1)}, bf16[160,2048]{1,0:T(8,128)(2,1)S(1)}, u32[]{:S(2)}, u32[]{:S(2)}) collective-permute-start(bf16[160,2048]{1,0:T(8,128)(2,1)} %get-tuple-element.25), channel_id=1, source_target_pairs={{2,0},{4,2},{6,4},{8,6},{10,8},{12,10},{14,12},{16,14},{18,16},{20... | collective-permute-start | bytes 1966088 | tf_op jit(solution)/shard_map/ppermute | solution.py:277
  5.8 5.6 %collective-permute-start.1 = (bf16[128,128]{1,0:T(8,128)(2,1)S(1)}, bf16[128,128]{1,0:T(8,128)(2,1)S(1)}, u32[]{:S(2)}, u32[]{:S(2)}) collective-permute-start(bf16[128,128]{1,0:T(8,128)(2,1)S(1)} %get-tuple-element.42), channel_id=1, source_target_pairs={{0,1},{1,0},{2,3},{3,2},{4,5},{5,4},{6,7},{7,6},{8,9},{9,8},{10,11... | collective-permute-start | bytes 98312 | tf_op jit(solution)/shard_map/ppermute | solution.py:286
  6.3 21.2 %collective-permute-start = (bf16[24,2048]{1,0:T(8,128)(2,1)}, bf16[24,2048]{1,0:T(8,128)(2,1)S(1)}, u32[]{:S(2)}, u32[]{:S(2)}) collective-permute-start(bf16[24,2048]{1,0:T(8,128)(2,1)} %get-tuple-element.22), channel_id=1, source_target_pairs={{0,2},{2,4},{4,6},{6,8},{8,10},{10,12},{12,14},{14,16},{16,18},{18... | collective-permute-start | bytes 294920 | tf_op jit(solution)/shard_map/ppermute | solution.py:277
  11.4 16.1 %copy-start.4 = (bf16[256,128]{1,0:T(8,128)(2,1)}, bf16[256,128]{1,0:T(8,128)(2,1)S(1)}, u32[]{:S(2)}) copy-start(bf16[256,128]{1,0:T(8,128)(2,1)S(1)} %constant_dynamic-update-slice_fusion.32.taps) | copy-start | bytes 196612
  27.6 0.6 copy-start.8
  37.6 21.4 %collective-permute-start.2 = (bf16[128,2048]{1,0:T(8,128)(2,1)}, bf16[128,2048]{1,0:T(8,128)(2,1)S(1)}, u32[]{:S(2)}, u32[]{:S(2)}) collective-permute-start(bf16[128,2048]{1,0:T(8,128)(2,1)} %get-tuple-element.24), channel_id=1, source_target_pairs={{0,2},{2,4},{4,6},{6,8},{8,10},{10,12},{12,14},{14,16},{16,18},{18... | collective-permute-start | bytes 1572872 | tf_op jit(solution)/shard_map/ppermute | solution.py:277
  41.9 0.9 copy-start.6
  59.0 9.9 %collective-permute-start.8 = (bf16[128,128]{1,0:T(8,128)(2,1)S(1)}, bf16[128,128]{1,0:T(8,128)(2,1)S(1)}, u32[]{:S(2)}, u32[]{:S(2)}) collective-permute-start(bf16[128,128]{1,0:T(8,128)(2,1)S(1)} %dynamic-slice_convert_fusion), channel_id=1, source_target_pairs={{0,1},{1,0},{2,3},{3,2},{4,5},{5,4},{6,7},{7,6},{8,9},{9,8},{10,11... | collective-permute-start | bytes 98312 | tf_op jit(solution)/shard_map/ppermute | solution.py:298
  59.0 0.8 copy-start.7
  59.8 8.1 %copy-start.1 = (f32[24,2048]{1,0:T(8,128)S(1)}, f32[24,2048]{1,0:T(8,128)}, u32[]{:S(2)}) copy-start(f32[24,2048]{1,0:T(8,128)} %get-tuple-element.32.sums) | copy-start | bytes 589828
  59.9 9.1 %copy-start.2 = (f32[256,128]{1,0:T(8,128)S(1)}, f32[256,128]{1,0:T(8,128)}, u32[]{:S(2)}) copy-start(f32[256,128]{1,0:T(8,128)} %get-tuple-element.38) | copy-start | bytes 393220
  67.9 15.2 %copy-start = (f32[8,2048]{1,0:T(8,128)S(1)}, f32[8,2048]{1,0:T(8,128)}, u32[]{:S(2)}) copy-start(f32[8,2048]{1,0:T(8,128)} %get-tuple-element.37) | copy-start | bytes 196612
  68.9 4.3 %collective-permute-start.4 = (bf16[8,2048]{1,0:T(8,128)(2,1)S(1)}, bf16[8,2048]{1,0:T(8,128)(2,1)S(1)}, u32[]{:S(2)}, u32[]{:S(2)}) collective-permute-start(bf16[8,2048]{1,0:T(8,128)(2,1)S(1)} %convert_element_type.58), channel_id=1, source_target_pairs={{0,2},{2,0},{4,6},{6,4},{8,10},{10,8},{12,14},{14,12},{16,18},{18,... | collective-permute-start | bytes 98312 | tf_op jit(solution)/shard_map/ppermute | solution.py:310
  69.1 5.6 %collective-permute-start.9 = (bf16[24,2048]{1,0:T(8,128)(2,1)S(1)}, bf16[24,2048]{1,0:T(8,128)(2,1)S(1)}, u32[]{:S(2)}, u32[]{:S(2)}) collective-permute-start(bf16[24,2048]{1,0:T(8,128)(2,1)S(1)} %fusion), channel_id=1, source_target_pairs={{0,2},{2,0},{4,6},{6,4},{8,10},{10,8},{12,14},{14,12},{16,18},{18,... | collective-permute-start | bytes 294920 | tf_op jit(solution)/shard_map/ppermute | solution.py:310
  74.0 4.3 %collective-permute-start.5 = (bf16[8,2048]{1,0:T(8,128)(2,1)S(1)}, bf16[8,2048]{1,0:T(8,128)(2,1)S(1)}, u32[]{:S(2)}, u32[]{:S(2)}) collective-permute-start(bf16[8,2048]{1,0:T(8,128)(2,1)S(1)} %fusion.4), channel_id=1, source_target_pairs={{0,4},{2,6},{4,0},{6,2},{8,12},{10,14},{12,8},{14,10},{16,20},{18,... | collective-permute-start | bytes 98312 | tf_op jit(solution)/shard_map/ppermute | solution.py:310
  74.8 6.0 %collective-permute-start.10 = (bf16[24,2048]{1,0:T(8,128)(2,1)S(1)}, bf16[24,2048]{1,0:T(8,128)(2,1)S(1)}, u32[]{:S(2)}, u32[]{:S(2)}) collective-permute-start(bf16[24,2048]{1,0:T(8,128)(2,1)S(1)} %fusion.6), channel_id=1, source_target_pairs={{0,4},{2,6},{4,0},{6,2},{8,12},{10,14},{12,8},{14,10},{16,20},{18,... | collective-permute-start | bytes 294920 | tf_op jit(solution)/shard_map/ppermute | solution.py:310
  79.1 4.0 %collective-permute-start.6 = (bf16[8,2048]{1,0:T(8,128)(2,1)S(1)}, bf16[8,2048]{1,0:T(8,128)(2,1)S(1)}, u32[]{:S(2)}, u32[]{:S(2)}) collective-permute-start(bf16[8,2048]{1,0:T(8,128)(2,1)S(1)} %fusion.5), channel_id=1, source_target_pairs={{0,8},{2,10},{4,12},{6,14},{8,0},{10,2},{12,4},{14,6},{16,24},{18,... | collective-permute-start | bytes 98312 | tf_op jit(solution)/shard_map/ppermute | solution.py:310
  80.8 5.0 %collective-permute-start.11 = (bf16[24,2048]{1,0:T(8,128)(2,1)S(1)}, bf16[24,2048]{1,0:T(8,128)(2,1)S(1)}, u32[]{:S(2)}, u32[]{:S(2)}) collective-permute-start(bf16[24,2048]{1,0:T(8,128)(2,1)S(1)} %fusion.1), channel_id=1, source_target_pairs={{0,8},{2,10},{4,12},{6,14},{8,0},{10,2},{12,4},{14,6},{16,24},{18,... | collective-permute-start | bytes 294920 | tf_op jit(solution)/shard_map/ppermute | solution.py:310
  83.2 5.2 %collective-permute-start.7 = (bf16[8,2048]{1,0:T(8,128)(2,1)S(1)}, bf16[8,2048]{1,0:T(8,128)(2,1)S(1)}, u32[]{:S(2)}, u32[]{:S(2)}) collective-permute-start(bf16[8,2048]{1,0:T(8,128)(2,1)S(1)} %get-tuple-element.39), channel_id=1, source_target_pairs={{0,16},{2,18},{4,20},{6,22},{8,24},{10,26},{12,28},{14,30},{16,0},... | collective-permute-start | bytes 98312 | tf_op jit(solution)/shard_map/ppermute | solution.py:310
  85.8 6.6 %collective-permute-start.12 = (bf16[24,2048]{1,0:T(8,128)(2,1)S(1)}, bf16[24,2048]{1,0:T(8,128)(2,1)S(1)}, u32[]{:S(2)}, u32[]{:S(2)}) collective-permute-start(bf16[24,2048]{1,0:T(8,128)(2,1)S(1)} %fusion.2), channel_id=1, source_target_pairs={{0,16},{2,18},{4,20},{6,22},{8,24},{10,26},{12,28},{14,30},{16,0},... | collective-permute-start | bytes 294920 | tf_op jit(solution)/shard_map/ppermute | solution.py:310
  92.7 0.7 copy-start.5

commit v3 on v2

--- a/solution.py
+++ b/solution.py
@@ -62,6 +62,10 @@
     return xr * taps[0] + xi * taps[1], xi * taps[2] - xr * taps[1]
 
 
+def blocks(wide, width):
+    return [slice(at, at + width) for at in range(0, wide, width)]
+
+
 def rounded(value):
     return value.astype(BF16).astype(F32)
 
@@ -78,9 +82,9 @@
     return [(at, min(CHUNK, count - at)) for at in range(0, count, CHUNK)]
 
 
-def put(ref, at, value):
+def put(ref, at, value, lane=0):
     for h, lanes in halves(value.shape[1]):
-        ref[h, at : at + value.shape[0]] = value[:, lanes]
+        ref[h + lane // LANES, at : at + value.shape[0]] = value[:, lanes]
 
 
 def causal(ref, h, at, count, weights):
@@ -166,16 +170,42 @@
             qs = causal(xq, h, HALO + at, size, wq)
             ggi_out[span, lanes] = (g[span, lanes].astype(F32) * qs).astype(BF16)
     behind_out[...] = gated_out[rows - BLOCK :, :]
-    first = to_spectrum(half[...], gated_out[:BLOCK, :])
-    inner_out[...] = from_spectrum(low[...], *times(first, tap_spec))
+    for lanes in blocks(width, taps.shape[0]):
+        first = to_spectrum(half[...], gated_out[:BLOCK, lanes])
+        inner_out[:, lanes] = from_spectrum(low[...], *times(first, tap_spec))
+
+
+def middle_kernel(
+    q, g, gated, w, spec, whole, high,
+    gq_out, next_out, sums_out, more_out,
+    xq, yq,
+):
+    rows, width = gated.shape
+    rest = rows - BLOCK
+    for lanes in blocks(width, spec.shape[2]):
+        wide = lanes.stop - lanes.start
+        window = jnp.concatenate(
+            [gated[:, lanes], jnp.zeros((WINDOW - rows, wide), BF16)], axis=0
+        )
+        prod = times(to_spectrum(whole[...], window), spec)
+        sig = from_spectrum(high[: rest + HALO, :], *prod)
+        put(yq, 0, rounded(g[:, lanes].astype(F32) * sig[:rest]), lanes.start)
+        more_out[:, lanes] = sig[rest:]
+    put(xq, 0, q[BLOCK - 2 * HALO :, :].astype(F32))
+    for h, lanes in halves(width):
+        next_out[:HALO, lanes] = yq[h, :HALO]
+        next_out[HALO:, lanes] = yq[h, rest - HALO : rest]
+        gq_out[:, lanes] = anticausal(yq, h, 0, rest, taps_of(w, 0, lanes)).astype(BF16)
+        sums_out[:, lanes] = lag_sums(yq, 0, xq, 2 * HALO, h, rest, w.shape[1])
 
 
 def third_kernel(
-    q, k, v, g, tails, ahead, gated, ggi, ks, vs, w, spec, half, whole, low, high,
-    gk_out, gv_out, gq_out, next_out, sums_out, medium_out,
-    xq, xk, xv, yq, yk, yv, acc,
+    me, k, v, tails, ends, ahead, gated, ggi, ks, vs, more, taps, w, spec, half, whole, low,
+    gk_out, gv_out, next_out, sums_out, send_out, own_out, *rest_refs,
 ):
+    *more_out, xe, xk, xv, yk, yv, acc, mscr = rest_refs
     rows, width = k.shape
+    groups = spec.shape[2]
     rest = rows - BLOCK
     step = pl.program_id(0)
     count = w.shape[1]
@@ -184,91 +214,122 @@
     def _():
         acc[...] = jnp.zeros_like(acc)
 
+    head = ahead[: 4 * HALO, :].astype(F32)
     tail = tails[...].astype(F32)
-    head = ahead[: 4 * HALO, :].astype(F32)
-    for at, (ref, x) in enumerate(((xq, q), (xk, k), (xv, v))):
-        put(ref, 0, tail[at * HALO : (at + 1) * HALO])
-        put(ref, HALO, x[...].astype(F32))
-        put(ref, HALO + rows, head[at * HALO : (at + 1) * HALO])
-    gated_new, ggi_new, ks_new, vs_new = [], [], [], []
+    end = ends[...].astype(F32)
+    for at in range(3):
+        put(xe.at[at], HALO, end[at * HALO : (at + 1) * HALO])
+        put(xe.at[at], 2 * HALO, head[at * HALO : (at + 1) * HALO])
+        put(xe.at[at], 0, jnp.zeros((HALO, width), F32))
+    news = [[], [], []]
     for h, lanes in halves(width):
-        kn, vn, qn = (
-            causal(ref, h, HALO + rows, HALO, taps_of(w, i, lanes))
-            for ref, i in ((xk, 1), (xv, 2), (xq, 0))
-        )
-        ks_new.append(kn)
-        vs_new.append(vn)
-        gated_new.append(kn * vn)
-        ggi_new.append(head[3 * HALO :, lanes] * qn)
-    ks_new, vs_new, gated_new, ggi_new = (
-        jnp.concatenate(x, axis=1) for x in (ks_new, vs_new, gated_new, ggi_new)
-    )
-    blank = jnp.zeros((WINDOW - rows - HALO, width), F32)
-    rest_new = jnp.concatenate([gated_new, blank], axis=0).astype(BF16)
-    window = jnp.concatenate([gated[...], rest_new], axis=0)
-    sig = from_spectrum(high[: rest + HALO, :], *times(to_spectrum(whole[...], window), spec))
-    put(yq, 0, rounded(g[BLOCK:, :].astype(F32) * sig[:rest]))
-    put(yq, rest, rounded(head[3 * HALO :] * sig[rest:]))
+        for at in range(3):
+            news[at].append(causal(xe.at[at], h, 2 * HALO, HALO, taps_of(w, at, lanes)))
+    qs_new, ks_new, vs_new = (jnp.concatenate(x, axis=1) for x in news)
+    gated_new = rounded(ks_new * vs_new)
+    ggi_new = head[3 * HALO :] * qs_new
+    put(xe.at[0], HALO, gated_new)
     for h, lanes in halves(width):
-        next_out[:, lanes] = yq[h, :HALO]
-
+        total = more[:, lanes]
+        for j in range(HALO):
+            at = lanes.start % groups
+            total = total + taps[j : j + 1, at : at + LANES] * xe[0, h, HALO - j : 2 * HALO - j]
+        next_out[:, lanes] = rounded(head[3 * HALO :, lanes] * total)
+    put(xk, 0, tail[HALO : 2 * HALO])
+    put(xk, HALO, k[...].astype(F32))
+    put(xv, 0, tail[2 * HALO :])
+    put(xv, HALO, v[...].astype(F32))
     fill = 3 * BLOCK - rows - HALO - BLOCK
-    later = jnp.concatenate(
-        [ggi_new, ahead[4 * HALO :, :].astype(F32), jnp.zeros((fill, width), F32)], axis=0
-    ).astype(BF16)
-    ggi_ext = jnp.concatenate([ggi[...], later], axis=0)
-    own = jnp.concatenate([gated[...], jnp.zeros((WINDOW - rows, width), BF16)], axis=0)
-    for at in range(2):
-        win = to_spectrum(whole[...], ggi_ext[at * BLOCK : at * BLOCK + WINDOW])
-        gs = to_spectrum(half[...], own[at * BLOCK : (at + 1) * BLOCK])
-        acc[0] += gs[:BLOCK] * win[:BLOCK]
-        acc[1] += gs[BLOCK:] * win[BLOCK:]
-        acc[2] += gs[:BLOCK] * win[BLOCK:] - gs[BLOCK:] * win[:BLOCK]
-        prod = times_conj(win, spec)
-        if at == 0:
-            gg = from_spectrum(low[...], *prod)
-            put(yk, 0, rounded(gg * vs[:BLOCK, :]))
-            put(yv, 0, rounded(gg * ks[:BLOCK, :]))
-        else:
-            gg = from_spectrum(low[: rest + HALO, :], *prod)
-            put(yk, BLOCK, rounded(gg[:rest] * vs[BLOCK:, :]))
-            put(yv, BLOCK, rounded(gg[:rest] * ks[BLOCK:, :]))
-            put(yk, rows, rounded(gg[rest:] * vs_new))
-            put(yv, rows, rounded(gg[rest:] * ks_new))
+    for lanes in blocks(width, groups):
+        later = jnp.concatenate(
+            [ggi_new[:, lanes], ahead[4 * HALO :, lanes].astype(F32), jnp.zeros((fill, groups), F32)],
+            axis=0,
+        ).astype(BF16)
+        ggi_ext = jnp.concatenate([ggi[:, lanes], later], axis=0)
+        own = jnp.concatenate([gated[:, lanes], jnp.zeros((WINDOW - rows, groups), BF16)], axis=0)
+        for at in range(2):
+            win = to_spectrum(whole[...], ggi_ext[at * BLOCK : at * BLOCK + WINDOW])
+            gs = to_spectrum(half[...], own[at * BLOCK : (at + 1) * BLOCK])
+            acc[0] += gs[:BLOCK] * win[:BLOCK]
+            acc[1] += gs[BLOCK:] * win[BLOCK:]
+            acc[2] += gs[:BLOCK] * win[BLOCK:] - gs[BLOCK:] * win[:BLOCK]
+            prod = times_conj(win, spec)
+            if at == 0:
+                gg = from_spectrum(low[...], *prod)
+                gk = (gg * vs[:BLOCK, lanes]).astype(BF16)
+                gv = (gg * ks[:BLOCK, lanes]).astype(BF16)
+                span = slice(0, BLOCK)
+            else:
+                gg = from_spectrum(low[: rest + HALO, :], *prod)
+                zero = jnp.zeros((HALO, groups), F32)
+                gk = jnp.concatenate(
+                    [gg[:rest] * vs[BLOCK:, lanes], gg[rest:] * vs_new[:, lanes], zero], axis=0
+                ).astype(BF16)
+                gv = jnp.concatenate(
+                    [gg[:rest] * ks[BLOCK:, lanes], gg[rest:] * ks_new[:, lanes], zero], axis=0
+                ).astype(BF16)
+                span = slice(BLOCK, rows + 2 * HALO)
+            gk_out[span, lanes] = gk
+            gv_out[span, lanes] = gv
+            put(yk, span.start, gk.astype(F32), lanes.start)
+            put(yv, span.start, gv.astype(F32), lanes.start)
+        for h in range(lanes.start // LANES, lanes.stop // LANES):
+            here = slice(h * LANES, (h + 1) * LANES)
+            sums_out[:HALO, here] = lag_sums(yk, 0, xk, HALO, h, rows, count)
+            sums_out[HALO:, here] = lag_sums(yv, 0, xv, HALO, h, rows, count)
+    send_out[...] = sums_out[...].astype(BF16)
+
+    @pl.when(step == pl.num_programs(0) - 1)
+    def _():
+        first = lax.broadcasted_iota(jnp.int32, (BLOCK, groups), 0) == 0
+        real = acc[0] + jnp.where(first, 0.0, acc[1])
+        imag = jnp.where(first, acc[1], acc[2])
+        mscr[...] = from_spectrum(low[...], real, imag).T
+        mine = own_out.shape[0]
+        share = groups // mine
+        for at in range(share):
+            part = mscr[pl.ds(pl.multiple_of(lax.rem(me[0] + at, share) * mine, mine), mine)]
+            if at == 0:
+                own_out[...] = part
+            else:
+                more_out[at - 1][...] = part.astype(BF16)
+
+
+def fourth_kernel(gk, gv, near, far, w, gq_in, gk_out, gv_out, gq_out, yq, yk, yv):
+    rows, width = gk_out.shape
+    put(yk, 0, gk[...].astype(F32))
+    put(yv, 0, gv[...].astype(F32))
+    put(yq, 0, near[...])
+    put(yq, HALO, far[...])
+    put(yq, 2 * HALO, jnp.zeros((HALO, width), F32))
+    old = gq_in[...].astype(F32)[:HALO]
     for h, lanes in halves(width):
         for i, ref, out in ((1, yk, gk_out), (2, yv, gv_out)):
             weights = taps_of(w, i, lanes)
             for at, size in pieces(rows):
                 out[at : at + size, lanes] = anticausal(ref, h, at, size, weights).astype(BF16)
-        gq_out[:, lanes] = anticausal(yq, h, 0, rest, taps_of(w, 0, lanes)).astype(BF16)
-        sums_out[:HALO, lanes] = lag_sums(yk, 0, xk, HALO, h, rows, count)
-        sums_out[HALO : 2 * HALO, lanes] = lag_sums(yv, 0, xv, HALO, h, rows, count)
-        sums_out[2 * HALO :, lanes] = lag_sums(yq, 0, xq, HALO + BLOCK, h, rest, count)
-
-    @pl.when(step == pl.num_programs(0) - 1)
-    def _():
-        first = lax.broadcasted_iota(jnp.int32, (BLOCK, width), 0) == 0
-        real = acc[0] + jnp.where(first, 0.0, acc[1])
-        imag = jnp.where(first, acc[1], acc[2])
-        medium_out[...] = from_spectrum(low[...], real, imag).T
-
-
-def fourth_kernel(
-    q, g, tails, inner, behind, following, sums, w, spec, half, high, gq_in,
-    gq_out, sums_out,
+        fixed = anticausal(yq, h, 0, HALO, taps_of(w, 0, lanes))
+        gq_out[:, lanes] = jnp.concatenate([old[:, lanes], fixed], axis=0).astype(BF16)
+
+
+def fifth_kernel(
+    q, tails, following, sums, w, g, inner, behind, spec, half, high, gq_in,
+    gq_out, sums_out, send_out,
     xq, yq,
 ):
     width = q.shape[1]
     put(xq, 0, tails[...].astype(F32)[:HALO])
     put(xq, HALO, q[...].astype(F32))
-    edge = from_spectrum(high[...], *times(to_spectrum(half[...], behind[...]), spec))
-    put(yq, 0, rounded(g[...].astype(F32) * (inner[...] + edge)))
     put(yq, BLOCK, following[...])
+    for lanes in blocks(width, spec.shape[2]):
+        edge = from_spectrum(high[...], *times(to_spectrum(half[...], behind[:, lanes]), spec))
+        put(yq, 0, rounded(g[:, lanes].astype(F32) * (inner[:, lanes] + edge)), lanes.start)
     for h, lanes in halves(width):
         weights = taps_of(w, 0, lanes)
         for at, size in pieces(BLOCK):
             gq_out[at : at + size, lanes] = anticausal(yq, h, at, size, weights).astype(BF16)
         sums_out[:, lanes] = sums[:, lanes] + lag_sums(yq, 0, xq, HALO, h, BLOCK, w.shape[1])
+    send_out[...] = sums_out[...].astype(BF16)
 
 
 def shift(value, axis, steps):
@@ -288,35 +349,36 @@
     return result
 
 
-def scatter_sum(value, axis):
+def exchange_sum(own, sends, axis):
     count = lax.axis_size(axis)
-    rows = value.shape[0] // count
-    me = lax.axis_index(axis)
-    total = lax.dynamic_slice(value, (me * rows, 0), (rows, value.shape[1]))
-    for step in range(1, count):
-        part = lax.dynamic_slice(value, ((me + step) % count * rows, 0), (rows, value.shape[1]))
+    total = own
+    for step, part in enumerate(sends, 1):
         total = total + lax.ppermute(
-            part.astype(BF16), axis, [(s, (s + step) % count) for s in range(count)]
+            part, axis, [(s, (s + step) % count) for s in range(count)]
         ).astype(F32)
     return total
 
 
-def sum_over(value, axis):
+def sum_over(value, sent, axis, reverse=False):
     count = lax.axis_size(axis)
     if count & (count - 1):
         return lax.psum(value, axis)
-    distance = 1
-    while distance < count:
-        other = lax.ppermute(value.astype(BF16), axis, [(s, s ^ distance) for s in range(count)])
+    steps = range(count.bit_length() - 1)
+    for bit in reversed(steps) if reverse else steps:
+        other = lax.ppermute(sent, axis, [(s, s ^ (1 << bit)) for s in range(count)])
         value = value + other.astype(F32)
-        distance *= 2
+        sent = value.astype(BF16)
     return value
+
+
+def in_hbm(value):
+    return pltpu.with_memory_space_constraint(value, pltpu.HBM)
 
 
 def shards(query, key, value, grad_out, short_filter, medium_filter):
     rows, channels = query.shape
     groups = medium_filter.shape[0] * lax.axis_size("fsdp")
-    width, tiles = groups, channels // groups
+    width = groups
     rest = rows - BLOCK
     taps_short = short_filter.shape[1]
     whole, half, low, high = (jnp.asarray(m) for m in transforms())
@@ -353,77 +415,122 @@
         scratch_shapes=[scratch(BLOCK + 2 * HALO, wide)],
         name="first",
     )(query, grad_out, query, key, value, key, value, short_filter)
-    tails = shift(tails, "seq", 1)
-    ahead = shift(ahead, "seq", -1)
+    ends = tails
+    tails = in_hbm(shift(tails, "seq", 1))
+    ahead = in_hbm(shift(ahead, "seq", -1))
     taps = gather_rows(medium_filter.astype(BF16), "fsdp")
 
     gated, ggi, ks, vs, inner, behind, spec = pl.pallas_call(
         second_kernel,
-        grid=(tiles,),
-        in_specs=[col(rows)] * 4
-        + [col(3 * HALO), filters(), fixed(taps.shape), fixed(half.shape), fixed(low.shape)],
-        out_specs=[col(rows)] * 4 + [col(BLOCK), col(BLOCK), fixed((3, BLOCK, width))],
+        grid=(channels // wide,),
+        in_specs=[col(rows, 0, wide)] * 4
+        + [col(3 * HALO, 0, wide), filters(wide), fixed(taps.shape), fixed(half.shape), fixed(low.shape)],
+        out_specs=[col(rows, 0, wide)] * 4 + [col(BLOCK, 0, wide)] * 2 + [ fixed((3, BLOCK, width))],
         out_shape=[
             out(rows, BF16), out(rows, BF16), out(rows, F32), out(rows, F32),
             out(BLOCK, F32), out(BLOCK, BF16), jax.ShapeDtypeStruct((3, BLOCK, width), F32),
         ],
-        scratch_shapes=[scratch(rows + HALO)] * 3 + [pltpu.VMEM((3, BLOCK, width), F32)],
+        scratch_shapes=[scratch(rows + HALO, wide)] * 3 + [pltpu.VMEM((3, BLOCK, width), F32)],
         cost_estimate=cost(4e9, 20e6),
         name="second",
     )(query, key, value, grad_out, tails, short_filter, taps, half, low)
-    behind = shift(behind, "seq", 1)
-
-    grad_key, grad_value, grad_query, following, sums, medium = pl.pallas_call(
+    behind = in_hbm(shift(behind, "seq", 1))
+
+    share = lax.axis_size("fsdp")
+    me = lax.axis_index("fsdp").astype(jnp.int32).reshape(1)
+    many = channels // wide
+
+    def big(count, at=0):
+        return pl.BlockSpec((count, wide), lambda i, *_: (at, i))
+
+    def still(shape):
+        return pl.BlockSpec(shape, lambda i, *_: (0,) * len(shape))
+
+    big_filters = pl.BlockSpec((3, taps_short, wide), lambda i, *_: (0, 0, i))
+    tap_rows = taps[:, :HALO].astype(F32).T
+    corner = BLOCK // rest
+    edge_block = rows // (2 * HALO) - 1
+    grad_query, nexts, sums_q, more = pl.pallas_call(
+        middle_kernel,
+        grid=(many,),
+        in_specs=[big(rows), big(rest, corner), big(rows), big_filters]
+        + [still((3, BLOCK, width)), still(whole.shape), still(high.shape)],
+        out_specs=[big(rest, corner), big(2 * HALO), big(HALO), big(HALO)],
+        out_shape=[out(rows, BF16), out(2 * HALO, F32), out(HALO, F32), out(HALO, F32)],
+        scratch_shapes=[scratch(rest + 2 * HALO, wide)] * 2,
+        cost_estimate=cost(2e9, 8e6),
+        name="middle",
+    )(query, grad_out, gated, short_filter, spec, whole, high)
+
+    mine = (width // share, BLOCK)
+    gk, gv, far, sums_kv, sent_kv, own, *sends = pl.pallas_call(
         third_kernel,
-        grid=(tiles,),
-        in_specs=[col(rows)] * 4
-        + [col(3 * HALO), col(BLOCK + 4 * HALO)]
-        + [col(rows)] * 4
-        + [filters(), fixed((3, BLOCK, width))]
-        + [fixed(m.shape) for m in (half, whole, low, high)],
-        out_specs=[
-            col(rows), col(rows), col(rest, BLOCK // rest), col(HALO), col(3 * HALO),
-            fixed((width, BLOCK)),
-        ],
-        out_shape=[
-            out(rows, BF16), out(rows, BF16), out(rows, BF16), out(HALO, F32),
-            out(3 * HALO, F32), jax.ShapeDtypeStruct((width, BLOCK), F32),
-        ],
-        scratch_shapes=[scratch(rows + 2 * HALO)] * 3
-        + [scratch(rest + 2 * HALO)]
-        + [scratch(rows + 2 * HALO)] * 2
-        + [pltpu.VMEM((3, BLOCK, width), F32)],
-        cost_estimate=cost(8e9, 30e6),
+        grid_spec=pltpu.PrefetchScalarGridSpec(
+            num_scalar_prefetch=1,
+            grid=(many,),
+            in_specs=[big(rows)] * 2
+            + [big(3 * HALO)] * 2
+            + [big(BLOCK + 4 * HALO)]
+            + [big(rows)] * 4
+            + [big(HALO), still(tap_rows.shape), big_filters, still((3, BLOCK, width))]
+            + [still(m.shape) for m in (half, whole, low)],
+            out_specs=[big(rows + 2 * HALO)] * 2
+            + [big(HALO)]
+            + [big(2 * HALO)] * 2
+            + [still(mine)] * share,
+            scratch_shapes=[pltpu.VMEM((3, wide // LANES, 3 * HALO, LANES), F32)]
+            + [scratch(rows + 2 * HALO, wide)] * 4
+            + [pltpu.VMEM((3, BLOCK, width), F32), pltpu.VMEM((width, BLOCK), F32)],
+        ),
+        out_shape=[out(rows + 2 * HALO, BF16)] * 2
+        + [out(HALO, F32), out(2 * HALO, F32), out(2 * HALO, BF16)]
+        + [jax.ShapeDtypeStruct(mine, F32)]
+        + [jax.ShapeDtypeStruct(mine, BF16)] * (share - 1),
+        cost_estimate=cost(8e9, 20e6),
         name="third",
-    )(query, key, value, grad_out, tails, ahead, gated, ggi, ks, vs, short_filter, spec,
-      half, whole, low, high)
-
-    grad_query, sums_q = pl.pallas_call(
+    )(me, key, value, tails, ends, ahead, gated, ggi, ks, vs, more, tap_rows,
+      short_filter, spec, half, whole, low)
+    medium = exchange_sum(own, sends, "fsdp")
+
+    grad_key, grad_value, grad_query = pl.pallas_call(
         fourth_kernel,
-        grid=(tiles,),
-        in_specs=[col(BLOCK)] * 2
-        + [col(3 * HALO), col(BLOCK), col(BLOCK), col(HALO), col(HALO, 2), filters()]
-        + [fixed((3, BLOCK, width)), fixed(half.shape), fixed(high.shape)]
+        grid=(many,),
+        in_specs=[big(rows + 2 * HALO)] * 2
+        + [big(HALO, 1), big(HALO), big_filters, big(2 * HALO, edge_block)],
+        out_specs=[big(rows), big(rows), big(2 * HALO, edge_block)],
+        out_shape=[out(rows, BF16)] * 3,
+        scratch_shapes=[scratch(3 * HALO, wide)] + [scratch(rows + 2 * HALO, wide)] * 2,
+        input_output_aliases={5: 2},
+        cost_estimate=cost(4e9, 10e6),
+        name="fourth",
+    )(gk, gv, nexts, far, short_filter, grad_query)
+
+    grad_query, sums_q, sent_q = pl.pallas_call(
+        fifth_kernel,
+        grid=(many,),
+        in_specs=[big(BLOCK), big(3 * HALO), big(HALO), big(HALO), big_filters]
+        + [big(BLOCK)] * 3
+        + [still((3, BLOCK, width)), still(half.shape), still(high.shape)]
         + [pl.BlockSpec(memory_space=pl.ANY)],
-        out_specs=[col(BLOCK), col(HALO)],
-        out_shape=[out(rows, BF16), out(HALO, F32)],
-        scratch_shapes=[scratch(BLOCK + HALO)] * 2,
+        out_specs=[big(BLOCK), big(HALO), big(HALO)],
+        out_shape=[out(rows, BF16), out(HALO, F32), out(HALO, BF16)],
+        scratch_shapes=[scratch(BLOCK + HALO, wide)] * 2,
         input_output_aliases={11: 0},
         cost_estimate=cost(2e9, 8e6),
-        name="fourth",
-    )(query, grad_out, tails, inner, behind, following, sums, short_filter, spec, half, high,
+        name="fifth",
+    )(query, tails, nexts, sums_q, short_filter, grad_out, inner, behind, spec, half, high,
       grad_query)
 
-    medium = scatter_sum(medium, "fsdp")
     per = channels // BLOCK
     count = medium.shape[0] // per
     packed = jnp.concatenate([medium[i * count : (i + 1) * count] for i in range(per)], axis=1)
-    early = jnp.concatenate([sums[: 2 * HALO], packed], axis=0)
-    early = sum_over(early, "seq")
-    sums_q = sum_over(sums_q, "seq")
+    early = jnp.concatenate([sums_kv, packed], axis=0)
+    sent = jnp.concatenate([sent_kv, packed.astype(BF16)], axis=0)
+    early = sum_over(early, sent, "seq", reverse=True)
+    late = sum_over(sums_q, sent_q, "seq")
     packed = early[2 * HALO :]
     grad_medium = jnp.concatenate([packed[:, i * BLOCK : (i + 1) * BLOCK] for i in range(per)], axis=0)
-    grad_short = jnp.stack([sums_q[:taps_short], early[:taps_short], early[HALO : HALO + taps_short]])
+    grad_short = jnp.stack([late[:taps_short], early[:taps_short], early[HALO : HALO + taps_short]])
     return grad_query, grad_key, grad_value, grad_short, grad_medium
 
 

time: 94.3 us -> 80.1 us (0.85)
  waiting for transfers between devices: 28.1 us -> 9.26 us
  starting transfers between devices: 20.7 us -> 24.8 us
    ppermute x3, waiting for transfers between devices: 16.1 us -> 0.26 us  [shift(): lax.ppermute(value, axis, [(s, s + steps) for s in range(initial, last)])]
    ppermute x9, starting transfers between devices: 9.49 us -> 14.2 us  [the longest x8 14.1 us: sum_over(): other = lax.ppermute(sent, axis, [(s, s ^ 1 << bit) for s in range(count)])]
    ppermute x9, waiting for transfers between devices: 12 us -> 9 us  [the longest x8 9 us: sum_over(): other = lax.ppermute(sent, axis, [(s, s ^ 1 << bit) for s in range(count)])]
    unnamed x48 -> x47, local copies, waits for them, and re-layouts: 2.41 us -> 3.36 us
    convert_element_type x8 -> x7, other arithmetic: 2.73 us -> 1.85 us  [the longest x6 1.84 us: sum_over(): sent = value.astype(BF16)]
    pallas_call x3 -> x5, Pallas kernels: 32.9 us -> 33.1 us  [the longest x1 9.42 us: shards(): pl.pallas_call(third_kernel, grid_spec=pltpu.PrefetchScalarGridSpec(num_s...]
  transfers between devices with their start and end apart: 13 -> 13, of which waited for: 7 -> 6; matrix products, arithmetic and copies ran while one was open for 4% -> 4% of each run, Pallas kernels for 35% -> 46%
where the time goes in v3:
time: 80.1 us; the launch traced here: 79.4 us
  Pallas kernels  36.9 us (46%)
  starting transfers between devices  24.8 us (31%)
  waiting for transfers between devices  9.26 us (12%)
  local copies, waits for them, and re-layouts  4.15 us (5%)
  other arithmetic  3.23 us (4%)
  between operations  1.09 us (1%)
    ppermute x8, starting transfers between devices, sum_over(): other = lax.ppermute(sent, axis, [(s, s ^ 1 << bit) for s in range(count)])  14.1 us
    ppermute x3, starting transfers between devices, shift(): lax.ppermute(value, axis, [(s, s + steps) for s in range(initial, last)])  10 us
    pallas_call x1, Pallas kernels, shards(): pl.pallas_call(third_kernel, grid_spec=pltpu.PrefetchScalarGridSpec(num_s...  9.42 us
    ppermute x8, waiting for transfers between devices, sum_over(): other = lax.ppermute(sent, axis, [(s, s ^ 1 << bit) for s in range(count)])  9 us
    pallas_call x1, Pallas kernels, shards(): pl.pallas_call(second_kernel, grid=(channels // wide,), in_specs=[col(row...  7.64 us
    pallas_call x1, Pallas kernels, shards(): pl.pallas_call(middle_kernel, grid=(many,), in_specs=[big(rows), big(rest...  5.88 us
    pallas_call x1, Pallas kernels, shards(): pl.pallas_call(fifth_kernel, grid=(many,), in_specs=[big(BLOCK), big(3 *...  5.74 us
    pallas_call x1, Pallas kernels, shards(): pl.pallas_call(fourth_kernel, grid=(many,), in_specs=[big(rows + 2 * HALO...  4.38 us
  transfers between devices with their start and end apart: 13, of which 6 were waited for; matrix products, arithmetic and copies ran while one was open for 4% of the time, Pallas kernels for 46%

profile of v3, /device:TPU:0, one launch (start us, length us, event | category | flops | bytes accessed | tf_op | source)
XLA Modules:
  0.0 79.4 jit_solution(9594044572527392738)
XLA Ops:
  0.6 0.9 %copy.17 = bf16[128,128]{0,1:T(8,128)(2,1)S(1)} copy(f32[128,128]{1,0:T(8,128)} %param.15) | data formatting | bytes 98304 | tf_op args[5]
  1.6 0.6 collective-permute-start.1
  2.1 3.8 %first.1 = (bf16[24,2048]{1,0:T(8,128)(2,1)}, bf16[160,2048]{1,0:T(8,128)(2,1)}) custom-call(bf16[192,2048]{1,0:T(8,128)(2,1)} %q.7, bf16[192,2048]{1,0:T(8,128)(2,1)} %g.7, bf16[192,2048]{1,0:T(8,128)(2,1)} %q.7, bf16[192,2048]{1,0:T(8,128)(2,1)} %k.3, bf16[192,2048]{1,0:T(8,128)(2,1)} %v.3, bf16[192,2048]{1,0:T(8,128)(2,1)} %k.3, bf16[192,2048]{1,0:T(8,128)(2,1)} %v.3, ...), custom_call_target="tpu_custom_call" | custom-call | tf_op jit(solution)/shard_map/first/pallas_call | solution.py:406
  6.0 4.4 %collective-permute-start = (bf16[24,2048]{1,0:T(8,128)(2,1)}, bf16[24,2048]{1,0:T(8,128)(2,1)S(1)}, u32[]{:S(2)}, u32[]{:S(2)}) collective-permute-start(bf16[24,2048]{1,0:T(8,128)(2,1)} %get-tuple-element.31.ends), channel_id=1, source_target_pairs={{0,2},{2,4},{4,6},{6,8},{8,10},{10,12},{12,14},{14,16},{16,18},{18... | collective-permute-start | bytes 294920 | tf_op jit(solution)/shard_map/ppermute | solution.py:338
  10.4 1.3 %collective-permute-start.3 = (bf16[160,2048]{1,0:T(8,128)(2,1)}, bf16[160,2048]{1,0:T(8,128)(2,1)S(1)}, u32[]{:S(2)}, u32[]{:S(2)}) collective-permute-start(bf16[160,2048]{1,0:T(8,128)(2,1)} %get-tuple-element.38), channel_id=1, source_target_pairs={{2,0},{4,2},{6,4},{8,6},{10,8},{12,10},{14,12},{16,14},{18,16},{20... | collective-permute-start | bytes 1966088 | tf_op jit(solution)/shard_map/ppermute | solution.py:338
  11.8 0.6 convert_bitcast_fusion.taps
  12.4 0.7 copy.18.taps
  13.4 0.7 copy-done.7
  14.0 7.6 %second.1 = (bf16[192,2048]{1,0:T(8,128)(2,1)}, bf16[192,2048]{1,0:T(8,128)(2,1)}, f32[192,2048]{1,0:T(8,128)}, f32[192,2048]{1,0:T(8,128)}, f32[128,2048]{1,0:T...) custom-call(bf16[192,2048]{1,0:T(8,128)(2,1)} %q.7, bf16[192,2048]{1,0:T(8,128)(2,1)} %k.3, ...), custom_call_target="tpu_custom_call" | custom-call | flops 4000000000 | bytes 20000000 | tf_op jit(solution)/shard_map/second/pallas_call | solution.py:423
  21.7 4.3 %collective-permute-start.2 = (bf16[128,2048]{1,0:T(8,128)(2,1)}, bf16[128,2048]{1,0:T(8,128)(2,1)S(1)}, u32[]{:S(2)}, u32[]{:S(2)}) collective-permute-start(bf16[128,2048]{1,0:T(8,128)(2,1)} %get-tuple-element.37), channel_id=1, source_target_pairs={{0,2},{2,4},{4,6},{6,8},{8,10},{10,12},{12,14},{14,16},{16,18},{18... | collective-permute-start | bytes 1572872 | tf_op jit(solution)/shard_map/ppermute | solution.py:338
  26.0 5.9 %middle.1 = (bf16[192,2048]{1,0:T(8,128)(2,1)}, f32[16,2048]{1,0:T(8,128)}, f32[8,2048]{1,0:T(8,128)}, f32[8,2048]{1,0:T(8,128)}) custom-call(bf16[192,2048]{1,0:T(8,128)(2,1)} %q.7, bf16[192,2048]{1,0:T(8,128)(2,1)} %g.7, bf16[192,2048]{1,0:T(8,128)(2,1)} %get-tuple-element.32.gated, f32[3,7,2048]{2,1,0:T(8,128)} %w.11, ...), custom_call_target="tpu_custom_call" | custom-call | flops 2000000000 | bytes 8000000 | tf_op jit(solution)/shard_map/middle/pallas_call | solution.py:453
  31.9 0.8 %copy-done.5 = bf16[160,2048]{1,0:T(8,128)(2,1)} copy-done((bf16[160,2048]{1,0:T(8,128)(2,1)}, bf16[160,2048]{1,0:T(8,128)(2,1)S(1)}, u32[]{:S(2)}) %copy-start.5) | copy-done | bytes 655384
  32.7 9.4 %third.1 = (bf16[208,2048]{1,0:T(8,128)(2,1)}, bf16[208,2048]{1,0:T(8,128)(2,1)}, f32[8,2048]{1,0:T(8,128)}, f32[16,2048]{1,0:T(8,128)}, bf16[16,2048]{1,0:T(8,1...) custom-call(s32[1]{0:T(128)} %bitcast.me, bf16[192,2048]{1,0:T(8,128)(2,1)} %k.3, bf16[192,2048]{1,0:T(8,128)(2,1)} %v.3, ...), custom_call_target="tpu_custom_call" | custom-call | flops 8000000000 | bytes 20000000 | tf_op jit(solution)/shard_map/third/pallas_call | solution.py:466
  42.2 4.4 %fourth.1 = (bf16[192,2048]{1,0:T(8,128)(2,1)}, bf16[192,2048]{1,0:T(8,128)(2,1)}, bf16[192,2048]{1,0:T(8,128)(2,1)}) custom-call(bf16[208,2048]{1,0:T(8,128)(2,1)} %get-tuple-element.43.gk, bf16[208,2048]{1,0:T(8,128)(2,1)} %get-tuple-element.44.gv, f32[16,2048]{1,0:T(8,128)} %get-tuple-element.34.near.following, ...), custom_call_target="tpu_custom_call", output_to_operand_aliasing={{2}: (5, {})} | custom-call | flops 4000000000 | bytes 10000000 | tf_op jit(solution)/shard_map/fourth/pallas_call | solution.py:495
  46.6 0.8 %copy-done.6 = bf16[128,2048]{1,0:T(8,128)(2,1)} copy-done((bf16[128,2048]{1,0:T(8,128)(2,1)}, bf16[128,2048]{1,0:T(8,128)(2,1)S(1)}, u32[]{:S(2)}) %copy-start.6) | copy-done | bytes 524312
  47.4 5.7 %fifth.1 = (bf16[192,2048]{1,0:T(8,128)(2,1)}, f32[8,2048]{1,0:T(8,128)}, bf16[8,2048]{1,0:T(8,128)(2,1)}) custom-call(bf16[192,2048]{1,0:T(8,128)(2,1)} %q.7, bf16[24,2048]{1,0:T(8,128)(2,1)} %copy-done.7, f32[16,2048]{1,0:T(8,128)} %get-tuple-element.34.near.following, f32[8,2048]{1,0:T(8,128)} %get-tuple-element.35.sums, ...), custom_call_target="tpu_custom_call", output_to_operand_aliasing={{0}: (11, {})} | custom-call | flops 2000000000 | bytes 8000000 | tf_op jit(solution)/shard_map/fifth/pallas_call | solution.py:508
  53.2 2.4 %collective-permute-start.4 = (bf16[8,2048]{1,0:T(8,128)(2,1)}, bf16[8,2048]{1,0:T(8,128)(2,1)S(1)}, u32[]{:S(2)}, u32[]{:S(2)}) collective-permute-start(bf16[8,2048]{1,0:T(8,128)(2,1)} %get-tuple-element.52), channel_id=1, source_target_pairs={{0,2},{2,0},{4,6},{6,4},{8,10},{10,8},{12,14},{14,12},{16,18},{18,... | collective-permute-start | bytes 98312 | tf_op jit(solution)/shard_map/ppermute | solution.py:368
  55.8 2.7 %collective-permute-start.9 = (bf16[24,2048]{1,0:T(8,128)(2,1)S(1)}, bf16[24,2048]{1,0:T(8,128)(2,1)S(1)}, u32[]{:S(2)}, u32[]{:S(2)}) collective-permute-start(bf16[24,2048]{1,0:T(8,128)(2,1)S(1)} %pad_maximum_fusion.1), channel_id=1, source_target_pairs={{0,16},{2,18},{4,20},{6,22},{8,24},{10,26},{12,28},{14,30},{16,0},... | collective-permute-start | bytes 294920 | tf_op jit(solution)/shard_map/ppermute | solution.py:368
  58.5 0.9 %fusion.3 = bf16[8,2048]{1,0:T(8,128)(2,1)S(1)} fusion(f32[8,2048]{1,0:T(8,128)} %get-tuple-element.51, bf16[8,2048]{1,0:T(8,128)(2,1)S(1)} %collective-permute-done.4), kind=kLoop, calls=%fused_computation.48 | loop fusion | flops 49152 | bytes 131072 | tf_op jit(solution)/shard_map/convert_element_type | solution.py:370
  59.4 2.5 %collective-permute-start.5 = (bf16[8,2048]{1,0:T(8,128)(2,1)S(1)}, bf16[8,2048]{1,0:T(8,128)(2,1)S(1)}, u32[]{:S(2)}, u32[]{:S(2)}) collective-permute-start(bf16[8,2048]{1,0:T(8,128)(2,1)S(1)} %fusion.3), channel_id=1, source_target_pairs={{0,4},{2,6},{4,0},{6,2},{8,12},{10,14},{12,8},{14,10},{16,20},{18,... | collective-permute-start | bytes 98312 | tf_op jit(solution)/shard_map/ppermute | solution.py:368
  61.8 2.0 %collective-permute-done.9 = bf16[24,2048]{1,0:T(8,128)(2,1)S(1)} collective-permute-done((bf16[24,2048]{1,0:T(8,128)(2,1)S(1)}, bf16[24,2048]{1,0:T(8,128)(2,1)S(1)}, u32[]{:S(2)}, u32[]{:S(2)}) %collective-permute-start.9) | collective-permute-done | bytes 98336 | tf_op jit(solution)/shard_map/ppermute | solution.py:368
  63.8 0.8 collective-permute-start.10
  64.6 0.9 %fusion.4 = bf16[8,2048]{1,0:T(8,128)(2,1)S(1)} fusion(bf16[8,2048]{1,0:T(8,128)(2,1)S(1)} %collective-permute-done.5, f32[8,2048]{1,0:T(8,128)} %get-tuple-element.51, bf16[8,2048]{1,0:T(8,128)(2,1)S(1)} %collective-permute-done.4), kind=kLoop, calls=%fused_computation.49 | loop fusion | flops 81920 | bytes 163840 | tf_op jit(solution)/shard_map/convert_element_type | solution.py:370
  65.5 1.4 %collective-permute-start.6 = (bf16[8,2048]{1,0:T(8,128)(2,1)S(1)}, bf16[8,2048]{1,0:T(8,128)(2,1)S(1)}, u32[]{:S(2)}, u32[]{:S(2)}) collective-permute-start(bf16[8,2048]{1,0:T(8,128)(2,1)S(1)} %fusion.4), channel_id=1, source_target_pairs={{0,8},{2,10},{4,12},{6,14},{8,0},{10,2},{12,4},{14,6},{16,24},{18,... | collective-permute-start | bytes 98312 | tf_op jit(solution)/shard_map/ppermute | solution.py:368
  66.9 2.0 %collective-permute-done.10 = bf16[24,2048]{1,0:T(8,128)(2,1)S(1)} collective-permute-done((bf16[24,2048]{1,0:T(8,128)(2,1)S(1)}, bf16[24,2048]{1,0:T(8,128)(2,1)S(1)}, u32[]{:S(2)}, u32[]{:S(2)}) %collective-permute-start.10) | collective-permute-done | bytes 98336 | tf_op jit(solution)/shard_map/ppermute | solution.py:368
  68.9 2.1 %collective-permute-start.11 = (bf16[24,2048]{1,0:T(8,128)(2,1)S(1)}, bf16[24,2048]{1,0:T(8,128)(2,1)S(1)}, u32[]{:S(2)}, u32[]{:S(2)}) collective-permute-start(bf16[24,2048]{1,0:T(8,128)(2,1)S(1)} %fusion), channel_id=1, source_target_pairs={{0,4},{2,6},{4,0},{6,2},{8,12},{10,14},{12,8},{14,10},{16,20},{18,... | collective-permute-start | bytes 294920 | tf_op jit(solution)/shard_map/ppermute | solution.py:368
  71.1 1.8 %collective-permute-start.7 = (bf16[8,2048]{1,0:T(8,128)(2,1)S(1)}, bf16[8,2048]{1,0:T(8,128)(2,1)S(1)}, u32[]{:S(2)}, u32[]{:S(2)}) collective-permute-start(bf16[8,2048]{1,0:T(8,128)(2,1)S(1)} %get-tuple-element.57), channel_id=1, source_target_pairs={{0,16},{2,18},{4,20},{6,22},{8,24},{10,26},{12,28},{14,30},{16,0},... | collective-permute-start | bytes 98312 | tf_op jit(solution)/shard_map/ppermute | solution.py:368
  72.9 0.8 collective-permute-done.11
  73.7 0.4 collective-permute-start.12
  74.1 1.8 %collective-permute-done.7 = bf16[8,2048]{1,0:T(8,128)(2,1)S(1)} collective-permute-done((bf16[8,2048]{1,0:T(8,128)(2,1)S(1)}, bf16[8,2048]{1,0:T(8,128)(2,1)S(1)}, u32[]{:S(2)}, u32[]{:S(2)}) %collective-permute-start.7) | collective-permute-done | bytes 32800 | tf_op jit(solution)/shard_map/ppermute | solution.py:368
  76.0 2.4 %collective-permute-done.12 = bf16[24,2048]{1,0:T(8,128)(2,1)S(1)} collective-permute-done((bf16[24,2048]{1,0:T(8,128)(2,1)S(1)}, bf16[24,2048]{1,0:T(8,128)(2,1)S(1)}, u32[]{:S(2)}, u32[]{:S(2)}) %collective-permute-start.12) | collective-permute-done | bytes 98336 | tf_op jit(solution)/shard_map/ppermute | solution.py:368
  78.7 0.7 pad_maximum_fusion
  (67 shorter events, 0.8 us)
Async XLA Ops:
  1.6 10.2 %collective-permute-start.1 = (bf16[128,128]{0,1:T(8,128)(2,1)S(1)}, bf16[128,128]{0,1:T(8,128)(2,1)S(1)}, u32[]{:S(2)}, u32[]{:S(2)}) collective-permute-start(bf16[128,128]{0,1:T(8,128)(2,1)S(1)} %copy.17), channel_id=1, source_target_pairs={{0,1},{1,0},{2,3},{3,2},{4,5},{5,4},{6,7},{7,6},{8,9},{9,8},{10,11... | collective-permute-start | bytes 98312 | tf_op jit(solution)/shard_map/ppermute | solution.py:347
  6.0 7.4 %collective-permute-start = (bf16[24,2048]{1,0:T(8,128)(2,1)}, bf16[24,2048]{1,0:T(8,128)(2,1)S(1)}, u32[]{:S(2)}, u32[]{:S(2)}) collective-permute-start(bf16[24,2048]{1,0:T(8,128)(2,1)} %get-tuple-element.31.ends), channel_id=1, source_target_pairs={{0,2},{2,4},{4,6},{6,8},{8,10},{10,12},{12,14},{14,16},{16,18},{18... | collective-permute-start | bytes 294920 | tf_op jit(solution)/shard_map/ppermute | solution.py:338
  10.4 21.5 %collective-permute-start.3 = (bf16[160,2048]{1,0:T(8,128)(2,1)}, bf16[160,2048]{1,0:T(8,128)(2,1)S(1)}, u32[]{:S(2)}, u32[]{:S(2)}) collective-permute-start(bf16[160,2048]{1,0:T(8,128)(2,1)} %get-tuple-element.38), channel_id=1, source_target_pairs={{2,0},{4,2},{6,4},{8,6},{10,8},{12,10},{14,12},{16,14},{18,16},{20... | collective-permute-start | bytes 1966088 | tf_op jit(solution)/shard_map/ppermute | solution.py:338
  13.4 0.7 copy-start.7
  21.7 25.0 %collective-permute-start.2 = (bf16[128,2048]{1,0:T(8,128)(2,1)}, bf16[128,2048]{1,0:T(8,128)(2,1)S(1)}, u32[]{:S(2)}, u32[]{:S(2)}) collective-permute-start(bf16[128,2048]{1,0:T(8,128)(2,1)} %get-tuple-element.37), channel_id=1, source_target_pairs={{0,2},{2,4},{4,6},{6,8},{8,10},{10,12},{12,14},{14,16},{16,18},{18... | collective-permute-start | bytes 1572872 | tf_op jit(solution)/shard_map/ppermute | solution.py:338
  31.9 0.8 %copy-start.5 = (bf16[160,2048]{1,0:T(8,128)(2,1)}, bf16[160,2048]{1,0:T(8,128)(2,1)S(1)}, u32[]{:S(2)}) copy-start(bf16[160,2048]{1,0:T(8,128)(2,1)S(1)} %collective-permute-done.3.ahead) | copy-start | bytes 1966084
  42.2 13.5 %collective-permute-start.8 = (bf16[128,128]{1,0:T(8,128)(2,1)}, bf16[128,128]{1,0:T(8,128)(2,1)S(1)}, u32[]{:S(2)}, u32[]{:S(2)}) collective-permute-start(bf16[128,128]{1,0:T(8,128)(2,1)} %get-tuple-element.55), channel_id=1, source_target_pairs={{0,1},{1,0},{2,3},{3,2},{4,5},{5,4},{6,7},{7,6},{8,9},{9,8},{10,11... | collective-permute-start | bytes 98312 | tf_op jit(solution)/shard_map/ppermute | solution.py:356
  46.6 0.8 %copy-start.6 = (bf16[128,2048]{1,0:T(8,128)(2,1)}, bf16[128,2048]{1,0:T(8,128)(2,1)S(1)}, u32[]{:S(2)}) copy-start(bf16[128,2048]{1,0:T(8,128)(2,1)S(1)} %collective-permute-done.2.behind) | copy-start | bytes 1572868
  47.4 8.2 %copy-start.3 = (f32[128,128]{1,0:T(8,128)S(1)}, f32[128,128]{1,0:T(8,128)}, u32[]{:S(2)}) copy-start(f32[128,128]{1,0:T(8,128)} %get-tuple-element.54) | copy-start | bytes 196612
  47.4 8.4 %copy-start.2 = (bf16[16,2048]{1,0:T(8,128)(2,1)S(1)}, bf16[16,2048]{1,0:T(8,128)(2,1)}, u32[]{:S(2)}) copy-start(bf16[16,2048]{1,0:T(8,128)(2,1)} %get-tuple-element.56) | copy-start | bytes 196612
  47.4 16.4 %copy-start = (f32[16,2048]{1,0:T(8,128)S(1)}, f32[16,2048]{1,0:T(8,128)}, u32[]{:S(2)}) copy-start(f32[16,2048]{1,0:T(8,128)} %get-tuple-element.53) | copy-start | bytes 393220
  53.2 17.9 %copy-start.1 = (f32[8,2048]{1,0:T(8,128)S(1)}, f32[8,2048]{1,0:T(8,128)}, u32[]{:S(2)}) copy-start(f32[8,2048]{1,0:T(8,128)} %get-tuple-element.51) | copy-start | bytes 196612
  53.2 5.3 %collective-permute-start.4 = (bf16[8,2048]{1,0:T(8,128)(2,1)}, bf16[8,2048]{1,0:T(8,128)(2,1)S(1)}, u32[]{:S(2)}, u32[]{:S(2)}) collective-permute-start(bf16[8,2048]{1,0:T(8,128)(2,1)} %get-tuple-element.52), channel_id=1, source_target_pairs={{0,2},{2,0},{4,6},{6,4},{8,10},{10,8},{12,14},{14,12},{16,18},{18,... | collective-permute-start | bytes 98312 | tf_op jit(solution)/shard_map/ppermute | solution.py:368
  55.8 8.0 %collective-permute-start.9 = (bf16[24,2048]{1,0:T(8,128)(2,1)S(1)}, bf16[24,2048]{1,0:T(8,128)(2,1)S(1)}, u32[]{:S(2)}, u32[]{:S(2)}) collective-permute-start(bf16[24,2048]{1,0:T(8,128)(2,1)S(1)} %pad_maximum_fusion.1), channel_id=1, source_target_pairs={{0,16},{2,18},{4,20},{6,22},{8,24},{10,26},{12,28},{14,30},{16,0},... | collective-permute-start | bytes 294920 | tf_op jit(solution)/shard_map/ppermute | solution.py:368
  59.4 5.2 %collective-permute-start.5 = (bf16[8,2048]{1,0:T(8,128)(2,1)S(1)}, bf16[8,2048]{1,0:T(8,128)(2,1)S(1)}, u32[]{:S(2)}, u32[]{:S(2)}) collective-permute-start(bf16[8,2048]{1,0:T(8,128)(2,1)S(1)} %fusion.3), channel_id=1, source_target_pairs={{0,4},{2,6},{4,0},{6,2},{8,12},{10,14},{12,8},{14,10},{16,20},{18,... | collective-permute-start | bytes 98312 | tf_op jit(solution)/shard_map/ppermute | solution.py:368
  63.8 5.0 %collective-permute-start.10 = (bf16[24,2048]{1,0:T(8,128)(2,1)S(1)}, bf16[24,2048]{1,0:T(8,128)(2,1)S(1)}, u32[]{:S(2)}, u32[]{:S(2)}) collective-permute-start(bf16[24,2048]{1,0:T(8,128)(2,1)S(1)} %fusion.5), channel_id=1, source_target_pairs={{0,8},{2,10},{4,12},{6,14},{8,0},{10,2},{12,4},{14,6},{16,24},{18,... | collective-permute-start | bytes 294920 | tf_op jit(solution)/shard_map/ppermute | solution.py:368
  65.5 5.6 %collective-permute-start.6 = (bf16[8,2048]{1,0:T(8,128)(2,1)S(1)}, bf16[8,2048]{1,0:T(8,128)(2,1)S(1)}, u32[]{:S(2)}, u32[]{:S(2)}) collective-permute-start(bf16[8,2048]{1,0:T(8,128)(2,1)S(1)} %fusion.4), channel_id=1, source_target_pairs={{0,8},{2,10},{4,12},{6,14},{8,0},{10,2},{12,4},{14,6},{16,24},{18,... | collective-permute-start | bytes 98312 | tf_op jit(solution)/shard_map/ppermute | solution.py:368
  68.9 4.7 %collective-permute-start.11 = (bf16[24,2048]{1,0:T(8,128)(2,1)S(1)}, bf16[24,2048]{1,0:T(8,128)(2,1)S(1)}, u32[]{:S(2)}, u32[]{:S(2)}) collective-permute-start(bf16[24,2048]{1,0:T(8,128)(2,1)S(1)} %fusion), channel_id=1, source_target_pairs={{0,4},{2,6},{4,0},{6,2},{8,12},{10,14},{12,8},{14,10},{16,20},{18,... | collective-permute-start | bytes 294920 | tf_op jit(solution)/shard_map/ppermute | solution.py:368
  71.1 4.9 %collective-permute-start.7 = (bf16[8,2048]{1,0:T(8,128)(2,1)S(1)}, bf16[8,2048]{1,0:T(8,128)(2,1)S(1)}, u32[]{:S(2)}, u32[]{:S(2)}) collective-permute-start(bf16[8,2048]{1,0:T(8,128)(2,1)S(1)} %get-tuple-element.57), channel_id=1, source_target_pairs={{0,16},{2,18},{4,20},{6,22},{8,24},{10,26},{12,28},{14,30},{16,0},... | collective-permute-start | bytes 98312 | tf_op jit(solution)/shard_map/ppermute | solution.py:368
  73.7 4.7 %collective-permute-start.12 = (bf16[24,2048]{1,0:T(8,128)(2,1)S(1)}, bf16[24,2048]{1,0:T(8,128)(2,1)S(1)}, u32[]{:S(2)}, u32[]{:S(2)}) collective-permute-start(bf16[24,2048]{1,0:T(8,128)(2,1)S(1)} %fusion.1), channel_id=1, source_target_pairs={{0,2},{2,0},{4,6},{6,4},{8,10},{10,8},{12,14},{14,12},{16,18},{18,... | collective-permute-start | bytes 294920 | tf_op jit(solution)/shard_map/ppermute | solution.py:368
  78.6 0.7 copy-start.4

commit v4 on v3

--- a/solution.py
+++ b/solution.py
@@ -71,6 +71,7 @@
 
 
 LANES = 128
+ROOM = 40 * 1024 * 1024
 CHUNK = 64
 
 
@@ -138,7 +139,7 @@
 
 def second_kernel(
     q, k, v, g, tails, w, taps, half, low,
-    gated_out, ggi_out, ks_out, vs_out, inner_out, behind_out, spec_out,
+    gated_out, ggi_out, ks_out, vs_out, inner_out, behind_out, spec_out, rows_out,
     xq, xk, xv, tap_spec,
 ):
     rows, width = q.shape
@@ -153,6 +154,7 @@
         tap_spec[1] = jnp.where(first, 0.0, imag)
         tap_spec[2] = jnp.where(first, imag, real)
         spec_out[...] = tap_spec[...]
+        rows_out[...] = taps[...].astype(F32).T[:HALO]
 
     tail = tails[...].astype(F32)
     for at, (ref, x) in enumerate(((xq, q), (xk, k), (xv, v))):
@@ -313,11 +315,16 @@
 
 
 def fifth_kernel(
-    q, tails, following, sums, w, g, inner, behind, spec, half, high, gq_in,
-    gq_out, sums_out, send_out,
-    xq, yq,
+    q, tails, following, sums, w, g, inner, behind, spec, half, high, gq_in, own, *refs,
 ):
+    *parts, gq_out, sums_out, send_out, xq, yq = refs
     width = q.shape[1]
+    total = own[...]
+    for part in parts:
+        total = total + part[...].astype(F32)
+    count = total.shape[0] // (width // LANES)
+    for h, lanes in halves(width):
+        sums_out[HALO:, lanes] = total[h * count : (h + 1) * count]
     put(xq, 0, tails[...].astype(F32)[:HALO])
     put(xq, HALO, q[...].astype(F32))
     put(yq, BLOCK, following[...])
@@ -328,7 +335,7 @@
         weights = taps_of(w, 0, lanes)
         for at, size in pieces(BLOCK):
             gq_out[at : at + size, lanes] = anticausal(yq, h, at, size, weights).astype(BF16)
-        sums_out[:, lanes] = sums[:, lanes] + lag_sums(yq, 0, xq, HALO, h, BLOCK, w.shape[1])
+        sums_out[:HALO, lanes] = sums[:, lanes] + lag_sums(yq, 0, xq, HALO, h, BLOCK, w.shape[1])
     send_out[...] = sums_out[...].astype(BF16)
 
 
@@ -349,14 +356,12 @@
     return result
 
 
-def exchange_sum(own, sends, axis):
+def exchanged(sends, axis):
     count = lax.axis_size(axis)
-    total = own
-    for step, part in enumerate(sends, 1):
-        total = total + lax.ppermute(
-            part, axis, [(s, (s + step) % count) for s in range(count)]
-        ).astype(F32)
-    return total
+    return [
+        lax.ppermute(part, axis, [(s, (s + step) % count) for s in range(count)])
+        for step, part in enumerate(sends, 1)
+    ]
 
 
 def sum_over(value, sent, axis, reverse=False):
@@ -401,7 +406,13 @@
     def cost(flops, moved):
         return pl.CostEstimate(flops=int(flops), bytes_accessed=int(moved), transcendentals=0)
 
-    wide = 2 * width
+    query, key, value, grad_out, short_filter = (
+        in_hbm(x) for x in (query, key, value, grad_out, short_filter)
+    )
+    whole, half, low, high = (in_hbm(x) for x in (whole, half, low, high))
+    room = pltpu.CompilerParams(vmem_limit_bytes=ROOM)
+    wide = min(4 * width, channels)
+    pair = min(2 * width, channels)
     last = rows // (2 * HALO) - 1
     tails, ahead = pl.pallas_call(
         first_kernel,
@@ -414,27 +425,30 @@
         out_shape=[out(3 * HALO, BF16), out(BLOCK + 4 * HALO, BF16)],
         scratch_shapes=[scratch(BLOCK + 2 * HALO, wide)],
         name="first",
+        compiler_params=room,
     )(query, grad_out, query, key, value, key, value, short_filter)
     ends = tails
-    tails = in_hbm(shift(tails, "seq", 1))
-    ahead = in_hbm(shift(ahead, "seq", -1))
+    tails = shift(tails, "seq", 1)
+    ahead = shift(ahead, "seq", -1)
     taps = gather_rows(medium_filter.astype(BF16), "fsdp")
 
-    gated, ggi, ks, vs, inner, behind, spec = pl.pallas_call(
+    gated, ggi, ks, vs, inner, behind, spec, tap_rows = pl.pallas_call(
         second_kernel,
         grid=(channels // wide,),
         in_specs=[col(rows, 0, wide)] * 4
         + [col(3 * HALO, 0, wide), filters(wide), fixed(taps.shape), fixed(half.shape), fixed(low.shape)],
-        out_specs=[col(rows, 0, wide)] * 4 + [col(BLOCK, 0, wide)] * 2 + [ fixed((3, BLOCK, width))],
+        out_specs=[col(rows, 0, wide)] * 4 + [col(BLOCK, 0, wide)] * 2 + [fixed((3, BLOCK, width)), fixed((HALO, width))],
         out_shape=[
             out(rows, BF16), out(rows, BF16), out(rows, F32), out(rows, F32),
             out(BLOCK, F32), out(BLOCK, BF16), jax.ShapeDtypeStruct((3, BLOCK, width), F32),
+            jax.ShapeDtypeStruct((HALO, width), F32),
         ],
         scratch_shapes=[scratch(rows + HALO, wide)] * 3 + [pltpu.VMEM((3, BLOCK, width), F32)],
         cost_estimate=cost(4e9, 20e6),
         name="second",
+        compiler_params=room,
     )(query, key, value, grad_out, tails, short_filter, taps, half, low)
-    behind = in_hbm(shift(behind, "seq", 1))
+    behind = shift(behind, "seq", 1)
 
     share = lax.axis_size("fsdp")
     me = lax.axis_index("fsdp").astype(jnp.int32).reshape(1)
@@ -443,11 +457,14 @@
     def big(count, at=0):
         return pl.BlockSpec((count, wide), lambda i, *_: (at, i))
 
+    def two(count, at=0):
+        return pl.BlockSpec((count, pair), lambda i, *_: (at, i))
+
     def still(shape):
         return pl.BlockSpec(shape, lambda i, *_: (0,) * len(shape))
 
+    two_filters = pl.BlockSpec((3, taps_short, pair), lambda i, *_: (0, 0, i))
     big_filters = pl.BlockSpec((3, taps_short, wide), lambda i, *_: (0, 0, i))
-    tap_rows = taps[:, :HALO].astype(F32).T
     corner = BLOCK // rest
     edge_block = rows // (2 * HALO) - 1
     grad_query, nexts, sums_q, more = pl.pallas_call(
@@ -460,6 +477,7 @@
         scratch_shapes=[scratch(rest + 2 * HALO, wide)] * 2,
         cost_estimate=cost(2e9, 8e6),
         name="middle",
+        compiler_params=room,
     )(query, grad_out, gated, short_filter, spec, whole, high)
 
     mine = (width // share, BLOCK)
@@ -467,19 +485,19 @@
         third_kernel,
         grid_spec=pltpu.PrefetchScalarGridSpec(
             num_scalar_prefetch=1,
-            grid=(many,),
-            in_specs=[big(rows)] * 2
-            + [big(3 * HALO)] * 2
-            + [big(BLOCK + 4 * HALO)]
-            + [big(rows)] * 4
-            + [big(HALO), still(tap_rows.shape), big_filters, still((3, BLOCK, width))]
+            grid=(channels // pair,),
+            in_specs=[two(rows)] * 2
+            + [two(3 * HALO)] * 2
+            + [two(BLOCK + 4 * HALO)]
+            + [two(rows)] * 4
+            + [two(HALO), still(tap_rows.shape), two_filters, still((3, BLOCK, width))]
             + [still(m.shape) for m in (half, whole, low)],
-            out_specs=[big(rows + 2 * HALO)] * 2
-            + [big(HALO)]
-            + [big(2 * HALO)] * 2
+            out_specs=[two(rows + 2 * HALO)] * 2
+            + [two(HALO)]
+            + [two(2 * HALO)] * 2
             + [still(mine)] * share,
-            scratch_shapes=[pltpu.VMEM((3, wide // LANES, 3 * HALO, LANES), F32)]
-            + [scratch(rows + 2 * HALO, wide)] * 4
+            scratch_shapes=[pltpu.VMEM((3, pair // LANES, 3 * HALO, LANES), F32)]
+            + [scratch(rows + 2 * HALO, pair)] * 4
             + [pltpu.VMEM((3, BLOCK, width), F32), pltpu.VMEM((width, BLOCK), F32)],
         ),
         out_shape=[out(rows + 2 * HALO, BF16)] * 2
@@ -488,9 +506,10 @@
         + [jax.ShapeDtypeStruct(mine, BF16)] * (share - 1),
         cost_estimate=cost(8e9, 20e6),
         name="third",
+        compiler_params=room,
     )(me, key, value, tails, ends, ahead, gated, ggi, ks, vs, more, tap_rows,
       short_filter, spec, half, whole, low)
-    medium = exchange_sum(own, sends, "fsdp")
+    parts = exchanged(sends, "fsdp")
 
     grad_key, grad_value, grad_query = pl.pallas_call(
         fourth_kernel,
@@ -503,33 +522,34 @@
         input_output_aliases={5: 2},
         cost_estimate=cost(4e9, 10e6),
         name="fourth",
+        compiler_params=room,
     )(gk, gv, nexts, far, short_filter, grad_query)
 
+    extra = mine[0] * BLOCK // channels
     grad_query, sums_q, sent_q = pl.pallas_call(
         fifth_kernel,
         grid=(many,),
         in_specs=[big(BLOCK), big(3 * HALO), big(HALO), big(HALO), big_filters]
         + [big(BLOCK)] * 3
         + [still((3, BLOCK, width)), still(half.shape), still(high.shape)]
-        + [pl.BlockSpec(memory_space=pl.ANY)],
-        out_specs=[big(BLOCK), big(HALO), big(HALO)],
-        out_shape=[out(rows, BF16), out(HALO, F32), out(HALO, BF16)],
+        + [pl.BlockSpec(memory_space=pl.ANY)]
+        + [pl.BlockSpec((mine[0] * wide // channels, BLOCK), lambda i: (i, 0))] * share,
+        out_specs=[big(BLOCK), big(HALO + extra), big(HALO + extra)],
+        out_shape=[out(rows, BF16), out(HALO + extra, F32), out(HALO + extra, BF16)],
         scratch_shapes=[scratch(BLOCK + HALO, wide)] * 2,
         input_output_aliases={11: 0},
         cost_estimate=cost(2e9, 8e6),
         name="fifth",
+        compiler_params=room,
     )(query, tails, nexts, sums_q, short_filter, grad_out, inner, behind, spec, half, high,
-      grad_query)
-
-    per = channels // BLOCK
-    count = medium.shape[0] // per
-    packed = jnp.concatenate([medium[i * count : (i + 1) * count] for i in range(per)], axis=1)
-    early = jnp.concatenate([sums_kv, packed], axis=0)
-    sent = jnp.concatenate([sent_kv, packed.astype(BF16)], axis=0)
-    early = sum_over(early, sent, "seq", reverse=True)
+      grad_query, own, *parts)
+
+    early = sum_over(sums_kv, sent_kv, "seq", reverse=True)
     late = sum_over(sums_q, sent_q, "seq")
-    packed = early[2 * HALO :]
-    grad_medium = jnp.concatenate([packed[:, i * BLOCK : (i + 1) * BLOCK] for i in range(per)], axis=0)
+    packed = late[HALO:]
+    grad_medium = jnp.concatenate(
+        [packed[:, at : at + BLOCK] for at in range(0, channels, BLOCK)], axis=0
+    )
     grad_short = jnp.stack([late[:taps_short], early[:taps_short], early[HALO : HALO + taps_short]])
     return grad_query, grad_key, grad_value, grad_short, grad_medium
 

time: 80.1 us -> 77 us (0.961)
  Pallas kernels: 36.9 us -> 29.1 us
  starting transfers between devices: 24.8 us -> 30.9 us
  waiting for transfers between devices: 9.26 us -> 13.8 us
  local copies, waits for them, and re-layouts: 4.15 us -> 0.1 us
  other arithmetic: 3.23 us -> 1.79 us
    ppermute x8, starting transfers between devices: 14.1 us -> 20.1 us  [sum_over(): other = lax.ppermute(sent, axis, [(s, s ^ 1 << bit) for s in range(count)])]
    unnamed x47 -> x17, local copies, waits for them, and re-layouts: 3.36 us -> 0.05 us
    ppermute x3, waiting for transfers between devices: 0.26 us -> 2.69 us  [shift(): lax.ppermute(value, axis, [(s, s + steps) for s in range(initial, last)])]
    ppermute x8, waiting for transfers between devices: 9 us -> 11.1 us  [sum_over(): other = lax.ppermute(sent, axis, [(s, s ^ 1 << bit) for s in range(count)])]
    pallas_call x1, Pallas kernels: 3.82 us -> 1.96 us  [shards(): pl.pallas_call(first_kernel, grid=(channels // wide,), in_specs=[col(BLOC...]
    convert_element_type x6, other arithmetic: 1.84 us -> 0.15 us  [sum_over(): sent = value.astype(BF16)]
    pallas_call x1, Pallas kernels: 7.64 us -> 5.99 us  [shards(): pl.pallas_call(second_kernel, grid=(channels // wide,), in_specs=[col(row...]
    pallas_call x1, Pallas kernels: 5.74 us -> 4.46 us  [shards(): pl.pallas_call(fifth_kernel, grid=(many,), in_specs=[big(BLOCK), big(3 *...]
  transfers between devices with their start and end apart: 13 -> 13, of which waited for: 6 -> 7; matrix products, arithmetic and copies ran while one was open for 4% -> 0% of each run, Pallas kernels for 46% -> 38%
where the time goes in v4:
time: 77 us; the launch traced here: 76.6 us
  starting transfers between devices  30.9 us (40%)
  Pallas kernels  29.1 us (38%)
  waiting for transfers between devices  13.8 us (18%)
  other arithmetic  1.79 us (2%)
  between operations  0.94 us (1%)
    ppermute x8, starting transfers between devices, sum_over(): other = lax.ppermute(sent, axis, [(s, s ^ 1 << bit) for s in range(count)])  20.1 us
    ppermute x8, waiting for transfers between devices, sum_over(): other = lax.ppermute(sent, axis, [(s, s ^ 1 << bit) for s in range(count)])  11.1 us
    ppermute x3, starting transfers between devices, shift(): lax.ppermute(value, axis, [(s, s + steps) for s in range(initial, last)])  10.1 us
    pallas_call x1, Pallas kernels, shards(): pl.pallas_call(third_kernel, grid_spec=pltpu.PrefetchScalarGridSpec(num_s...  8.25 us
    pallas_call x1, Pallas kernels, shards(): pl.pallas_call(second_kernel, grid=(channels // wide,), in_specs=[col(row...  5.99 us
    pallas_call x1, Pallas kernels, shards(): pl.pallas_call(middle_kernel, grid=(many,), in_specs=[big(rows), big(rest...  5.03 us
    pallas_call x1, Pallas kernels, shards(): pl.pallas_call(fifth_kernel, grid=(many,), in_specs=[big(BLOCK), big(3 *...  4.46 us
    pallas_call x1, Pallas kernels, shards(): pl.pallas_call(fourth_kernel, grid=(many,), in_specs=[big(rows + 2 * HALO...  3.45 us
  transfers between devices with their start and end apart: 13, of which 7 were waited for; matrix products, arithmetic and copies ran while one was open for 0% of the time, Pallas kernels for 38%

profile of v4, /device:TPU:0, one launch (start us, length us, event | category | flops | bytes accessed | tf_op | source)
XLA Modules:
  0.0 76.6 jit_solution(17701890415069024779)
XLA Ops:
  0.7 0.9 %constant_dynamic-update-slice_fusion.17 = (bf16[256,128]{1,0:T(8,128)(2,1)S(1)}, bf16[128,128]{1,0:T(8,128)(2,1)S(1)}) fusion(bf16[256,128]{1,0:T(8,128)(2,1)S(1)} %broadcast_in_dim.3, s32[]{:T(128)S(6)} %select_n.13, f32[128,128]{1,0:T(8,128)} %param.15), kind=kLoop, calls=%fused_computation.33 | loop fusion | flops 16384 | bytes 131076 | tf_op jit(solution)/shard_map/dynamic_update_slice | solution.py:352
  1.5 0.6 collective-permute-start.1
  2.1 2.0 %first.1 = (bf16[24,2048]{1,0:T(8,128)(2,1)S(1)}, bf16[160,2048]{1,0:T(8,128)(2,1)S(1)}) custom-call(bf16[192,2048]{1,0:T(8,128)(2,1)} %q.7, bf16[192,2048]{1,0:T(8,128)(2,1)} %g.7, bf16[192,2048]{1,0:T(8,128)(2,1)} %q.7, bf16[192,2048]{1,0:T(8,128)(2,1)} %k.3, bf16[192,2048]{1,0:T(8,128)(2,1)} %v.3, bf16[192,2048]{1,0:T(8,128)(2,1)} %k.3, ...), custom_call_target="tpu_custom_call" | custom-call | tf_op jit(solution)/shard_map/first/pallas_call | solution.py:417
  4.0 4.4 %collective-permute-start = (bf16[24,2048]{1,0:T(8,128)(2,1)S(1)}, bf16[24,2048]{1,0:T(8,128)(2,1)S(1)}, u32[]{:S(2)}, u32[]{:S(2)}) collective-permute-start(bf16[24,2048]{1,0:T(8,128)(2,1)S(1)} %get-tuple-element.32.ends), channel_id=1, source_target_pairs={{0,2},{2,4},{4,6},{6,8},{8,10},{10,12},{12,14},{14,16},{16,18},{18... | collective-permute-start | bytes 294920 | tf_op jit(solution)/shard_map/ppermute | solution.py:345
  8.5 1.3 %collective-permute-start.3 = (bf16[160,2048]{1,0:T(8,128)(2,1)S(1)}, bf16[160,2048]{1,0:T(8,128)(2,1)S(1)}, u32[]{:S(2)}, u32[]{:S(2)}) collective-permute-start(bf16[160,2048]{1,0:T(8,128)(2,1)S(1)} %get-tuple-element.39), channel_id=1, source_target_pairs={{2,0},{4,2},{6,4},{8,6},{10,8},{12,10},{14,12},{16,14},{18,16},{20... | collective-permute-start | bytes 1966088 | tf_op jit(solution)/shard_map/ppermute | solution.py:345
  9.8 0.0 collective-permute-done.1
  9.8 1.3 %collective-permute-done.tails = bf16[24,2048]{1,0:T(8,128)(2,1)S(1)} collective-permute-done((bf16[24,2048]{1,0:T(8,128)(2,1)S(1)}, bf16[24,2048]{1,0:T(8,128)(2,1)S(1)}, u32[]{:S(2)}, u32[]{:S(2)}) %collective-permute-start) | collective-permute-done | bytes 98336 | tf_op jit(solution)/shard_map/ppermute | solution.py:345
  11.1 6.0 %second.1 = (bf16[192,2048]{1,0:T(8,128)(2,1)S(1)}, bf16[192,2048]{1,0:T(8,128)(2,1)S(1)}, f32[192,2048]{1,0:T(8,128)S(1)}, f32[192,2048]{1,0:T(8,128)S(1)}, f32...) custom-call(bf16[192,2048]{1,0:T(8,128)(2,1)} %q.7, ...), custom_call_target="tpu_custom_call" | custom-call | flops 4000000000 | bytes 20000000 | tf_op jit(solution)/shard_map/second/pallas_call | solution.py:435
  17.1 4.4 %collective-permute-start.2 = (bf16[128,2048]{1,0:T(8,128)(2,1)S(1)}, bf16[128,2048]{1,0:T(8,128)(2,1)S(1)}, u32[]{:S(2)}, u32[]{:S(2)}) collective-permute-start(bf16[128,2048]{1,0:T(8,128)(2,1)S(1)} %get-tuple-element.38), channel_id=1, source_target_pairs={{0,2},{2,4},{4,6},{6,8},{8,10},{10,12},{12,14},{14,16},{16,18},{18... | collective-permute-start | bytes 1572872 | tf_op jit(solution)/shard_map/ppermute | solution.py:345
  21.6 5.0 %middle.1 = (bf16[192,2048]{1,0:T(8,128)(2,1)}, f32[16,2048]{1,0:T(8,128)S(1)}, f32[8,2048]{1,0:T(8,128)S(1)}, f32[8,2048]{1,0:T(8,128)S(1)}) custom-call(bf16[192,2048]{1,0:T(8,128)(2,1)} %q.7, bf16[192,2048]{1,0:T(8,128)(2,1)} %g.7, bf16[192,2048]{1,0:T(8,128)(2,1)S(1)} %get-tuple-element.33.gated, f32[3,7,2048]{2,1,0:T(8,128)} %w.11, ...), custom_call_target="tpu_custom_call" | custom-call | flops 2000000000 | bytes 8000000 | tf_op jit(solution)/shard_map/middle/pallas_call | solution.py:470
  26.6 1.4 %collective-permute-done.3.ahead = bf16[160,2048]{1,0:T(8,128)(2,1)S(1)} collective-permute-done((bf16[160,2048]{1,0:T(8,128)(2,1)S(1)}, bf16[160,2048]{1,0:T(8,128)(2,1)S(1)}, u32[]{:S(2)}, u32[]{:S(2)}) %collective-permute-start.3) | collective-permute-done | bytes 655392 | tf_op jit(solution)/shard_map/ppermute | solution.py:345
  28.0 8.3 %third.1 = (bf16[208,2048]{1,0:T(8,128)(2,1)S(1)}, bf16[208,2048]{1,0:T(8,128)(2,1)S(1)}, f32[8,2048]{1,0:T(8,128)S(1)}, f32[16,2048]{1,0:T(8,128)S(1)}, bf16[16...) custom-call(s32[1]{0:T(128)} %bitcast.me, bf16[192,2048]{1,0:T(8,128)(2,1)} %k.3, ...), custom_call_target="tpu_custom_call" | custom-call | flops 8000000000 | bytes 20000000 | tf_op jit(solution)/shard_map/third/pallas_call | solution.py:484
  36.2 0.1 collective-permute-start.4
  36.3 2.6 %collective-permute-start.9 = (bf16[16,2048]{1,0:T(8,128)(2,1)S(1)}, bf16[16,2048]{1,0:T(8,128)(2,1)S(1)}, u32[]{:S(2)}, u32[]{:S(2)}) collective-permute-start(bf16[16,2048]{1,0:T(8,128)(2,1)S(1)} %get-tuple-element.58), channel_id=1, source_target_pairs={{0,16},{2,18},{4,20},{6,22},{8,24},{10,26},{12,28},{14,30},{16,0},... | collective-permute-start | bytes 196616 | tf_op jit(solution)/shard_map/ppermute | solution.py:373
  39.0 3.5 %fourth.1 = (bf16[192,2048]{1,0:T(8,128)(2,1)}, bf16[192,2048]{1,0:T(8,128)(2,1)}, bf16[192,2048]{1,0:T(8,128)(2,1)}) custom-call(bf16[208,2048]{1,0:T(8,128)(2,1)S(1)} %get-tuple-element.45.gk, bf16[208,2048]{1,0:T(8,128)(2,1)S(1)} %get-tuple-element.46.gv, f32[16,2048]{1,0:T(8,128)S(1)} %get-tuple-element.35.near.following, ...), custom_call_target="tpu_custom_call", output_to_operand_aliasing={{2}: (5, {})} | custom-call | flops 4000000000 | bytes 10000000 | tf_op jit(solution)/shard_map/fourth/pallas_call | solution.py:514
  42.4 0.0 collective-permute-done.2.behind
  42.4 0.0 collective-permute-done.4.refs_0_
  42.4 4.5 %fifth.1 = (bf16[192,2048]{1,0:T(8,128)(2,1)}, f32[16,2048]{1,0:T(8,128)S(1)}, bf16[16,2048]{1,0:T(8,128)(2,1)S(1)}) custom-call(bf16[192,2048]{1,0:T(8,128)(2,1)} %q.7, bf16[24,2048]{1,0:T(8,128)(2,1)S(1)} %collective-permute-done.tails, f32[16,2048]{1,0:T(8,128)S(1)} %get-tuple-element.35.near.following, ...), custom_call_target="tpu_custom_call", output_to_operand_aliasing={{0}: (11, {})} | custom-call | flops 2000000000 | bytes 8000000 | tf_op jit(solution)/shard_map/fifth/pallas_call | solution.py:529
  46.9 2.4 %collective-permute-start.5 = (bf16[16,2048]{1,0:T(8,128)(2,1)S(1)}, bf16[16,2048]{1,0:T(8,128)(2,1)S(1)}, u32[]{:S(2)}, u32[]{:S(2)}) collective-permute-start(bf16[16,2048]{1,0:T(8,128)(2,1)S(1)} %get-tuple-element.56), channel_id=1, source_target_pairs={{0,2},{2,0},{4,6},{6,4},{8,10},{10,8},{12,14},{14,12},{16,18},{18,... | collective-permute-start | bytes 196616 | tf_op jit(solution)/shard_map/ppermute | solution.py:373
  49.3 1.6 %collective-permute-start.10 = (bf16[16,2048]{1,0:T(8,128)(2,1)S(1)}, bf16[16,2048]{1,0:T(8,128)(2,1)S(1)}, u32[]{:S(2)}, u32[]{:S(2)}) collective-permute-start(bf16[16,2048]{1,0:T(8,128)(2,1)S(1)} %fusion.2), channel_id=1, source_target_pairs={{0,8},{2,10},{4,12},{6,14},{8,0},{10,2},{12,4},{14,6},{16,24},{18,... | collective-permute-start | bytes 196616 | tf_op jit(solution)/shard_map/ppermute | solution.py:373
  51.0 0.7 collective-permute-done.5
  51.7 11.5 %collective-permute-start.6 = (bf16[16,2048]{1,0:T(8,128)(2,1)S(1)}, bf16[16,2048]{1,0:T(8,128)(2,1)S(1)}, u32[]{:S(2)}, u32[]{:S(2)}) collective-permute-start(bf16[16,2048]{1,0:T(8,128)(2,1)S(1)} %fusion), channel_id=1, source_target_pairs={{0,4},{2,6},{4,0},{6,2},{8,12},{10,14},{12,8},{14,10},{16,20},{18,... | collective-permute-start | bytes 196616 | tf_op jit(solution)/shard_map/ppermute | solution.py:373
  63.3 0.1 collective-permute-start.11
  63.4 2.7 %collective-permute-done.6 = bf16[16,2048]{1,0:T(8,128)(2,1)S(1)} collective-permute-done((bf16[16,2048]{1,0:T(8,128)(2,1)S(1)}, bf16[16,2048]{1,0:T(8,128)(2,1)S(1)}, u32[]{:S(2)}, u32[]{:S(2)}) %collective-permute-start.6) | collective-permute-done | bytes 65568 | tf_op jit(solution)/shard_map/ppermute | solution.py:373
  66.1 1.6 %collective-permute-start.7 = (bf16[16,2048]{1,0:T(8,128)(2,1)S(1)}, bf16[16,2048]{1,0:T(8,128)(2,1)S(1)}, u32[]{:S(2)}, u32[]{:S(2)}) collective-permute-start(bf16[16,2048]{1,0:T(8,128)(2,1)S(1)} %fusion.4), channel_id=1, source_target_pairs={{0,8},{2,10},{4,12},{6,14},{8,0},{10,2},{12,4},{14,6},{16,24},{18,... | collective-permute-start | bytes 196616 | tf_op jit(solution)/shard_map/ppermute | solution.py:373
  67.8 0.1 collective-permute-start.12
  67.9 2.5 %collective-permute-done.7 = bf16[16,2048]{1,0:T(8,128)(2,1)S(1)} collective-permute-done((bf16[16,2048]{1,0:T(8,128)(2,1)S(1)}, bf16[16,2048]{1,0:T(8,128)(2,1)S(1)}, u32[]{:S(2)}, u32[]{:S(2)}) %collective-permute-start.7) | collective-permute-done | bytes 65568 | tf_op jit(solution)/shard_map/ppermute | solution.py:373
  70.4 0.1 collective-permute-start.8
  70.5 1.6 %collective-permute-done.12 = bf16[16,2048]{1,0:T(8,128)(2,1)S(1)} collective-permute-done((bf16[16,2048]{1,0:T(8,128)(2,1)S(1)}, bf16[16,2048]{1,0:T(8,128)(2,1)S(1)}, u32[]{:S(2)}, u32[]{:S(2)}) %collective-permute-start.12) | collective-permute-done | bytes 65568 | tf_op jit(solution)/shard_map/ppermute | solution.py:373
  72.2 3.5 %collective-permute-done.8 = bf16[16,2048]{1,0:T(8,128)(2,1)S(1)} collective-permute-done((bf16[16,2048]{1,0:T(8,128)(2,1)S(1)}, bf16[16,2048]{1,0:T(8,128)(2,1)S(1)}, u32[]{:S(2)}, u32[]{:S(2)}) %collective-permute-start.8) | collective-permute-done | bytes 65568 | tf_op jit(solution)/shard_map/ppermute | solution.py:373
  75.9 0.0 copy-start
  75.9 0.7 pad_maximum_fusion
  (32 shorter events, 0.3 us)
Async XLA Ops:
  1.5 8.3 %collective-permute-start.1 = (bf16[128,128]{1,0:T(8,128)(2,1)S(1)}, bf16[128,128]{1,0:T(8,128)(2,1)S(1)}, u32[]{:S(2)}, u32[]{:S(2)}) collective-permute-start(bf16[128,128]{1,0:T(8,128)(2,1)S(1)} %get-tuple-element.60), channel_id=1, source_target_pairs={{0,1},{1,0},{2,3},{3,2},{4,5},{5,4},{6,7},{7,6},{8,9},{9,8},{10,11... | collective-permute-start | bytes 98312 | tf_op jit(solution)/shard_map/ppermute | solution.py:354
  4.0 7.1 %collective-permute-start = (bf16[24,2048]{1,0:T(8,128)(2,1)S(1)}, bf16[24,2048]{1,0:T(8,128)(2,1)S(1)}, u32[]{:S(2)}, u32[]{:S(2)}) collective-permute-start(bf16[24,2048]{1,0:T(8,128)(2,1)S(1)} %get-tuple-element.32.ends), channel_id=1, source_target_pairs={{0,2},{2,4},{4,6},{6,8},{8,10},{10,12},{12,14},{14,16},{16,18},{18... | collective-permute-start | bytes 294920 | tf_op jit(solution)/shard_map/ppermute | solution.py:345
  8.5 19.5 %collective-permute-start.3 = (bf16[160,2048]{1,0:T(8,128)(2,1)S(1)}, bf16[160,2048]{1,0:T(8,128)(2,1)S(1)}, u32[]{:S(2)}, u32[]{:S(2)}) collective-permute-start(bf16[160,2048]{1,0:T(8,128)(2,1)S(1)} %get-tuple-element.39), channel_id=1, source_target_pairs={{2,0},{4,2},{6,4},{8,6},{10,8},{12,10},{14,12},{16,14},{18,16},{20... | collective-permute-start | bytes 1966088 | tf_op jit(solution)/shard_map/ppermute | solution.py:345
  17.1 25.3 %collective-permute-start.2 = (bf16[128,2048]{1,0:T(8,128)(2,1)S(1)}, bf16[128,2048]{1,0:T(8,128)(2,1)S(1)}, u32[]{:S(2)}, u32[]{:S(2)}) collective-permute-start(bf16[128,2048]{1,0:T(8,128)(2,1)S(1)} %get-tuple-element.38), channel_id=1, source_target_pairs={{0,2},{2,4},{4,6},{6,8},{8,10},{10,12},{12,14},{14,16},{16,18},{18... | collective-permute-start | bytes 1572872 | tf_op jit(solution)/shard_map/ppermute | solution.py:345
  36.2 6.2 %collective-permute-start.4 = (bf16[128,128]{1,0:T(8,128)(2,1)S(1)}, bf16[128,128]{1,0:T(8,128)(2,1)S(1)}, u32[]{:S(2)}, u32[]{:S(2)}) collective-permute-start(bf16[128,128]{1,0:T(8,128)(2,1)S(1)} %get-tuple-element.51), channel_id=1, source_target_pairs={{0,1},{1,0},{2,3},{3,2},{4,5},{5,4},{6,7},{7,6},{8,9},{9,8},{10,11... | collective-permute-start | bytes 98312 | tf_op jit(solution)/shard_map/ppermute | solution.py:362
  36.3 13.0 %collective-permute-start.9 = (bf16[16,2048]{1,0:T(8,128)(2,1)S(1)}, bf16[16,2048]{1,0:T(8,128)(2,1)S(1)}, u32[]{:S(2)}, u32[]{:S(2)}) collective-permute-start(bf16[16,2048]{1,0:T(8,128)(2,1)S(1)} %get-tuple-element.58), channel_id=1, source_target_pairs={{0,16},{2,18},{4,20},{6,22},{8,24},{10,26},{12,28},{14,30},{16,0},... | collective-permute-start | bytes 196616 | tf_op jit(solution)/shard_map/ppermute | solution.py:373
  46.9 4.8 %collective-permute-start.5 = (bf16[16,2048]{1,0:T(8,128)(2,1)S(1)}, bf16[16,2048]{1,0:T(8,128)(2,1)S(1)}, u32[]{:S(2)}, u32[]{:S(2)}) collective-permute-start(bf16[16,2048]{1,0:T(8,128)(2,1)S(1)} %get-tuple-element.56), channel_id=1, source_target_pairs={{0,2},{2,0},{4,6},{6,4},{8,10},{10,8},{12,14},{14,12},{16,18},{18,... | collective-permute-start | bytes 196616 | tf_op jit(solution)/shard_map/ppermute | solution.py:373
  49.3 13.9 %collective-permute-start.10 = (bf16[16,2048]{1,0:T(8,128)(2,1)S(1)}, bf16[16,2048]{1,0:T(8,128)(2,1)S(1)}, u32[]{:S(2)}, u32[]{:S(2)}) collective-permute-start(bf16[16,2048]{1,0:T(8,128)(2,1)S(1)} %fusion.2), channel_id=1, source_target_pairs={{0,8},{2,10},{4,12},{6,14},{8,0},{10,2},{12,4},{14,6},{16,24},{18,... | collective-permute-start | bytes 196616 | tf_op jit(solution)/shard_map/ppermute | solution.py:373
  51.7 14.3 %collective-permute-start.6 = (bf16[16,2048]{1,0:T(8,128)(2,1)S(1)}, bf16[16,2048]{1,0:T(8,128)(2,1)S(1)}, u32[]{:S(2)}, u32[]{:S(2)}) collective-permute-start(bf16[16,2048]{1,0:T(8,128)(2,1)S(1)} %fusion), channel_id=1, source_target_pairs={{0,4},{2,6},{4,0},{6,2},{8,12},{10,14},{12,8},{14,10},{16,20},{18,... | collective-permute-start | bytes 196616 | tf_op jit(solution)/shard_map/ppermute | solution.py:373
  63.3 4.5 %collective-permute-start.11 = (bf16[16,2048]{1,0:T(8,128)(2,1)S(1)}, bf16[16,2048]{1,0:T(8,128)(2,1)S(1)}, u32[]{:S(2)}, u32[]{:S(2)}) collective-permute-start(bf16[16,2048]{1,0:T(8,128)(2,1)S(1)} %fusion.5), channel_id=1, source_target_pairs={{0,4},{2,6},{4,0},{6,2},{8,12},{10,14},{12,8},{14,10},{16,20},{18,... | collective-permute-start | bytes 196616 | tf_op jit(solution)/shard_map/ppermute | solution.py:373
  66.1 4.3 %collective-permute-start.7 = (bf16[16,2048]{1,0:T(8,128)(2,1)S(1)}, bf16[16,2048]{1,0:T(8,128)(2,1)S(1)}, u32[]{:S(2)}, u32[]{:S(2)}) collective-permute-start(bf16[16,2048]{1,0:T(8,128)(2,1)S(1)} %fusion.4), channel_id=1, source_target_pairs={{0,8},{2,10},{4,12},{6,14},{8,0},{10,2},{12,4},{14,6},{16,24},{18,... | collective-permute-start | bytes 196616 | tf_op jit(solution)/shard_map/ppermute | solution.py:373
  67.8 4.3 %collective-permute-start.12 = (bf16[16,2048]{1,0:T(8,128)(2,1)S(1)}, bf16[16,2048]{1,0:T(8,128)(2,1)S(1)}, u32[]{:S(2)}, u32[]{:S(2)}) collective-permute-start(bf16[16,2048]{1,0:T(8,128)(2,1)S(1)} %fusion.3), channel_id=1, source_target_pairs={{0,2},{2,0},{4,6},{6,4},{8,10},{10,8},{12,14},{14,12},{16,18},{18,... | collective-permute-start | bytes 196616 | tf_op jit(solution)/shard_map/ppermute | solution.py:373
  70.4 5.2 %collective-permute-start.8 = (bf16[16,2048]{1,0:T(8,128)(2,1)S(1)}, bf16[16,2048]{1,0:T(8,128)(2,1)S(1)}, u32[]{:S(2)}, u32[]{:S(2)}) collective-permute-start(bf16[16,2048]{1,0:T(8,128)(2,1)S(1)} %fusion.1), channel_id=1, source_target_pairs={{0,16},{2,18},{4,20},{6,22},{8,24},{10,26},{12,28},{14,30},{16,0},... | collective-permute-start | bytes 196616 | tf_op jit(solution)/shard_map/ppermute | solution.py:373
  75.9 0.7 copy-start

commit v5 on v4

--- a/solution.py
+++ b/solution.py
@@ -138,24 +138,11 @@
 
 
 def second_kernel(
-    q, k, v, g, tails, w, taps, half, low,
-    gated_out, ggi_out, ks_out, vs_out, inner_out, behind_out, spec_out, rows_out,
-    xq, xk, xv, tap_spec,
+    q, k, v, g, tails, w,
+    gated_out, ggi_out, ks_out, vs_out, behind_out,
+    xq, xk, xv,
 ):
     rows, width = q.shape
-
-    @pl.when(pl.program_id(0) == 0)
-    def _():
-        both = jnp.concatenate([taps[...], taps[...]], axis=1)
-        spec = lax.dot_general(half[...], both, (((1,), (1,)), ((), ())), preferred_element_type=F32)
-        real, imag = spec[:BLOCK], spec[BLOCK:]
-        first = lax.broadcasted_iota(jnp.int32, real.shape, 0) == 0
-        tap_spec[0] = real
-        tap_spec[1] = jnp.where(first, 0.0, imag)
-        tap_spec[2] = jnp.where(first, imag, real)
-        spec_out[...] = tap_spec[...]
-        rows_out[...] = taps[...].astype(F32).T[:HALO]
-
     tail = tails[...].astype(F32)
     for at, (ref, x) in enumerate(((xq, q), (xk, k), (xv, v))):
         put(ref, 0, tail[at * HALO : (at + 1) * HALO])
@@ -172,23 +159,37 @@
             qs = causal(xq, h, HALO + at, size, wq)
             ggi_out[span, lanes] = (g[span, lanes].astype(F32) * qs).astype(BF16)
     behind_out[...] = gated_out[rows - BLOCK :, :]
-    for lanes in blocks(width, taps.shape[0]):
-        first = to_spectrum(half[...], gated_out[:BLOCK, lanes])
-        inner_out[:, lanes] = from_spectrum(low[...], *times(first, tap_spec))
-
-
-def middle_kernel(
-    q, g, gated, w, spec, whole, high,
-    gq_out, next_out, sums_out, more_out,
-    xq, yq,
-):
+
+
+def middle_kernel(me, q, g, gated, w, half, whole, high, own_taps, *refs):
+    *more_taps, gq_out, next_out, sums_out, more_out, spec_out, rows_out, xq, yq, spec, taps = refs
     rows, width = gated.shape
     rest = rows - BLOCK
-    for lanes in blocks(width, spec.shape[2]):
-        wide = lanes.stop - lanes.start
-        window = jnp.concatenate(
-            [gated[:, lanes], jnp.zeros((WINDOW - rows, wide), BF16)], axis=0
+    groups = taps.shape[0]
+
+    @pl.when(pl.program_id(0) == 0)
+    def _():
+        mine = own_taps.shape[0]
+        share = groups // mine
+        for at, part in enumerate([own_taps] + more_taps):
+            place = lax.rem(me[0] + share - at, share) * mine
+            taps[pl.ds(pl.multiple_of(place, mine), mine)] = part[...].astype(BF16).astype(F32)
+        whole_taps = taps[...].astype(BF16)
+        both = jnp.concatenate([whole_taps, whole_taps], axis=1)
+        whole_spec = lax.dot_general(
+            half[...], both, (((1,), (1,)), ((), ())), preferred_element_type=F32
         )
+        real, imag = whole_spec[:BLOCK], whole_spec[BLOCK:]
+        first = lax.broadcasted_iota(jnp.int32, real.shape, 0) == 0
+        spec[0] = real
+        spec[1] = jnp.where(first, 0.0, imag)
+        spec[2] = jnp.where(first, imag, real)
+        spec_out[...] = spec[...]
+        rows_out[...] = taps[...].T[:HALO]
+
+    for lanes in blocks(width, groups):
+        pad = jnp.zeros((WINDOW - rows, groups), BF16)
+        window = jnp.concatenate([gated[:, lanes], pad], axis=0)
         prod = times(to_spectrum(whole[...], window), spec)
         sig = from_spectrum(high[: rest + HALO, :], *prod)
         put(yq, 0, rounded(g[:, lanes].astype(F32) * sig[:rest]), lanes.start)
@@ -203,7 +204,7 @@
 
 def third_kernel(
     me, k, v, tails, ends, ahead, gated, ggi, ks, vs, more, taps, w, spec, half, whole, low,
-    gk_out, gv_out, next_out, sums_out, send_out, own_out, *rest_refs,
+    gk_out, gv_out, next_out, sums_out, own_out, *rest_refs,
 ):
     *more_out, xe, xk, xv, yk, yv, acc, mscr = rest_refs
     rows, width = k.shape
@@ -279,7 +280,6 @@
             here = slice(h * LANES, (h + 1) * LANES)
             sums_out[:HALO, here] = lag_sums(yk, 0, xk, HALO, h, rows, count)
             sums_out[HALO:, here] = lag_sums(yv, 0, xv, HALO, h, rows, count)
-    send_out[...] = sums_out[...].astype(BF16)
 
     @pl.when(step == pl.num_programs(0) - 1)
     def _():
@@ -314,46 +314,51 @@
         gq_out[:, lanes] = jnp.concatenate([old[:, lanes], fixed], axis=0).astype(BF16)
 
 
-def fifth_kernel(
-    q, tails, following, sums, w, g, inner, behind, spec, half, high, gq_in, own, *refs,
-):
-    *parts, gq_out, sums_out, send_out, xq, yq = refs
-    width = q.shape[1]
+def pack_kernel(sums, own, *refs):
+    *parts, late_out, send_out = refs
     total = own[...]
     for part in parts:
         total = total + part[...].astype(F32)
-    count = total.shape[0] // (width // LANES)
-    for h, lanes in halves(width):
-        sums_out[HALO:, lanes] = total[h * count : (h + 1) * count]
+    spread = halves(sums.shape[1])
+    count = total.shape[0] // len(spread)
+    late_out[: 2 * HALO] = sums[...]
+    for h, lanes in spread:
+        late_out[2 * HALO :, lanes] = total[h * count : (h + 1) * count]
+    send_out[...] = late_out[...].astype(BF16)
+
+
+def fifth_kernel(
+    q, tails, sums, g, gated, behind, spec, whole, high,
+    yq_out, sums_out, send_out,
+    xq, yq,
+):
+    width = q.shape[1]
     put(xq, 0, tails[...].astype(F32)[:HALO])
     put(xq, HALO, q[...].astype(F32))
+    for lanes in blocks(width, spec.shape[2]):
+        window = jnp.concatenate([behind[:, lanes], gated[:, lanes]], axis=0)
+        sig = from_spectrum(high[...], *times(to_spectrum(whole[...], window), spec))
+        grad = (g[:, lanes].astype(F32) * sig).astype(BF16)
+        yq_out[:, lanes] = grad
+        put(yq, 0, grad.astype(F32), lanes.start)
+    for h, lanes in halves(width):
+        sums_out[:, lanes] = sums[:, lanes] + lag_sums(yq, 0, xq, HALO, h, BLOCK, sums.shape[0] - 1)
+    send_out[...] = sums_out[...].astype(BF16)
+
+
+def sixth_kernel(grad, following, w, gq_in, gq_out, yq):
+    put(yq, 0, grad[...].astype(F32))
     put(yq, BLOCK, following[...])
-    for lanes in blocks(width, spec.shape[2]):
-        edge = from_spectrum(high[...], *times(to_spectrum(half[...], behind[:, lanes]), spec))
-        put(yq, 0, rounded(g[:, lanes].astype(F32) * (inner[:, lanes] + edge)), lanes.start)
-    for h, lanes in halves(width):
+    for h, lanes in halves(grad.shape[1]):
         weights = taps_of(w, 0, lanes)
         for at, size in pieces(BLOCK):
             gq_out[at : at + size, lanes] = anticausal(yq, h, at, size, weights).astype(BF16)
-        sums_out[:HALO, lanes] = sums[:, lanes] + lag_sums(yq, 0, xq, HALO, h, BLOCK, w.shape[1])
-    send_out[...] = sums_out[...].astype(BF16)
 
 
 def shift(value, axis, steps):
     count = lax.axis_size(axis)
     initial, last = (max(0, -steps), min(count, count - steps))
     return lax.ppermute(value, axis, [(s, s + steps) for s in range(initial, last)])
-
-
-def gather_rows(value, axis):
-    count, rows = lax.axis_size(axis), value.shape[0]
-    me = lax.axis_index(axis)
-    result = jnp.zeros((count * rows, value.shape[1]), value.dtype)
-    result = lax.dynamic_update_slice(result, value, (me * rows, 0))
-    for step in range(1, count):
-        other = lax.ppermute(value, axis, [(s, (s + step) % count) for s in range(count)])
-        result = lax.dynamic_update_slice(result, other, ((me - step) % count * rows, 0))
-    return result
 
 
 def exchanged(sends, axis):
@@ -364,16 +369,31 @@
     ]
 
 
-def sum_over(value, sent, axis, reverse=False):
+def swap(value, axis, bit):
+    count = lax.axis_size(axis)
+    return lax.ppermute(value, axis, [(s, s ^ (1 << bit)) for s in range(count)])
+
+
+def sums_over(early, sent_early, late, sent_late, axis):
     count = lax.axis_size(axis)
     if count & (count - 1):
-        return lax.psum(value, axis)
-    steps = range(count.bit_length() - 1)
-    for bit in reversed(steps) if reverse else steps:
-        other = lax.ppermute(sent, axis, [(s, s ^ (1 << bit)) for s in range(count)])
-        value = value + other.astype(F32)
-        sent = value.astype(BF16)
-    return value
+        return lax.psum(early, axis), lax.psum(late, axis)
+    bits = count.bit_length() - 1
+    alone = 1 * bits // 4
+    for bit in range(bits - 1, bits - 1 - alone, -1):
+        early = early + swap(sent_early, axis, bit).astype(F32)
+        sent_early = early.astype(BF16)
+    total = jnp.concatenate([early, late], axis=0)
+    sent = jnp.concatenate([sent_early, sent_late], axis=0)
+    for bit in range(bits - alone):
+        total = total + swap(sent, axis, bit).astype(F32)
+        sent = total.astype(BF16)
+    early, late = total[: early.shape[0]], total[early.shape[0] :]
+    sent = late.astype(BF16)
+    for bit in range(bits - alone, bits):
+        late = late + swap(sent, axis, bit).astype(F32)
+        sent = late.astype(BF16)
+    return early, late
 
 
 def in_hbm(value):
@@ -390,9 +410,6 @@
 
     def col(count, at=0, wide=width):
         return pl.BlockSpec((count, wide), lambda i: (at, i))
-
-    def fixed(shape):
-        return pl.BlockSpec(shape, lambda i: (0,) * len(shape))
 
     def filters(wide=width):
         return pl.BlockSpec((3, taps_short, wide), lambda i: (0, 0, i))
@@ -414,7 +431,7 @@
     wide = min(4 * width, channels)
     pair = min(2 * width, channels)
     last = rows // (2 * HALO) - 1
-    tails, ahead = pl.pallas_call(
+    ends, ahead = pl.pallas_call(
         first_kernel,
         grid=(channels // wide,),
         in_specs=[col(BLOCK + 2 * HALO, 0, wide)] * 2
@@ -427,30 +444,26 @@
         name="first",
         compiler_params=room,
     )(query, grad_out, query, key, value, key, value, short_filter)
-    ends = tails
-    tails = shift(tails, "seq", 1)
+    tails = shift(ends, "seq", 1)
     ahead = shift(ahead, "seq", -1)
-    taps = gather_rows(medium_filter.astype(BF16), "fsdp")
-
-    gated, ggi, ks, vs, inner, behind, spec, tap_rows = pl.pallas_call(
+    share = lax.axis_size("fsdp")
+    taps = exchanged([medium_filter.astype(BF16)] * (share - 1), "fsdp")
+
+    gated, ggi, ks, vs, behind = pl.pallas_call(
         second_kernel,
         grid=(channels // wide,),
-        in_specs=[col(rows, 0, wide)] * 4
-        + [col(3 * HALO, 0, wide), filters(wide), fixed(taps.shape), fixed(half.shape), fixed(low.shape)],
-        out_specs=[col(rows, 0, wide)] * 4 + [col(BLOCK, 0, wide)] * 2 + [fixed((3, BLOCK, width)), fixed((HALO, width))],
+        in_specs=[col(rows, 0, wide)] * 4 + [col(3 * HALO, 0, wide), filters(wide)],
+        out_specs=[col(rows, 0, wide)] * 4 + [col(BLOCK, 0, wide)],
         out_shape=[
-            out(rows, BF16), out(rows, BF16), out(rows, F32), out(rows, F32),
-            out(BLOCK, F32), out(BLOCK, BF16), jax.ShapeDtypeStruct((3, BLOCK, width), F32),
-            jax.ShapeDtypeStruct((HALO, width), F32),
+            out(rows, BF16), out(rows, BF16), out(rows, F32), out(rows, F32), out(BLOCK, BF16),
         ],
-        scratch_shapes=[scratch(rows + HALO, wide)] * 3 + [pltpu.VMEM((3, BLOCK, width), F32)],
+        scratch_shapes=[scratch(rows + HALO, wide)] * 3,
         cost_estimate=cost(4e9, 20e6),
         name="second",
         compiler_params=room,
-    )(query, key, value, grad_out, tails, short_filter, taps, half, low)
+    )(query, key, value, grad_out, tails, short_filter)
     behind = shift(behind, "seq", 1)
 
-    share = lax.axis_size("fsdp")
     me = lax.axis_index("fsdp").astype(jnp.int32).reshape(1)
     many = channels // wide
 
@@ -467,21 +480,30 @@
     big_filters = pl.BlockSpec((3, taps_short, wide), lambda i, *_: (0, 0, i))
     corner = BLOCK // rest
     edge_block = rows // (2 * HALO) - 1
-    grad_query, nexts, sums_q, more = pl.pallas_call(
+    grad_query, nexts, sums_q, more, spec, tap_rows = pl.pallas_call(
         middle_kernel,
-        grid=(many,),
-        in_specs=[big(rows), big(rest, corner), big(rows), big_filters]
-        + [still((3, BLOCK, width)), still(whole.shape), still(high.shape)],
-        out_specs=[big(rest, corner), big(2 * HALO), big(HALO), big(HALO)],
-        out_shape=[out(rows, BF16), out(2 * HALO, F32), out(HALO, F32), out(HALO, F32)],
-        scratch_shapes=[scratch(rest + 2 * HALO, wide)] * 2,
-        cost_estimate=cost(2e9, 8e6),
+        grid_spec=pltpu.PrefetchScalarGridSpec(
+            num_scalar_prefetch=1,
+            grid=(many,),
+            in_specs=[big(rows), big(rest, corner), big(rows), big_filters]
+            + [still(m.shape) for m in (half, whole, high)]
+            + [still(medium_filter.shape)] * share,
+            out_specs=[big(rest, corner), big(2 * HALO), big(HALO), big(HALO)]
+            + [still((3, BLOCK, width)), still((HALO, width))],
+            scratch_shapes=[scratch(rest + 2 * HALO, wide)] * 2
+            + [pltpu.VMEM((3, BLOCK, width), F32), pltpu.VMEM((width, BLOCK), F32)],
+        ),
+        out_shape=[
+            out(rows, BF16), out(2 * HALO, F32), out(HALO, F32), out(HALO, F32),
+            jax.ShapeDtypeStruct((3, BLOCK, width), F32), jax.ShapeDtypeStruct((HALO, width), F32),
+        ],
+        cost_estimate=cost(4e9, 8e6),
         name="middle",
         compiler_params=room,
-    )(query, grad_out, gated, short_filter, spec, whole, high)
+    )(me, query, grad_out, gated, short_filter, half, whole, high, medium_filter, *taps)
 
     mine = (width // share, BLOCK)
-    gk, gv, far, sums_kv, sent_kv, own, *sends = pl.pallas_call(
+    gk, gv, far, sums_kv, own, *sends = pl.pallas_call(
         third_kernel,
         grid_spec=pltpu.PrefetchScalarGridSpec(
             num_scalar_prefetch=1,
@@ -494,14 +516,14 @@
             + [still(m.shape) for m in (half, whole, low)],
             out_specs=[two(rows + 2 * HALO)] * 2
             + [two(HALO)]
-            + [two(2 * HALO)] * 2
+            + [two(2 * HALO)]
             + [still(mine)] * share,
             scratch_shapes=[pltpu.VMEM((3, pair // LANES, 3 * HALO, LANES), F32)]
             + [scratch(rows + 2 * HALO, pair)] * 4
             + [pltpu.VMEM((3, BLOCK, width), F32), pltpu.VMEM((width, BLOCK), F32)],
         ),
         out_shape=[out(rows + 2 * HALO, BF16)] * 2
-        + [out(HALO, F32), out(2 * HALO, F32), out(2 * HALO, BF16)]
+        + [out(HALO, F32), out(2 * HALO, F32)]
         + [jax.ShapeDtypeStruct(mine, F32)]
         + [jax.ShapeDtypeStruct(mine, BF16)] * (share - 1),
         cost_estimate=cost(8e9, 20e6),
@@ -526,27 +548,43 @@
     )(gk, gv, nexts, far, short_filter, grad_query)
 
     extra = mine[0] * BLOCK // channels
-    grad_query, sums_q, sent_q = pl.pallas_call(
+    tall = (2 * HALO + extra, channels)
+    sums_kv, sent_kv = pl.pallas_call(
+        pack_kernel,
+        out_shape=[jax.ShapeDtypeStruct(tall, F32), jax.ShapeDtypeStruct(tall, BF16)],
+        name="pack",
+        compiler_params=room,
+    )(sums_kv, own, *parts)
+
+    grads, sums_q, sent_q = pl.pallas_call(
         fifth_kernel,
         grid=(many,),
-        in_specs=[big(BLOCK), big(3 * HALO), big(HALO), big(HALO), big_filters]
+        in_specs=[big(BLOCK), big(3 * HALO), big(HALO)]
         + [big(BLOCK)] * 3
-        + [still((3, BLOCK, width)), still(half.shape), still(high.shape)]
-        + [pl.BlockSpec(memory_space=pl.ANY)]
-        + [pl.BlockSpec((mine[0] * wide // channels, BLOCK), lambda i: (i, 0))] * share,
-        out_specs=[big(BLOCK), big(HALO + extra), big(HALO + extra)],
-        out_shape=[out(rows, BF16), out(HALO + extra, F32), out(HALO + extra, BF16)],
+        + [still((3, BLOCK, width)), still(whole.shape), still(high.shape)],
+        out_specs=[big(BLOCK), big(HALO), big(HALO)],
+        out_shape=[out(BLOCK, BF16), out(HALO, F32), out(HALO, BF16)],
         scratch_shapes=[scratch(BLOCK + HALO, wide)] * 2,
-        input_output_aliases={11: 0},
         cost_estimate=cost(2e9, 8e6),
         name="fifth",
         compiler_params=room,
-    )(query, tails, nexts, sums_q, short_filter, grad_out, inner, behind, spec, half, high,
-      grad_query, own, *parts)
-
-    early = sum_over(sums_kv, sent_kv, "seq", reverse=True)
-    late = sum_over(sums_q, sent_q, "seq")
-    packed = late[HALO:]
+    )(query, tails, sums_q, grad_out, gated, behind, spec, whole, high)
+
+    grad_query = pl.pallas_call(
+        sixth_kernel,
+        grid=(many,),
+        in_specs=[big(BLOCK), big(HALO), big_filters, pl.BlockSpec(memory_space=pl.ANY)],
+        out_specs=big(BLOCK),
+        out_shape=out(rows, BF16),
+        scratch_shapes=[scratch(BLOCK + HALO, wide)],
+        input_output_aliases={3: 0},
+        cost_estimate=cost(2e9, 3e6),
+        name="sixth",
+        compiler_params=room,
+    )(grads, nexts, short_filter, grad_query)
+
+    early, late = sums_over(sums_kv, sent_kv, sums_q, sent_q, "seq")
+    packed = early[2 * HALO :]
     grad_medium = jnp.concatenate(
         [packed[:, at : at + BLOCK] for at in range(0, channels, BLOCK)], axis=0
     )

time: 77 us -> 76.6 us (level)
  waiting for transfers between devices: 13.8 us -> 12.7 us
  Pallas kernels: 29.1 us -> 30.2 us
  other arithmetic: 1.79 us -> 0.88 us
    ppermute x9 -> x5, waiting for transfers between devices: 11.1 us -> 7.54 us  [swap(): return lax.ppermute(value, axis, [(s, s ^ 1 << bit) for s in range(count)])]
    pallas_call x1 -> x3, Pallas kernels: 5.03 us -> 7.58 us  [the longest x1 5.36 us: shards(): pl.pallas_call(middle_kernel, grid_spec=pltpu.PrefetchScalarGridSpec(num_...]
    pallas_call x1, Pallas kernels: 5.99 us -> 4.5 us  [shards(): pl.pallas_call(second_kernel, grid=(channels // wide,), in_specs=[col(row...]
    ppermute x3, waiting for transfers between devices: 2.69 us -> 3.97 us  [shift(): lax.ppermute(value, axis, [(s, s + steps) for s in range(initial, last)])]
    ppermute x1 -> x2, waiting for transfers between devices: 0.01 us -> 1.2 us  [exchanged(): lax.ppermute(part, axis, [(s, (s + step) % count) for s in range(count)])]
    dynamic_update_slice x1 -> x0, other arithmetic: 0.87 us -> none  [gather_rows(): result = lax.dynamic_update_slice(result, value, (me * rows, 0))]
    ppermute x9 -> x5, starting transfers between devices: 20.7 us -> 20.9 us  [swap(): return lax.ppermute(value, axis, [(s, s ^ 1 << bit) for s in range(count)])]
  transfers between devices with their start and end apart: 13 -> 10, of which waited for: 7 -> 7; matrix products, arithmetic and copies ran while one was open for 0% -> 0% of each run, Pallas kernels for 38% -> 37%
where the time goes in v5:
time: 76.6 us; the launch traced here: 76.3 us
  starting transfers between devices  31.5 us (41%)
  Pallas kernels  30.2 us (39%)
  waiting for transfers between devices  12.7 us (17%)
  between operations  0.91 us (1%)
  other arithmetic  0.88 us (1%)
    ppermute x5, starting transfers between devices, swap(): return lax.ppermute(value, axis, [(s, s ^ 1 << bit) for s in range(count)])  20.9 us
    ppermute x3, starting transfers between devices, shift(): lax.ppermute(value, axis, [(s, s + steps) for s in range(initial, last)])  10.5 us
    pallas_call x1, Pallas kernels, shards(): pl.pallas_call(third_kernel, grid_spec=pltpu.PrefetchScalarGridSpec(num_s...  8.27 us
    ppermute x5, waiting for transfers between devices, swap(): return lax.ppermute(value, axis, [(s, s ^ 1 << bit) for s in range(count)])  7.54 us
    pallas_call x1, Pallas kernels, shards(): pl.pallas_call(middle_kernel, grid_spec=pltpu.PrefetchScalarGridSpec(num_...  5.36 us
    pallas_call x1, Pallas kernels, shards(): pl.pallas_call(second_kernel, grid=(channels // wide,), in_specs=[col(row...  4.5 us
    pallas_call x1, Pallas kernels, shards(): pl.pallas_call(fifth_kernel, grid=(many,), in_specs=[big(BLOCK), big(3 *...  4.41 us
    ppermute x3, waiting for transfers between devices, shift(): lax.ppermute(value, axis, [(s, s + steps) for s in range(initial, last)])  3.97 us
  transfers between devices with their start and end apart: 10, of which 7 were waited for; matrix products, arithmetic and copies ran while one was open for 0% of the time, Pallas kernels for 37%

profile of v5, /device:TPU:0, one launch (start us, length us, event | category | flops | bytes accessed | tf_op | source)
XLA Modules:
  0.0 76.3 jit_solution(9393851332167682477)
XLA Ops:
  0.6 0.0 copy-start
  0.6 2.0 %first.1 = (bf16[24,2048]{1,0:T(8,128)(2,1)S(1)}, bf16[160,2048]{1,0:T(8,128)(2,1)S(1)}) custom-call(bf16[192,2048]{1,0:T(8,128)(2,1)} %q.7, bf16[192,2048]{1,0:T(8,128)(2,1)} %g.7, bf16[192,2048]{1,0:T(8,128)(2,1)} %q.7, bf16[192,2048]{1,0:T(8,128)(2,1)} %k.3, bf16[192,2048]{1,0:T(8,128)(2,1)} %v.3, bf16[192,2048]{1,0:T(8,128)(2,1)} %k.3, ...), custom_call_target="tpu_custom_call" | custom-call | tf_op jit(solution)/shard_map/first/pallas_call | solution.py:434
  2.6 4.9 %collective-permute-start = (bf16[24,2048]{1,0:T(8,128)(2,1)S(1)}, bf16[24,2048]{1,0:T(8,128)(2,1)S(1)}, u32[]{:S(2)}, u32[]{:S(2)}) collective-permute-start(bf16[24,2048]{1,0:T(8,128)(2,1)S(1)} %get-tuple-element.32.ends), channel_id=1, source_target_pairs={{0,2},{2,4},{4,6},{6,8},{8,10},{10,12},{12,14},{14,16},{16,18},{18... | collective-permute-start | bytes 294920 | tf_op jit(solution)/shard_map/ppermute | solution.py:361
  7.5 0.0 copy-done
  7.5 0.1 collective-permute-start.1
  7.6 1.3 %collective-permute-start.3 = (bf16[160,2048]{1,0:T(8,128)(2,1)S(1)}, bf16[160,2048]{1,0:T(8,128)(2,1)S(1)}, u32[]{:S(2)}, u32[]{:S(2)}) collective-permute-start(bf16[160,2048]{1,0:T(8,128)(2,1)S(1)} %get-tuple-element.39), channel_id=1, source_target_pairs={{2,0},{4,2},{6,4},{8,6},{10,8},{12,10},{14,12},{16,14},{18,16},{20... | collective-permute-start | bytes 1966088 | tf_op jit(solution)/shard_map/ppermute | solution.py:361
  8.9 0.8 %collective-permute-done.tails = bf16[24,2048]{1,0:T(8,128)(2,1)S(1)} collective-permute-done((bf16[24,2048]{1,0:T(8,128)(2,1)S(1)}, bf16[24,2048]{1,0:T(8,128)(2,1)S(1)}, u32[]{:S(2)}, u32[]{:S(2)}) %collective-permute-start) | collective-permute-done | bytes 98336 | tf_op jit(solution)/shard_map/ppermute | solution.py:361
  9.7 4.5 %second.1 = (bf16[192,2048]{1,0:T(8,128)(2,1)S(1)}, bf16[192,2048]{1,0:T(8,128)(2,1)S(1)}, f32[192,2048]{1,0:T(8,128)S(1)}, f32[192,2048]{1,0:T(8,128)S(1)}, bf16[128,2048]{1,0:T(8,128)(2,1)S(1)}) custom-call(bf16[192,2048]{1,0:T(8,128)(2,1)} %q.7, bf16[192,2048]{1,0:T(8,128)(2,1)} %k.3, bf16[192,2048]{1,0:T(8,128)(2,1)} %v.3, bf16[192,2048]{1,0:T(8,128)(2,1)} %g.7, ...), custom_call_target="tpu_custom_call" | custom-call | flops 4000000000 | bytes 20000000 | tf_op jit(solution)/shard_map/second/pallas_call | solution.py:452
  14.2 4.3 %collective-permute-start.2 = (bf16[128,2048]{1,0:T(8,128)(2,1)S(1)}, bf16[128,2048]{1,0:T(8,128)(2,1)S(1)}, u32[]{:S(2)}, u32[]{:S(2)}) collective-permute-start(bf16[128,2048]{1,0:T(8,128)(2,1)S(1)} %get-tuple-element.35), channel_id=1, source_target_pairs={{0,2},{2,4},{4,6},{6,8},{8,10},{10,12},{12,14},{14,16},{16,18},{18... | collective-permute-start | bytes 1572872 | tf_op jit(solution)/shard_map/ppermute | solution.py:361
  18.6 0.0 collective-permute-done.1.refs_0_
  18.6 5.4 %middle.1 = (bf16[192,2048]{1,0:T(8,128)(2,1)}, f32[16,2048]{1,0:T(8,128)S(1)}, f32[8,2048]{1,0:T(8,128)S(1)}, f32[8,2048]{1,0:T(8,128)S(1)}, f32[3,128,256]{2,1,0:T(8,128)S(1)}, /*index=5*/f32[8,256]{1,0:T(8,128)S(1)}) custom-call(s32[1]{0:T(128)} %bitcast.me, bf16[192,2048]{1,0:T(8,128)(2,1)} %q.7, bf16[192,2048]{1,0:T(8,128)(2,1)} %g.7, ...), custom_call_target="tpu_custom_call" | custom-call | flops 4000000000 | bytes 8000000 | tf_op jit(solution)/shard_map/middle/pallas_call | solution.py:483
  23.9 3.2 %collective-permute-done.3.ahead = bf16[160,2048]{1,0:T(8,128)(2,1)S(1)} collective-permute-done((bf16[160,2048]{1,0:T(8,128)(2,1)S(1)}, bf16[160,2048]{1,0:T(8,128)(2,1)S(1)}, u32[]{:S(2)}, u32[]{:S(2)}) %collective-permute-start.3) | collective-permute-done | bytes 655392 | tf_op jit(solution)/shard_map/ppermute | solution.py:361
  27.1 8.3 %third.1 = (bf16[208,2048]{1,0:T(8,128)(2,1)S(1)}, bf16[208,2048]{1,0:T(8,128)(2,1)S(1)}, f32[8,2048]{1,0:T(8,128)S(1)}, f32[16,2048]{1,0:T(8,128)S(1)}, f32[128...) custom-call(s32[1]{0:T(128)} %bitcast.me, bf16[192,2048]{1,0:T(8,128)(2,1)} %k.3, bf16[192,2048]{1,0:T(8,128)(2,1)} %v.3, ...), custom_call_target="tpu_custom_call" | custom-call | flops 8000000000 | bytes 20000000 | tf_op jit(solution)/shard_map/third/pallas_call | solution.py:506
  35.4 0.1 collective-permute-start.4
  35.5 1.2 %collective-permute-done.4.refs_0_ = bf16[128,128]{1,0:T(8,128)(2,1)S(1)} collective-permute-done((bf16[128,128]{1,0:T(8,128)(2,1)S(1)}, bf16[128,128]{1,0:T(8,128)(2,1)S(1)}, u32[]{:S(2)}, u32[]{:S(2)}) %collective-permute-start.4) | collective-permute-done | bytes 32800 | tf_op jit(solution)/shard_map/ppermute | solution.py:367
  36.7 2.7 %collective-permute-start.5 = (bf16[24,2048]{1,0:T(8,128)(2,1)S(1)}, bf16[24,2048]{1,0:T(8,128)(2,1)S(1)}, u32[]{:S(2)}, u32[]{:S(2)}) collective-permute-start(bf16[24,2048]{1,0:T(8,128)(2,1)S(1)} %get-tuple-element.56), channel_id=1, source_target_pairs={{0,16},{2,18},{4,20},{6,22},{8,24},{10,26},{12,28},{14,30},{16,0},... | collective-permute-start | bytes 294920 | tf_op jit(solution)/shard_map/ppermute | solution.py:374
  39.4 0.0 collective-permute-done.2.behind
  39.4 4.4 %fifth.1 = (bf16[128,2048]{1,0:T(8,128)(2,1)S(1)}, f32[8,2048]{1,0:T(8,128)S(1)}, bf16[8,2048]{1,0:T(8,128)(2,1)S(1)}) custom-call(bf16[192,2048]{1,0:T(8,128)(2,1)} %q.7, bf16[24,2048]{1,0:T(8,128)(2,1)S(1)} %collective-permute-done.tails, f32[8,2048]{1,0:T(8,128)S(1)} %get-tuple-element.34.sums, bf16[192,2048]{1,0:T(8,128)(2,1)} %g.7, ...), custom_call_target="tpu_custom_call" | custom-call | flops 2000000000 | bytes 8000000 | tf_op jit(solution)/shard_map/fifth/pallas_call | solution.py:559
  43.8 0.9 %collective-permute-done.5 = bf16[24,2048]{1,0:T(8,128)(2,1)S(1)} collective-permute-done((bf16[24,2048]{1,0:T(8,128)(2,1)S(1)}, bf16[24,2048]{1,0:T(8,128)(2,1)S(1)}, u32[]{:S(2)}, u32[]{:S(2)}) %collective-permute-start.5) | collective-permute-done | bytes 98336 | tf_op jit(solution)/shard_map/ppermute | solution.py:374
  44.7 2.5 %collective-permute-start.6 = (bf16[32,2048]{1,0:T(8,128)(2,1)S(1)}, bf16[32,2048]{1,0:T(8,128)(2,1)S(1)}, u32[]{:S(2)}, u32[]{:S(2)}) collective-permute-start(bf16[32,2048]{1,0:T(8,128)(2,1)S(1)} %pad_maximum_fusion.1), channel_id=1, source_target_pairs={{0,2},{2,0},{4,6},{6,4},{8,10},{10,8},{12,14},{14,12},{16,18},{18,... | collective-permute-start | bytes 393224 | tf_op jit(solution)/shard_map/ppermute | solution.py:374
  47.1 3.0 %collective-permute-done.6 = bf16[32,2048]{1,0:T(8,128)(2,1)S(1)} collective-permute-done((bf16[32,2048]{1,0:T(8,128)(2,1)S(1)}, bf16[32,2048]{1,0:T(8,128)(2,1)S(1)}, u32[]{:S(2)}, u32[]{:S(2)}) %collective-permute-start.6) | collective-permute-done | bytes 131104 | tf_op jit(solution)/shard_map/ppermute | solution.py:374
  50.1 11.9 %collective-permute-start.7 = (bf16[32,2048]{1,0:T(8,128)(2,1)S(1)}, bf16[32,2048]{1,0:T(8,128)(2,1)S(1)}, u32[]{:S(2)}, u32[]{:S(2)}) collective-permute-start(bf16[32,2048]{1,0:T(8,128)(2,1)S(1)} %fusion.2), channel_id=1, source_target_pairs={{0,4},{2,6},{4,0},{6,2},{8,12},{10,14},{12,8},{14,10},{16,20},{18,... | collective-permute-start | bytes 393224 | tf_op jit(solution)/shard_map/ppermute | solution.py:374
  62.1 3.5 %fourth.1 = (bf16[192,2048]{1,0:T(8,128)(2,1)}, bf16[192,2048]{1,0:T(8,128)(2,1)}, bf16[192,2048]{1,0:T(8,128)(2,1)}) custom-call(bf16[208,2048]{1,0:T(8,128)(2,1)S(1)} %get-tuple-element.45.gk, bf16[208,2048]{1,0:T(8,128)(2,1)S(1)} %get-tuple-element.46.gv, f32[16,2048]{1,0:T(8,128)S(1)} %get-tuple-element.38.near.following, ...), custom_call_target="tpu_custom_call", output_to_operand_aliasing={{2}: (5, {})} | custom-call | flops 4000000000 | bytes 10000000 | tf_op jit(solution)/shard_map/fourth/pallas_call | solution.py:536
  65.5 0.0 collective-permute-done.7
  65.6 1.2 %collective-permute-start.8 = (bf16[32,2048]{1,0:T(8,128)(2,1)S(1)}, bf16[32,2048]{1,0:T(8,128)(2,1)S(1)}, u32[]{:S(2)}, u32[]{:S(2)}) collective-permute-start(bf16[32,2048]{1,0:T(8,128)(2,1)S(1)} %fusion), channel_id=1, source_target_pairs={{0,8},{2,10},{4,12},{6,14},{8,0},{10,2},{12,4},{14,6},{16,24},{18,... | collective-permute-start | bytes 393224 | tf_op jit(solution)/shard_map/ppermute | solution.py:374
  66.8 2.2 %sixth.1 = bf16[192,2048]{1,0:T(8,128)(2,1)} custom-call(bf16[128,2048]{1,0:T(8,128)(2,1)S(1)} %get-tuple-element.37.grad, f32[16,2048]{1,0:T(8,128)S(1)} %get-tuple-element.38.near.following, f32[3,7,2048]{2,1,0:T(8,128)} %w.11, bf16[192,2048]{1,0:T(8,128)(2,1)} %get-tuple-element.49.gq_in), custom_call_target="tpu_custom_call", output_to_operand_aliasing={{}: (3, {})} | custom-call | flops 2000000000 | bytes 3000000 | tf_op jit(solution)/shard_map/sixth/pallas_call | solution.py:573
  69.0 1.6 %collective-permute-done.8 = bf16[32,2048]{1,0:T(8,128)(2,1)S(1)} collective-permute-done((bf16[32,2048]{1,0:T(8,128)(2,1)S(1)}, bf16[32,2048]{1,0:T(8,128)(2,1)S(1)}, u32[]{:S(2)}, u32[]{:S(2)}) %collective-permute-start.8) | collective-permute-done | bytes 131104 | tf_op jit(solution)/shard_map/ppermute | solution.py:374
  70.6 0.1 convert_add_fusion
  70.7 2.6 %collective-permute-start.9 = (bf16[8,2048]{1,0:T(8,128)(2,1)S(1)}, bf16[8,2048]{1,0:T(8,128)(2,1)S(1)}, u32[]{:S(2)}, u32[]{:S(2)}) collective-permute-start(bf16[8,2048]{1,0:T(8,128)(2,1)S(1)} %slice.145), channel_id=1, source_target_pairs={{0,16},{2,18},{4,20},{6,22},{8,24},{10,26},{12,28},{14,30},{16,0},... | collective-permute-start | bytes 98312 | tf_op jit(solution)/shard_map/ppermute | solution.py:374
  73.4 0.0 copy-start.1
  73.5 2.1 %collective-permute-done.9 = bf16[8,2048]{1,0:T(8,128)(2,1)S(1)} collective-permute-done((bf16[8,2048]{1,0:T(8,128)(2,1)S(1)}, bf16[8,2048]{1,0:T(8,128)(2,1)S(1)}, u32[]{:S(2)}, u32[]{:S(2)}) %collective-permute-start.9) | collective-permute-done | bytes 32800 | tf_op jit(solution)/shard_map/ppermute | solution.py:374
  75.6 0.7 pad_maximum_fusion
  (27 shorter events, 0.2 us)
Async XLA Ops:
  0.6 6.9 %copy-start = (f32[128,128]{1,0:T(8,128)S(1)}, f32[128,128]{1,0:T(8,128)}, u32[]{:S(2)}) copy-start(f32[128,128]{1,0:T(8,128)} %own_taps.1) | copy-start | bytes 196612
  2.6 7.1 %collective-permute-start = (bf16[24,2048]{1,0:T(8,128)(2,1)S(1)}, bf16[24,2048]{1,0:T(8,128)(2,1)S(1)}, u32[]{:S(2)}, u32[]{:S(2)}) collective-permute-start(bf16[24,2048]{1,0:T(8,128)(2,1)S(1)} %get-tuple-element.32.ends), channel_id=1, source_target_pairs={{0,2},{2,4},{4,6},{6,8},{8,10},{10,12},{12,14},{14,16},{16,18},{18... | collective-permute-start | bytes 294920 | tf_op jit(solution)/shard_map/ppermute | solution.py:361
  7.5 11.0 %collective-permute-start.1 = (bf16[128,128]{1,0:T(8,128)(2,1)S(1)}, bf16[128,128]{1,0:T(8,128)(2,1)S(1)}, u32[]{:S(2)}, u32[]{:S(2)}) collective-permute-start(bf16[128,128]{1,0:T(8,128)(2,1)S(1)} %convert_element_type.30), channel_id=1, source_target_pairs={{0,1},{1,0},{2,3},{3,2},{4,5},{5,4},{6,7},{7,6},{8,9},{9,8},{10,11... | collective-permute-start | bytes 98312 | tf_op jit(solution)/shard_map/ppermute | solution.py:367
  7.6 19.5 %collective-permute-start.3 = (bf16[160,2048]{1,0:T(8,128)(2,1)S(1)}, bf16[160,2048]{1,0:T(8,128)(2,1)S(1)}, u32[]{:S(2)}, u32[]{:S(2)}) collective-permute-start(bf16[160,2048]{1,0:T(8,128)(2,1)S(1)} %get-tuple-element.39), channel_id=1, source_target_pairs={{2,0},{4,2},{6,4},{8,6},{10,8},{12,10},{14,12},{16,14},{18,16},{20... | collective-permute-start | bytes 1966088 | tf_op jit(solution)/shard_map/ppermute | solution.py:361
  14.2 25.1 %collective-permute-start.2 = (bf16[128,2048]{1,0:T(8,128)(2,1)S(1)}, bf16[128,2048]{1,0:T(8,128)(2,1)S(1)}, u32[]{:S(2)}, u32[]{:S(2)}) collective-permute-start(bf16[128,2048]{1,0:T(8,128)(2,1)S(1)} %get-tuple-element.35), channel_id=1, source_target_pairs={{0,2},{2,4},{4,6},{6,8},{8,10},{10,12},{12,14},{14,16},{16,18},{18... | collective-permute-start | bytes 1572872 | tf_op jit(solution)/shard_map/ppermute | solution.py:361
  35.4 1.3 %collective-permute-start.4 = (bf16[128,128]{1,0:T(8,128)(2,1)S(1)}, bf16[128,128]{1,0:T(8,128)(2,1)S(1)}, u32[]{:S(2)}, u32[]{:S(2)}) collective-permute-start(bf16[128,128]{1,0:T(8,128)(2,1)S(1)} %get-tuple-element.54), channel_id=1, source_target_pairs={{0,1},{1,0},{2,3},{3,2},{4,5},{5,4},{6,7},{7,6},{8,9},{9,8},{10,11... | collective-permute-start | bytes 98312 | tf_op jit(solution)/shard_map/ppermute | solution.py:367
  36.7 7.9 %collective-permute-start.5 = (bf16[24,2048]{1,0:T(8,128)(2,1)S(1)}, bf16[24,2048]{1,0:T(8,128)(2,1)S(1)}, u32[]{:S(2)}, u32[]{:S(2)}) collective-permute-start(bf16[24,2048]{1,0:T(8,128)(2,1)S(1)} %get-tuple-element.56), channel_id=1, source_target_pairs={{0,16},{2,18},{4,20},{6,22},{8,24},{10,26},{12,28},{14,30},{16,0},... | collective-permute-start | bytes 294920 | tf_op jit(solution)/shard_map/ppermute | solution.py:374
  44.7 5.4 %collective-permute-start.6 = (bf16[32,2048]{1,0:T(8,128)(2,1)S(1)}, bf16[32,2048]{1,0:T(8,128)(2,1)S(1)}, u32[]{:S(2)}, u32[]{:S(2)}) collective-permute-start(bf16[32,2048]{1,0:T(8,128)(2,1)S(1)} %pad_maximum_fusion.1), channel_id=1, source_target_pairs={{0,2},{2,0},{4,6},{6,4},{8,10},{10,8},{12,14},{14,12},{16,18},{18,... | collective-permute-start | bytes 393224 | tf_op jit(solution)/shard_map/ppermute | solution.py:374
  50.1 15.4 %collective-permute-start.7 = (bf16[32,2048]{1,0:T(8,128)(2,1)S(1)}, bf16[32,2048]{1,0:T(8,128)(2,1)S(1)}, u32[]{:S(2)}, u32[]{:S(2)}) collective-permute-start(bf16[32,2048]{1,0:T(8,128)(2,1)S(1)} %fusion.2), channel_id=1, source_target_pairs={{0,4},{2,6},{4,0},{6,2},{8,12},{10,14},{12,8},{14,10},{16,20},{18,... | collective-permute-start | bytes 393224 | tf_op jit(solution)/shard_map/ppermute | solution.py:374
  65.6 5.0 %collective-permute-start.8 = (bf16[32,2048]{1,0:T(8,128)(2,1)S(1)}, bf16[32,2048]{1,0:T(8,128)(2,1)S(1)}, u32[]{:S(2)}, u32[]{:S(2)}) collective-permute-start(bf16[32,2048]{1,0:T(8,128)(2,1)S(1)} %fusion), channel_id=1, source_target_pairs={{0,8},{2,10},{4,12},{6,14},{8,0},{10,2},{12,4},{14,6},{16,24},{18,... | collective-permute-start | bytes 393224 | tf_op jit(solution)/shard_map/ppermute | solution.py:374
  70.7 4.9 %collective-permute-start.9 = (bf16[8,2048]{1,0:T(8,128)(2,1)S(1)}, bf16[8,2048]{1,0:T(8,128)(2,1)S(1)}, u32[]{:S(2)}, u32[]{:S(2)}) collective-permute-start(bf16[8,2048]{1,0:T(8,128)(2,1)S(1)} %slice.145), channel_id=1, source_target_pairs={{0,16},{2,18},{4,20},{6,22},{8,24},{10,26},{12,28},{14,30},{16,0},... | collective-permute-start | bytes 98312 | tf_op jit(solution)/shard_map/ppermute | solution.py:374
  73.4 2.9 %copy-start.1 = (f32[128,128]{1,0:T(8,128)}, f32[128,128]{1,0:T(8,128)S(1)}, u32[]{:S(2)}) copy-start(f32[128,128]{1,0:T(8,128)S(1)} %constant_dynamic-update-slice_fusion) | copy-start | bytes 196612

commit v6 on v5

--- a/solution.py
+++ b/solution.py
@@ -71,7 +71,7 @@
 
 
 LANES = 128
-ROOM = 40 * 1024 * 1024
+ROOM = 20 * 1024 * 1024
 CHUNK = 64
 
 
@@ -161,7 +161,7 @@
     behind_out[...] = gated_out[rows - BLOCK :, :]
 
 
-def middle_kernel(me, q, g, gated, w, half, whole, high, own_taps, *refs):
+def middle_kernel(me, _, q, g, gated, w, half, whole, high, own_taps, *refs):
     *more_taps, gq_out, next_out, sums_out, more_out, spec_out, rows_out, xq, yq, spec, taps = refs
     rows, width = gated.shape
     rest = rows - BLOCK
@@ -172,8 +172,8 @@
         mine = own_taps.shape[0]
         share = groups // mine
         for at, part in enumerate([own_taps] + more_taps):
-            place = lax.rem(me[0] + share - at, share) * mine
-            taps[pl.ds(pl.multiple_of(place, mine), mine)] = part[...].astype(BF16).astype(F32)
+            start = lax.rem(me[0] + share - at, share) * mine
+            taps[pl.ds(pl.multiple_of(start, mine), mine)] = part[...].astype(BF16).astype(F32)
         whole_taps = taps[...].astype(BF16)
         both = jnp.concatenate([whole_taps, whole_taps], axis=1)
         whole_spec = lax.dot_general(
@@ -314,21 +314,25 @@
         gq_out[:, lanes] = jnp.concatenate([old[:, lanes], fixed], axis=0).astype(BF16)
 
 
-def pack_kernel(sums, own, *refs):
-    *parts, late_out, send_out = refs
+def pack_kernel(place, sums, own, *refs):
+    *parts, keep_out, send_out, both = refs
     total = own[...]
     for part in parts:
         total = total + part[...].astype(F32)
     spread = halves(sums.shape[1])
     count = total.shape[0] // len(spread)
-    late_out[: 2 * HALO] = sums[...]
+    both[: 2 * HALO] = sums[...]
     for h, lanes in spread:
-        late_out[2 * HALO :, lanes] = total[h * count : (h + 1) * count]
-    send_out[...] = late_out[...].astype(BF16)
+        both[2 * HALO :, lanes] = total[h * count : (h + 1) * count]
+    middle = sums.shape[1] // 2
+    left, right = both[:, :middle], both[:, middle:]
+    lower = lax.rem(place[0], 2) == 0
+    keep_out[...] = jnp.where(lower, left, right)
+    send_out[...] = jnp.where(lower, right, left).astype(BF16)
 
 
 def fifth_kernel(
-    q, tails, sums, g, gated, behind, spec, whole, high,
+    q, tails, sums, g, gated, behind, spec, lead, back,
     yq_out, sums_out, send_out,
     xq, yq,
 ):
@@ -337,7 +341,8 @@
     put(xq, HALO, q[...].astype(F32))
     for lanes in blocks(width, spec.shape[2]):
         window = jnp.concatenate([behind[:, lanes], gated[:, lanes]], axis=0)
-        sig = from_spectrum(high[...], *times(to_spectrum(whole[...], window), spec))
+        prod = jnp.concatenate(times(dot(lead[...], window), spec), axis=0)
+        sig = dot(back[...], prod.astype(BF16))
         grad = (g[:, lanes].astype(F32) * sig).astype(BF16)
         yq_out[:, lanes] = grad
         put(yq, 0, grad.astype(F32), lanes.start)
@@ -355,6 +360,29 @@
             gq_out[at : at + size, lanes] = anticausal(yq, h, at, size, weights).astype(BF16)
 
 
+def last_kernel(place, total, other, short_out, medium_out):
+    lower = lax.rem(place[0], 2) == 0
+    middle = total.shape[1]
+    taps = short_out.shape[1]
+    rows = total.shape[0] - 2 * HALO
+    mine, theirs = total[...], other[...].astype(F32)
+    late = mine[rows:] + theirs[rows:]
+    sides = (
+        jnp.where(lower, mine[:rows], theirs[:rows]),
+        jnp.where(lower, theirs[:rows], mine[:rows]),
+    )
+    for at, part in enumerate(sides):
+        here = slice(at * middle, (at + 1) * middle)
+        short_out[0, :, here] = late[at * HALO : at * HALO + taps]
+        short_out[1, :, here] = part[:taps]
+        short_out[2, :, here] = part[HALO : HALO + taps]
+        spread = halves(middle)
+        count = rows - 2 * HALO
+        for h, lanes in spread:
+            place = (at * len(spread) + h) * count
+            medium_out[place : place + count] = part[2 * HALO :, lanes]
+
+
 def shift(value, axis, steps):
     count = lax.axis_size(axis)
     initial, last = (max(0, -steps), min(count, count - steps))
@@ -374,26 +402,21 @@
     return lax.ppermute(value, axis, [(s, s ^ (1 << bit)) for s in range(count)])
 
 
-def sums_over(early, sent_early, late, sent_late, axis):
+def sums_over(kept, sent, late, sent_late, axis):
     count = lax.axis_size(axis)
-    if count & (count - 1):
-        return lax.psum(early, axis), lax.psum(late, axis)
     bits = count.bit_length() - 1
-    alone = 1 * bits // 4
-    for bit in range(bits - 1, bits - 1 - alone, -1):
-        early = early + swap(sent_early, axis, bit).astype(F32)
-        sent_early = early.astype(BF16)
-    total = jnp.concatenate([early, late], axis=0)
-    sent = jnp.concatenate([sent_early, sent_late], axis=0)
-    for bit in range(bits - alone):
+    middle = late.shape[1] // 2
+
+    def stacked(value):
+        return jnp.concatenate([value[:, :middle], value[:, middle:]], axis=0)
+
+    early = kept + swap(sent, axis, 0).astype(F32)
+    total = jnp.concatenate([early, stacked(late)], axis=0)
+    sent = jnp.concatenate([early.astype(BF16), stacked(sent_late)], axis=0)
+    for bit in range(bits - 1, 0, -1):
         total = total + swap(sent, axis, bit).astype(F32)
         sent = total.astype(BF16)
-    early, late = total[: early.shape[0]], total[early.shape[0] :]
-    sent = late.astype(BF16)
-    for bit in range(bits - alone, bits):
-        late = late + swap(sent, axis, bit).astype(F32)
-        sent = late.astype(BF16)
-    return early, late
+    return total, swap(sent, axis, 0)
 
 
 def in_hbm(value):
@@ -406,7 +429,9 @@
     width = groups
     rest = rows - BLOCK
     taps_short = short_filter.shape[1]
-    whole, half, low, high = (jnp.asarray(m) for m in transforms())
+    matrices = transforms()
+    whole, half, low, high = (jnp.asarray(m) for m in matrices)
+    lead, back = (jnp.asarray(m[:, :WINDOW].copy()) for m in (matrices[0], matrices[3]))
 
     def col(count, at=0, wide=width):
         return pl.BlockSpec((count, wide), lambda i: (at, i))
@@ -465,6 +490,7 @@
     behind = shift(behind, "seq", 1)
 
     me = lax.axis_index("fsdp").astype(jnp.int32).reshape(1)
+    place = lax.axis_index("seq").astype(jnp.int32).reshape(1)
     many = channels // wide
 
     def big(count, at=0):
@@ -483,7 +509,7 @@
     grad_query, nexts, sums_q, more, spec, tap_rows = pl.pallas_call(
         middle_kernel,
         grid_spec=pltpu.PrefetchScalarGridSpec(
-            num_scalar_prefetch=1,
+            num_scalar_prefetch=2,
             grid=(many,),
             in_specs=[big(rows), big(rest, corner), big(rows), big_filters]
             + [still(m.shape) for m in (half, whole, high)]
@@ -500,7 +526,7 @@
         cost_estimate=cost(4e9, 8e6),
         name="middle",
         compiler_params=room,
-    )(me, query, grad_out, gated, short_filter, half, whole, high, medium_filter, *taps)
+    )(me, place, query, grad_out, gated, short_filter, half, whole, high, medium_filter, *taps)
 
     mine = (width // share, BLOCK)
     gk, gv, far, sums_kv, own, *sends = pl.pallas_call(
@@ -548,27 +574,34 @@
     )(gk, gv, nexts, far, short_filter, grad_query)
 
     extra = mine[0] * BLOCK // channels
-    tall = (2 * HALO + extra, channels)
-    sums_kv, sent_kv = pl.pallas_call(
+    tall = (2 * HALO + extra, channels // 2)
+    kept, sent = pl.pallas_call(
         pack_kernel,
+        grid_spec=pltpu.PrefetchScalarGridSpec(
+            num_scalar_prefetch=1,
+            grid=(1,),
+            in_specs=[still((2 * HALO, channels))] + [still(mine)] * share,
+            out_specs=[still(tall)] * 2,
+            scratch_shapes=[pltpu.VMEM((2 * HALO + extra, channels), F32)],
+        ),
         out_shape=[jax.ShapeDtypeStruct(tall, F32), jax.ShapeDtypeStruct(tall, BF16)],
         name="pack",
         compiler_params=room,
-    )(sums_kv, own, *parts)
+    )(place, sums_kv, own, *parts)
 
     grads, sums_q, sent_q = pl.pallas_call(
         fifth_kernel,
         grid=(many,),
         in_specs=[big(BLOCK), big(3 * HALO), big(HALO)]
         + [big(BLOCK)] * 3
-        + [still((3, BLOCK, width)), still(whole.shape), still(high.shape)],
+        + [still((3, BLOCK, width)), still(lead.shape), still(back.shape)],
         out_specs=[big(BLOCK), big(HALO), big(HALO)],
         out_shape=[out(BLOCK, BF16), out(HALO, F32), out(HALO, BF16)],
         scratch_shapes=[scratch(BLOCK + HALO, wide)] * 2,
         cost_estimate=cost(2e9, 8e6),
         name="fifth",
         compiler_params=room,
-    )(query, tails, sums_q, grad_out, gated, behind, spec, whole, high)
+    )(query, tails, sums_q, grad_out, gated, behind, spec, lead, back)
 
     grad_query = pl.pallas_call(
         sixth_kernel,
@@ -583,12 +616,19 @@
         compiler_params=room,
     )(grads, nexts, short_filter, grad_query)
 
-    early, late = sums_over(sums_kv, sent_kv, sums_q, sent_q, "seq")
-    packed = early[2 * HALO :]
-    grad_medium = jnp.concatenate(
-        [packed[:, at : at + BLOCK] for at in range(0, channels, BLOCK)], axis=0
-    )
-    grad_short = jnp.stack([late[:taps_short], early[:taps_short], early[HALO : HALO + taps_short]])
+    total, other = sums_over(kept, sent, sums_q, sent_q, "seq")
+    grad_short, grad_medium = pl.pallas_call(
+        last_kernel,
+        grid_spec=pltpu.PrefetchScalarGridSpec(
+            num_scalar_prefetch=1,
+            grid=(1,),
+            in_specs=[still(total.shape)] * 2,
+            out_specs=[still(short_filter.shape), still(mine)],
+        ),
+        out_shape=[jax.ShapeDtypeStruct(short_filter.shape, F32), jax.ShapeDtypeStruct(mine, F32)],
+        name="finish",
+        compiler_params=room,
+    )(place, total, other)
     return grad_query, grad_key, grad_value, grad_short, grad_medium
 
 

time: 76.6 us -> 76.4 us (level)
  waiting for transfers between devices: 12.7 us -> 16.8 us
  starting transfers between devices: 31.5 us -> 28 us
    ppermute x5, starting transfers between devices: 20.9 us -> 17.3 us  [swap(): return lax.ppermute(value, axis, [(s, s ^ 1 << bit) for s in range(count)])]
    ppermute x3, waiting for transfers between devices: 3.97 us -> 7.15 us  [shift(): lax.ppermute(value, axis, [(s, s + steps) for s in range(initial, last)])]
    ppermute x5, waiting for transfers between devices: 7.54 us -> 9.69 us  [swap(): return lax.ppermute(value, axis, [(s, s ^ 1 << bit) for s in range(count)])]
    ppermute x2, waiting for transfers between devices: 1.2 us -> 0.01 us  [exchanged(): lax.ppermute(part, axis, [(s, (s + step) % count) for s in range(count)])]
  transfers between devices with their start and end apart: 10 -> 10, of which waited for: 7 -> 7; matrix products, arithmetic and copies ran while one was open for 0% -> 0% of each run, Pallas kernels for 37% -> 36%
where the time goes in v6:
time: 76.4 us; the launch traced here: 76 us
  Pallas kernels  30.3 us (40%)
  starting transfers between devices  28 us (37%)
  waiting for transfers between devices  16.8 us (22%)
  between operations  0.79 us (1%)
    ppermute x5, starting transfers between devices, swap(): return lax.ppermute(value, axis, [(s, s ^ 1 << bit) for s in range(count)])  17.3 us
    ppermute x3, starting transfers between devices, shift(): lax.ppermute(value, axis, [(s, s + steps) for s in range(initial, last)])  10.5 us
    ppermute x5, waiting for transfers between devices, swap(): return lax.ppermute(value, axis, [(s, s ^ 1 << bit) for s in range(count)])  9.69 us
    pallas_call x1, Pallas kernels, shards(): pl.pallas_call(third_kernel, grid_spec=pltpu.PrefetchScalarGridSpec(num_s...  8.35 us
    ppermute x3, waiting for transfers between devices, shift(): lax.ppermute(value, axis, [(s, s + steps) for s in range(initial, last)])  7.15 us
    pallas_call x1, Pallas kernels, shards(): pl.pallas_call(middle_kernel, grid_spec=pltpu.PrefetchScalarGridSpec(num_...  5.35 us
    pallas_call x1, Pallas kernels, shards(): pl.pallas_call(second_kernel, grid=(channels // wide,), in_specs=[col(row...  4.5 us
    pallas_call x1, Pallas kernels, shards(): pl.pallas_call(fifth_kernel, grid=(many,), in_specs=[big(BLOCK), big(3 *...  3.68 us
  transfers between devices with their start and end apart: 10, of which 7 were waited for; matrix products, arithmetic and copies ran while one was open for 0% of the time, Pallas kernels for 36%

profile of v6, /device:TPU:0, one launch (start us, length us, event | category | flops | bytes accessed | tf_op | source)
XLA Modules:
  0.0 76.0 jit_solution(396646458523027633)
XLA Ops:
  0.6 0.0 copy-start
  0.6 2.0 %first.1 = (bf16[24,2048]{1,0:T(8,128)(2,1)S(1)}, bf16[160,2048]{1,0:T(8,128)(2,1)S(1)}) custom-call(bf16[192,2048]{1,0:T(8,128)(2,1)} %q.7, bf16[192,2048]{1,0:T(8,128)(2,1)} %g.7, bf16[192,2048]{1,0:T(8,128)(2,1)} %q.7, bf16[192,2048]{1,0:T(8,128)(2,1)} %k.3, bf16[192,2048]{1,0:T(8,128)(2,1)} %v.3, bf16[192,2048]{1,0:T(8,128)(2,1)} %k.3, ...), custom_call_target="tpu_custom_call" | custom-call | tf_op jit(solution)/shard_map/first/pallas_call | solution.py:459
  2.6 4.9 %collective-permute-start = (bf16[24,2048]{1,0:T(8,128)(2,1)S(1)}, bf16[24,2048]{1,0:T(8,128)(2,1)S(1)}, u32[]{:S(2)}, u32[]{:S(2)}) collective-permute-start(bf16[24,2048]{1,0:T(8,128)(2,1)S(1)} %get-tuple-element.34.ends), channel_id=1, source_target_pairs={{0,2},{2,4},{4,6},{6,8},{8,10},{10,12},{12,14},{14,16},{16,18},{18... | collective-permute-start | bytes 294920 | tf_op jit(solution)/shard_map/ppermute | solution.py:389
  7.5 0.0 copy-done
  7.5 0.1 collective-permute-start.1
  7.6 1.3 %collective-permute-start.3 = (bf16[160,2048]{1,0:T(8,128)(2,1)S(1)}, bf16[160,2048]{1,0:T(8,128)(2,1)S(1)}, u32[]{:S(2)}, u32[]{:S(2)}) collective-permute-start(bf16[160,2048]{1,0:T(8,128)(2,1)S(1)} %get-tuple-element.41), channel_id=1, source_target_pairs={{2,0},{4,2},{6,4},{8,6},{10,8},{12,10},{14,12},{16,14},{18,16},{20... | collective-permute-start | bytes 1966088 | tf_op jit(solution)/shard_map/ppermute | solution.py:389
  8.9 0.8 %collective-permute-done.tails = bf16[24,2048]{1,0:T(8,128)(2,1)S(1)} collective-permute-done((bf16[24,2048]{1,0:T(8,128)(2,1)S(1)}, bf16[24,2048]{1,0:T(8,128)(2,1)S(1)}, u32[]{:S(2)}, u32[]{:S(2)}) %collective-permute-start) | collective-permute-done | bytes 98336 | tf_op jit(solution)/shard_map/ppermute | solution.py:389
  9.7 4.5 %second.1 = (bf16[192,2048]{1,0:T(8,128)(2,1)S(1)}, bf16[192,2048]{1,0:T(8,128)(2,1)S(1)}, f32[192,2048]{1,0:T(8,128)S(1)}, f32[192,2048]{1,0:T(8,128)S(1)}, bf16[128,2048]{1,0:T(8,128)(2,1)S(1)}) custom-call(bf16[192,2048]{1,0:T(8,128)(2,1)} %q.7, bf16[192,2048]{1,0:T(8,128)(2,1)} %k.3, bf16[192,2048]{1,0:T(8,128)(2,1)} %v.3, bf16[192,2048]{1,0:T(8,128)(2,1)} %g.7, ...), custom_call_target="tpu_custom_call" | custom-call | flops 4000000000 | bytes 20000000 | tf_op jit(solution)/shard_map/second/pallas_call | solution.py:477
  14.2 4.3 %collective-permute-start.2 = (bf16[128,2048]{1,0:T(8,128)(2,1)S(1)}, bf16[128,2048]{1,0:T(8,128)(2,1)S(1)}, u32[]{:S(2)}, u32[]{:S(2)}) collective-permute-start(bf16[128,2048]{1,0:T(8,128)(2,1)S(1)} %get-tuple-element.37), channel_id=1, source_target_pairs={{0,2},{2,4},{4,6},{6,8},{8,10},{10,12},{12,14},{14,16},{16,18},{18... | collective-permute-start | bytes 1572872 | tf_op jit(solution)/shard_map/ppermute | solution.py:389
  18.6 0.0 collective-permute-done.1.refs_0_
  18.6 5.4 %middle.1 = (bf16[192,2048]{1,0:T(8,128)(2,1)}, f32[16,2048]{1,0:T(8,128)S(1)}, f32[8,2048]{1,0:T(8,128)S(1)}, f32[8,2048]{1,0:T(8,128)S(1)}, f32[3,128,256]{2,1,0:T(8,128)S(1)}, /*index=5*/f32[8,256]{1,0:T(8,128)S(1)}) custom-call(s32[1]{0:T(128)} %bitcast.me, s32[1]{0:T(128)} %bitcast.1._.place, bf16[192,2048]{1,0:T(8,128)(2,1)} %q.7, ...), custom_call_target="tpu_custom_call" | custom-call | flops 4000000000 | bytes 8000000 | tf_op jit(solution)/shard_map/middle/pallas_call | solution.py:509
  23.9 3.2 %collective-permute-done.3.ahead = bf16[160,2048]{1,0:T(8,128)(2,1)S(1)} collective-permute-done((bf16[160,2048]{1,0:T(8,128)(2,1)S(1)}, bf16[160,2048]{1,0:T(8,128)(2,1)S(1)}, u32[]{:S(2)}, u32[]{:S(2)}) %collective-permute-start.3) | collective-permute-done | bytes 655392 | tf_op jit(solution)/shard_map/ppermute | solution.py:389
  27.1 8.4 %third.1 = (bf16[208,2048]{1,0:T(8,128)(2,1)S(1)}, bf16[208,2048]{1,0:T(8,128)(2,1)S(1)}, f32[8,2048]{1,0:T(8,128)S(1)}, f32[16,2048]{1,0:T(8,128)S(1)}, f32[128...) custom-call(s32[1]{0:T(128)} %bitcast.me, bf16[192,2048]{1,0:T(8,128)(2,1)} %k.3, bf16[192,2048]{1,0:T(8,128)(2,1)} %v.3, ...), custom_call_target="tpu_custom_call" | custom-call | flops 8000000000 | bytes 20000000 | tf_op jit(solution)/shard_map/third/pallas_call | solution.py:532
  35.5 0.1 collective-permute-start.4
  35.6 3.2 %collective-permute-done.2.behind = bf16[128,2048]{1,0:T(8,128)(2,1)S(1)} collective-permute-done((bf16[128,2048]{1,0:T(8,128)(2,1)S(1)}, bf16[128,2048]{1,0:T(8,128)(2,1)S(1)}, u32[]{:S(2)}, u32[]{:S(2)}) %collective-permute-start.2) | collective-permute-done | bytes 524320 | tf_op jit(solution)/shard_map/ppermute | solution.py:389
  38.7 0.0 copy-done.1
  38.7 0.0 copy-done.2
  38.7 3.7 %fifth.1 = (bf16[128,2048]{1,0:T(8,128)(2,1)S(1)}, f32[8,2048]{1,0:T(8,128)S(1)}, bf16[8,2048]{1,0:T(8,128)(2,1)S(1)}) custom-call(bf16[192,2048]{1,0:T(8,128)(2,1)} %q.7, bf16[24,2048]{1,0:T(8,128)(2,1)S(1)} %collective-permute-done.tails, f32[8,2048]{1,0:T(8,128)S(1)} %get-tuple-element.36.sums, bf16[192,2048]{1,0:T(8,128)(2,1)} %g.7, ...), custom_call_target="tpu_custom_call" | custom-call | flops 2000000000 | bytes 8000000 | tf_op jit(solution)/shard_map/fifth/pallas_call | solution.py:592
  42.4 0.0 collective-permute-done.4.refs_0_
  42.5 2.6 %collective-permute-start.5 = (bf16[24,1024]{1,0:T(8,128)(2,1)S(1)}, bf16[24,1024]{1,0:T(8,128)(2,1)S(1)}, u32[]{:S(2)}, u32[]{:S(2)}) collective-permute-start(bf16[24,1024]{1,0:T(8,128)(2,1)S(1)} %get-tuple-element.58), channel_id=1, source_target_pairs={{0,2},{2,0},{4,6},{6,4},{8,10},{10,8},{12,14},{14,12},{16,18},{18,... | collective-permute-start | bytes 147464 | tf_op jit(solution)/shard_map/ppermute | solution.py:402
  45.0 2.1 %collective-permute-done.5 = bf16[24,1024]{1,0:T(8,128)(2,1)S(1)} collective-permute-done((bf16[24,1024]{1,0:T(8,128)(2,1)S(1)}, bf16[24,1024]{1,0:T(8,128)(2,1)S(1)}, u32[]{:S(2)}, u32[]{:S(2)}) %collective-permute-start.5) | collective-permute-done | bytes 49184 | tf_op jit(solution)/shard_map/ppermute | solution.py:402
  47.1 2.7 %collective-permute-start.6 = (bf16[40,1024]{1,0:T(8,128)(2,1)S(1)}, bf16[40,1024]{1,0:T(8,128)(2,1)S(1)}, u32[]{:S(2)}, u32[]{:S(2)}) collective-permute-start(bf16[40,1024]{1,0:T(8,128)(2,1)S(1)} %pad_maximum_fusion), channel_id=1, source_target_pairs={{0,16},{2,18},{4,20},{6,22},{8,24},{10,26},{12,28},{14,30},{16,0},... | collective-permute-start | bytes 245768 | tf_op jit(solution)/shard_map/ppermute | solution.py:402
  49.8 2.8 %collective-permute-done.6 = bf16[40,1024]{1,0:T(8,128)(2,1)S(1)} collective-permute-done((bf16[40,1024]{1,0:T(8,128)(2,1)S(1)}, bf16[40,1024]{1,0:T(8,128)(2,1)S(1)}, u32[]{:S(2)}, u32[]{:S(2)}) %collective-permute-start.6) | collective-permute-done | bytes 81952 | tf_op jit(solution)/shard_map/ppermute | solution.py:402
  52.6 1.6 %collective-permute-start.7 = (bf16[40,1024]{1,0:T(8,128)(2,1)S(1)}, bf16[40,1024]{1,0:T(8,128)(2,1)S(1)}, u32[]{:S(2)}, u32[]{:S(2)}) collective-permute-start(bf16[40,1024]{1,0:T(8,128)(2,1)S(1)} %fusion.1), channel_id=1, source_target_pairs={{0,8},{2,10},{4,12},{6,14},{8,0},{10,2},{12,4},{14,6},{16,24},{18,... | collective-permute-start | bytes 245768 | tf_op jit(solution)/shard_map/ppermute | solution.py:402
  54.2 2.9 %collective-permute-done.7 = bf16[40,1024]{1,0:T(8,128)(2,1)S(1)} collective-permute-done((bf16[40,1024]{1,0:T(8,128)(2,1)S(1)}, bf16[40,1024]{1,0:T(8,128)(2,1)S(1)}, u32[]{:S(2)}, u32[]{:S(2)}) %collective-permute-start.7) | collective-permute-done | bytes 81952 | tf_op jit(solution)/shard_map/ppermute | solution.py:402
  57.2 10.1 %collective-permute-start.8 = (bf16[40,1024]{1,0:T(8,128)(2,1)S(1)}, bf16[40,1024]{1,0:T(8,128)(2,1)S(1)}, u32[]{:S(2)}, u32[]{:S(2)}) collective-permute-start(bf16[40,1024]{1,0:T(8,128)(2,1)S(1)} %fusion), channel_id=1, source_target_pairs={{0,4},{2,6},{4,0},{6,2},{8,12},{10,14},{12,8},{14,10},{16,20},{18,... | collective-permute-start | bytes 245768 | tf_op jit(solution)/shard_map/ppermute | solution.py:402
  67.3 3.5 %fourth.1 = (bf16[192,2048]{1,0:T(8,128)(2,1)}, bf16[192,2048]{1,0:T(8,128)(2,1)}, bf16[192,2048]{1,0:T(8,128)(2,1)}) custom-call(bf16[208,2048]{1,0:T(8,128)(2,1)S(1)} %get-tuple-element.47.gk, bf16[208,2048]{1,0:T(8,128)(2,1)S(1)} %get-tuple-element.48.gv, f32[16,2048]{1,0:T(8,128)S(1)} %get-tuple-element.40.near.following, ...), custom_call_target="tpu_custom_call", output_to_operand_aliasing={{2}: (5, {})} | custom-call | flops 4000000000 | bytes 10000000 | tf_op jit(solution)/shard_map/fourth/pallas_call | solution.py:562
  70.8 0.0 collective-permute-done.8
  70.8 0.4 collective-permute-start.9
  71.3 2.2 %sixth.1 = bf16[192,2048]{1,0:T(8,128)(2,1)} custom-call(bf16[128,2048]{1,0:T(8,128)(2,1)S(1)} %get-tuple-element.39.grad, f32[16,2048]{1,0:T(8,128)S(1)} %get-tuple-element.40.near.following, f32[3,7,2048]{2,1,0:T(8,128)} %w.11, bf16[192,2048]{1,0:T(8,128)(2,1)} %get-tuple-element.51.gq_in), custom_call_target="tpu_custom_call", output_to_operand_aliasing={{}: (3, {})} | custom-call | flops 2000000000 | bytes 3000000 | tf_op jit(solution)/shard_map/sixth/pallas_call | solution.py:606
  73.4 1.9 %collective-permute-done.9.other = bf16[40,1024]{1,0:T(8,128)(2,1)S(1)} collective-permute-done((bf16[40,1024]{1,0:T(8,128)(2,1)S(1)}, bf16[40,1024]{1,0:T(8,128)(2,1)S(1)}, u32[]{:S(2)}, u32[]{:S(2)}) %collective-permute-start.9) | collective-permute-done | bytes 81952 | tf_op jit(solution)/shard_map/ppermute | solution.py:402
  75.3 0.7 finish.1
  (11 shorter events, 0.2 us)
Async XLA Ops:
  0.6 6.9 %copy-start = (f32[128,128]{1,0:T(8,128)S(1)}, f32[128,128]{1,0:T(8,128)}, u32[]{:S(2)}) copy-start(f32[128,128]{1,0:T(8,128)} %own_taps.1) | copy-start | bytes 196612
  2.6 7.1 %collective-permute-start = (bf16[24,2048]{1,0:T(8,128)(2,1)S(1)}, bf16[24,2048]{1,0:T(8,128)(2,1)S(1)}, u32[]{:S(2)}, u32[]{:S(2)}) collective-permute-start(bf16[24,2048]{1,0:T(8,128)(2,1)S(1)} %get-tuple-element.34.ends), channel_id=1, source_target_pairs={{0,2},{2,4},{4,6},{6,8},{8,10},{10,12},{12,14},{14,16},{16,18},{18... | collective-permute-start | bytes 294920 | tf_op jit(solution)/shard_map/ppermute | solution.py:389
  7.5 11.0 %collective-permute-start.1 = (bf16[128,128]{1,0:T(8,128)(2,1)S(1)}, bf16[128,128]{1,0:T(8,128)(2,1)S(1)}, u32[]{:S(2)}, u32[]{:S(2)}) collective-permute-start(bf16[128,128]{1,0:T(8,128)(2,1)S(1)} %convert_element_type.27), channel_id=1, source_target_pairs={{0,1},{1,0},{2,3},{3,2},{4,5},{5,4},{6,7},{7,6},{8,9},{9,8},{10,11... | collective-permute-start | bytes 98312 | tf_op jit(solution)/shard_map/ppermute | solution.py:395
  7.6 19.5 %collective-permute-start.3 = (bf16[160,2048]{1,0:T(8,128)(2,1)S(1)}, bf16[160,2048]{1,0:T(8,128)(2,1)S(1)}, u32[]{:S(2)}, u32[]{:S(2)}) collective-permute-start(bf16[160,2048]{1,0:T(8,128)(2,1)S(1)} %get-tuple-element.41), channel_id=1, source_target_pairs={{2,0},{4,2},{6,4},{8,6},{10,8},{12,10},{14,12},{16,14},{18,16},{20... | collective-permute-start | bytes 1966088 | tf_op jit(solution)/shard_map/ppermute | solution.py:389
  14.2 24.5 %collective-permute-start.2 = (bf16[128,2048]{1,0:T(8,128)(2,1)S(1)}, bf16[128,2048]{1,0:T(8,128)(2,1)S(1)}, u32[]{:S(2)}, u32[]{:S(2)}) collective-permute-start(bf16[128,2048]{1,0:T(8,128)(2,1)S(1)} %get-tuple-element.37), channel_id=1, source_target_pairs={{0,2},{2,4},{4,6},{6,8},{8,10},{10,12},{12,14},{14,16},{16,18},{18... | collective-permute-start | bytes 1572872 | tf_op jit(solution)/shard_map/ppermute | solution.py:389
  27.1 11.6 %copy-start.1 = (bf16[256,256]{1,0:T(8,128)(2,1)S(1)}, bf16[256,256]{1,0:T(8,128)(2,1)}, u32[]{:S(2)}) copy-start(bf16[256,256]{1,0:T(8,128)(2,1)} %constant.24.clone.lead) | copy-start | bytes 393220
  27.1 11.6 %copy-start.2 = (bf16[128,256]{1,0:T(8,128)(2,1)S(1)}, bf16[128,256]{1,0:T(8,128)(2,1)}, u32[]{:S(2)}) copy-start(bf16[128,256]{1,0:T(8,128)(2,1)} %constant.25.clone.back) | copy-start | bytes 196612
  35.5 7.0 %collective-permute-start.4 = (bf16[128,128]{1,0:T(8,128)(2,1)S(1)}, bf16[128,128]{1,0:T(8,128)(2,1)S(1)}, u32[]{:S(2)}, u32[]{:S(2)}) collective-permute-start(bf16[128,128]{1,0:T(8,128)(2,1)S(1)} %get-tuple-element.56), channel_id=1, source_target_pairs={{0,1},{1,0},{2,3},{3,2},{4,5},{5,4},{6,7},{7,6},{8,9},{9,8},{10,11... | collective-permute-start | bytes 98312 | tf_op jit(solution)/shard_map/ppermute | solution.py:395
  42.5 4.6 %collective-permute-start.5 = (bf16[24,1024]{1,0:T(8,128)(2,1)S(1)}, bf16[24,1024]{1,0:T(8,128)(2,1)S(1)}, u32[]{:S(2)}, u32[]{:S(2)}) collective-permute-start(bf16[24,1024]{1,0:T(8,128)(2,1)S(1)} %get-tuple-element.58), channel_id=1, source_target_pairs={{0,2},{2,0},{4,6},{6,4},{8,10},{10,8},{12,14},{14,12},{16,18},{18,... | collective-permute-start | bytes 147464 | tf_op jit(solution)/shard_map/ppermute | solution.py:402
  47.1 5.5 %collective-permute-start.6 = (bf16[40,1024]{1,0:T(8,128)(2,1)S(1)}, bf16[40,1024]{1,0:T(8,128)(2,1)S(1)}, u32[]{:S(2)}, u32[]{:S(2)}) collective-permute-start(bf16[40,1024]{1,0:T(8,128)(2,1)S(1)} %pad_maximum_fusion), channel_id=1, source_target_pairs={{0,16},{2,18},{4,20},{6,22},{8,24},{10,26},{12,28},{14,30},{16,0},... | collective-permute-start | bytes 245768 | tf_op jit(solution)/shard_map/ppermute | solution.py:402
  52.6 4.5 %collective-permute-start.7 = (bf16[40,1024]{1,0:T(8,128)(2,1)S(1)}, bf16[40,1024]{1,0:T(8,128)(2,1)S(1)}, u32[]{:S(2)}, u32[]{:S(2)}) collective-permute-start(bf16[40,1024]{1,0:T(8,128)(2,1)S(1)} %fusion.1), channel_id=1, source_target_pairs={{0,8},{2,10},{4,12},{6,14},{8,0},{10,2},{12,4},{14,6},{16,24},{18,... | collective-permute-start | bytes 245768 | tf_op jit(solution)/shard_map/ppermute | solution.py:402
  57.2 13.6 %collective-permute-start.8 = (bf16[40,1024]{1,0:T(8,128)(2,1)S(1)}, bf16[40,1024]{1,0:T(8,128)(2,1)S(1)}, u32[]{:S(2)}, u32[]{:S(2)}) collective-permute-start(bf16[40,1024]{1,0:T(8,128)(2,1)S(1)} %fusion), channel_id=1, source_target_pairs={{0,4},{2,6},{4,0},{6,2},{8,12},{10,14},{12,8},{14,10},{16,20},{18,... | collective-permute-start | bytes 245768 | tf_op jit(solution)/shard_map/ppermute | solution.py:402
  70.8 4.5 %collective-permute-start.9 = (bf16[40,1024]{1,0:T(8,128)(2,1)S(1)}, bf16[40,1024]{1,0:T(8,128)(2,1)S(1)}, u32[]{:S(2)}, u32[]{:S(2)}) collective-permute-start(bf16[40,1024]{1,0:T(8,128)(2,1)S(1)} %get-tuple-element.63), channel_id=1, source_target_pairs={{0,2},{2,0},{4,6},{6,4},{8,10},{10,8},{12,14},{14,12},{16,18},{18,... | collective-permute-start | bytes 245768 | tf_op jit(solution)/shard_map/ppermute | solution.py:402

commit v7 on v6

--- a/solution.py
+++ b/solution.py
@@ -12,12 +12,6 @@
 WINDOW = 2 * BLOCK
 F32 = jnp.float32
 BF16 = jnp.bfloat16
-
-
-def split_terms(matrix):
-    high = matrix.astype(BF16)
-    low = (matrix - high.astype(np.float32)).astype(BF16)
-    return np.asarray(high), np.asarray(low)
 
 
 def transforms():
@@ -31,12 +25,9 @@
     scale = np.full(WINDOW, 2.0 / WINDOW)
     scale[0] = scale[BLOCK] = 1.0 / WINDOW
     inverse = forward.T * scale[None, :]
-    f_high, f_low = split_terms(forward.astype(np.float32))
-    i_high, i_low = split_terms(inverse.astype(np.float32))
-    whole = np.concatenate([f_high, f_low], axis=1)
-    half = np.concatenate([f_high[:, :BLOCK], f_low[:, :BLOCK]], axis=1)
-    back = np.concatenate([i_high, i_low], axis=1)
-    return whole, half, back[:BLOCK], back[BLOCK:]
+    forward = np.asarray(forward.astype(np.float32).astype(BF16))
+    inverse = np.asarray(inverse.astype(np.float32).astype(BF16))
+    return forward, forward[:, :BLOCK].copy(), inverse[:BLOCK], inverse[BLOCK:]
 
 
 def dot(left, right):
@@ -44,7 +35,7 @@
 
 
 def to_spectrum(matrix, rows):
-    return dot(matrix, jnp.concatenate([rows, rows], axis=0))
+    return dot(matrix, rows)
 
 
 def from_spectrum(matrix, real, imag):
@@ -175,7 +166,7 @@
             start = lax.rem(me[0] + share - at, share) * mine
             taps[pl.ds(pl.multiple_of(start, mine), mine)] = part[...].astype(BF16).astype(F32)
         whole_taps = taps[...].astype(BF16)
-        both = jnp.concatenate([whole_taps, whole_taps], axis=1)
+        both = whole_taps
         whole_spec = lax.dot_general(
             half[...], both, (((1,), (1,)), ((), ())), preferred_element_type=F32
         )
@@ -332,7 +323,7 @@
 
 
 def fifth_kernel(
-    q, tails, sums, g, gated, behind, spec, lead, back,
+    q, tails, sums, g, gated, behind, spec, whole, high,
     yq_out, sums_out, send_out,
     xq, yq,
 ):
@@ -341,8 +332,7 @@
     put(xq, HALO, q[...].astype(F32))
     for lanes in blocks(width, spec.shape[2]):
         window = jnp.concatenate([behind[:, lanes], gated[:, lanes]], axis=0)
-        prod = jnp.concatenate(times(dot(lead[...], window), spec), axis=0)
-        sig = dot(back[...], prod.astype(BF16))
+        sig = from_spectrum(high[...], *times(to_spectrum(whole[...], window), spec))
         grad = (g[:, lanes].astype(F32) * sig).astype(BF16)
         yq_out[:, lanes] = grad
         put(yq, 0, grad.astype(F32), lanes.start)
@@ -429,9 +419,7 @@
     width = groups
     rest = rows - BLOCK
     taps_short = short_filter.shape[1]
-    matrices = transforms()
-    whole, half, low, high = (jnp.asarray(m) for m in matrices)
-    lead, back = (jnp.asarray(m[:, :WINDOW].copy()) for m in (matrices[0], matrices[3]))
+    whole, half, low, high = (jnp.asarray(m) for m in transforms())
 
     def col(count, at=0, wide=width):
         return pl.BlockSpec((count, wide), lambda i: (at, i))
@@ -594,14 +582,14 @@
         grid=(many,),
         in_specs=[big(BLOCK), big(3 * HALO), big(HALO)]
         + [big(BLOCK)] * 3
-        + [still((3, BLOCK, width)), still(lead.shape), still(back.shape)],
+        + [still((3, BLOCK, width)), still(whole.shape), still(high.shape)],
         out_specs=[big(BLOCK), big(HALO), big(HALO)],
         out_shape=[out(BLOCK, BF16), out(HALO, F32), out(HALO, BF16)],
         scratch_shapes=[scratch(BLOCK + HALO, wide)] * 2,
         cost_estimate=cost(2e9, 8e6),
         name="fifth",
         compiler_params=room,
-    )(query, tails, sums_q, grad_out, gated, behind, spec, lead, back)
+    )(query, tails, sums_q, grad_out, gated, behind, spec, whole, high)
 
     grad_query = pl.pallas_call(
         sixth_kernel,

time: 76.4 us -> 75.7 us (level)
  Pallas kernels: 30.3 us -> 28.8 us
  waiting for transfers between devices: 16.8 us -> 18.3 us
    ppermute x3, waiting for transfers between devices: 7.15 us -> 8.59 us  [shift(): lax.ppermute(value, axis, [(s, s + steps) for s in range(initial, last)])]
    pallas_call x1, Pallas kernels: 5.35 us -> 4.53 us  [shards(): pl.pallas_call(middle_kernel, grid_spec=pltpu.PrefetchScalarGridSpec(num_...]
  transfers between devices with their start and end apart: 10 -> 10, of which waited for: 7 -> 7; matrix products, arithmetic and copies ran while one was open for 0% -> 0% of each run, Pallas kernels for 36% -> 35%
where the time goes in v7:
time: 75.7 us; the launch traced here: 75.4 us
  Pallas kernels  28.8 us (38%)
  starting transfers between devices  27.4 us (36%)
  waiting for transfers between devices  18.3 us (24%)
  between operations  0.79 us (1%)
    ppermute x5, starting transfers between devices, swap(): return lax.ppermute(value, axis, [(s, s ^ 1 << bit) for s in range(count)])  16.7 us
    ppermute x3, starting transfers between devices, shift(): lax.ppermute(value, axis, [(s, s + steps) for s in range(initial, last)])  10.5 us
    ppermute x5, waiting for transfers between devices, swap(): return lax.ppermute(value, axis, [(s, s ^ 1 << bit) for s in range(count)])  9.68 us
    ppermute x3, waiting for transfers between devices, shift(): lax.ppermute(value, axis, [(s, s + steps) for s in range(initial, last)])  8.59 us
    pallas_call x1, Pallas kernels, shards(): pl.pallas_call(third_kernel, grid_spec=pltpu.PrefetchScalarGridSpec(num_s...  7.73 us
    pallas_call x1, Pallas kernels, shards(): pl.pallas_call(middle_kernel, grid_spec=pltpu.PrefetchScalarGridSpec(num_...  4.53 us
    pallas_call x1, Pallas kernels, shards(): pl.pallas_call(second_kernel, grid=(channels // wide,), in_specs=[col(row...  4.5 us
    pallas_call x1, Pallas kernels, shards(): pl.pallas_call(fifth_kernel, grid=(many,), in_specs=[big(BLOCK), big(3 *...  3.72 us
  transfers between devices with their start and end apart: 10, of which 7 were waited for; matrix products, arithmetic and copies ran while one was open for 0% of the time, Pallas kernels for 35%

profile of v7, /device:TPU:0, one launch (start us, length us, event | category | flops | bytes accessed | tf_op | source)
XLA Modules:
  0.0 75.4 jit_solution(7821256127974635492)
XLA Ops:
  0.6 0.0 copy-start
  0.6 2.0 %first.1 = (bf16[24,2048]{1,0:T(8,128)(2,1)S(1)}, bf16[160,2048]{1,0:T(8,128)(2,1)S(1)}) custom-call(bf16[192,2048]{1,0:T(8,128)(2,1)} %q.7, bf16[192,2048]{1,0:T(8,128)(2,1)} %g.7, bf16[192,2048]{1,0:T(8,128)(2,1)} %q.7, bf16[192,2048]{1,0:T(8,128)(2,1)} %k.3, bf16[192,2048]{1,0:T(8,128)(2,1)} %v.3, bf16[192,2048]{1,0:T(8,128)(2,1)} %k.3, ...), custom_call_target="tpu_custom_call" | custom-call | tf_op jit(solution)/shard_map/first/pallas_call | solution.py:447
  2.6 4.9 %collective-permute-start = (bf16[24,2048]{1,0:T(8,128)(2,1)S(1)}, bf16[24,2048]{1,0:T(8,128)(2,1)S(1)}, u32[]{:S(2)}, u32[]{:S(2)}) collective-permute-start(bf16[24,2048]{1,0:T(8,128)(2,1)S(1)} %get-tuple-element.34.ends), channel_id=1, source_target_pairs={{0,2},{2,4},{4,6},{6,8},{8,10},{10,12},{12,14},{14,16},{16,18},{18... | collective-permute-start | bytes 294920 | tf_op jit(solution)/shard_map/ppermute | solution.py:379
  7.5 0.0 copy-done
  7.5 0.1 collective-permute-start.1
  7.6 1.3 %collective-permute-start.3 = (bf16[160,2048]{1,0:T(8,128)(2,1)S(1)}, bf16[160,2048]{1,0:T(8,128)(2,1)S(1)}, u32[]{:S(2)}, u32[]{:S(2)}) collective-permute-start(bf16[160,2048]{1,0:T(8,128)(2,1)S(1)} %get-tuple-element.41), channel_id=1, source_target_pairs={{2,0},{4,2},{6,4},{8,6},{10,8},{12,10},{14,12},{16,14},{18,16},{20... | collective-permute-start | bytes 1966088 | tf_op jit(solution)/shard_map/ppermute | solution.py:379
  8.9 0.8 %collective-permute-done.tails = bf16[24,2048]{1,0:T(8,128)(2,1)S(1)} collective-permute-done((bf16[24,2048]{1,0:T(8,128)(2,1)S(1)}, bf16[24,2048]{1,0:T(8,128)(2,1)S(1)}, u32[]{:S(2)}, u32[]{:S(2)}) %collective-permute-start) | collective-permute-done | bytes 98336 | tf_op jit(solution)/shard_map/ppermute | solution.py:379
  9.7 4.5 %second.1 = (bf16[192,2048]{1,0:T(8,128)(2,1)S(1)}, bf16[192,2048]{1,0:T(8,128)(2,1)S(1)}, f32[192,2048]{1,0:T(8,128)S(1)}, f32[192,2048]{1,0:T(8,128)S(1)}, bf16[128,2048]{1,0:T(8,128)(2,1)S(1)}) custom-call(bf16[192,2048]{1,0:T(8,128)(2,1)} %q.7, bf16[192,2048]{1,0:T(8,128)(2,1)} %k.3, bf16[192,2048]{1,0:T(8,128)(2,1)} %v.3, bf16[192,2048]{1,0:T(8,128)(2,1)} %g.7, ...), custom_call_target="tpu_custom_call" | custom-call | flops 4000000000 | bytes 20000000 | tf_op jit(solution)/shard_map/second/pallas_call | solution.py:465
  14.2 4.3 %collective-permute-start.2 = (bf16[128,2048]{1,0:T(8,128)(2,1)S(1)}, bf16[128,2048]{1,0:T(8,128)(2,1)S(1)}, u32[]{:S(2)}, u32[]{:S(2)}) collective-permute-start(bf16[128,2048]{1,0:T(8,128)(2,1)S(1)} %get-tuple-element.37), channel_id=1, source_target_pairs={{0,2},{2,4},{4,6},{6,8},{8,10},{10,12},{12,14},{14,16},{16,18},{18... | collective-permute-start | bytes 1572872 | tf_op jit(solution)/shard_map/ppermute | solution.py:379
  18.6 0.0 collective-permute-done.1.refs_0_
  18.6 4.5 %middle.1 = (bf16[192,2048]{1,0:T(8,128)(2,1)}, f32[16,2048]{1,0:T(8,128)S(1)}, f32[8,2048]{1,0:T(8,128)S(1)}, f32[8,2048]{1,0:T(8,128)S(1)}, f32[3,128,256]{2,1,0:T(8,128)S(1)}, /*index=5*/f32[8,256]{1,0:T(8,128)S(1)}) custom-call(s32[1]{0:T(128)} %bitcast.me, s32[1]{0:T(128)} %bitcast.1._.place, bf16[192,2048]{1,0:T(8,128)(2,1)} %q.7, ...), custom_call_target="tpu_custom_call" | custom-call | flops 4000000000 | bytes 8000000 | tf_op jit(solution)/shard_map/middle/pallas_call | solution.py:497
  23.1 4.0 %collective-permute-done.3.ahead = bf16[160,2048]{1,0:T(8,128)(2,1)S(1)} collective-permute-done((bf16[160,2048]{1,0:T(8,128)(2,1)S(1)}, bf16[160,2048]{1,0:T(8,128)(2,1)S(1)}, u32[]{:S(2)}, u32[]{:S(2)}) %collective-permute-start.3) | collective-permute-done | bytes 655392 | tf_op jit(solution)/shard_map/ppermute | solution.py:379
  27.1 7.7 %third.1 = (bf16[208,2048]{1,0:T(8,128)(2,1)S(1)}, bf16[208,2048]{1,0:T(8,128)(2,1)S(1)}, f32[8,2048]{1,0:T(8,128)S(1)}, f32[16,2048]{1,0:T(8,128)S(1)}, f32[128...) custom-call(s32[1]{0:T(128)} %bitcast.me, bf16[192,2048]{1,0:T(8,128)(2,1)} %k.3, bf16[192,2048]{1,0:T(8,128)(2,1)} %v.3, ...), custom_call_target="tpu_custom_call" | custom-call | flops 8000000000 | bytes 20000000 | tf_op jit(solution)/shard_map/third/pallas_call | solution.py:520
  34.9 0.1 collective-permute-start.4
  34.9 3.8 %collective-permute-done.2.behind = bf16[128,2048]{1,0:T(8,128)(2,1)S(1)} collective-permute-done((bf16[128,2048]{1,0:T(8,128)(2,1)S(1)}, bf16[128,2048]{1,0:T(8,128)(2,1)S(1)}, u32[]{:S(2)}, u32[]{:S(2)}) %collective-permute-start.2) | collective-permute-done | bytes 524320 | tf_op jit(solution)/shard_map/ppermute | solution.py:379
  38.7 3.7 %fifth.1 = (bf16[128,2048]{1,0:T(8,128)(2,1)S(1)}, f32[8,2048]{1,0:T(8,128)S(1)}, bf16[8,2048]{1,0:T(8,128)(2,1)S(1)}) custom-call(bf16[192,2048]{1,0:T(8,128)(2,1)} %q.7, bf16[24,2048]{1,0:T(8,128)(2,1)S(1)} %collective-permute-done.tails, f32[8,2048]{1,0:T(8,128)S(1)} %get-tuple-element.36.sums, bf16[192,2048]{1,0:T(8,128)(2,1)} %g.7, ...), custom_call_target="tpu_custom_call" | custom-call | flops 2000000000 | bytes 8000000 | tf_op jit(solution)/shard_map/fifth/pallas_call | solution.py:580
  42.5 0.0 collective-permute-done.4.refs_0_
  42.5 2.5 %collective-permute-start.5 = (bf16[24,1024]{1,0:T(8,128)(2,1)S(1)}, bf16[24,1024]{1,0:T(8,128)(2,1)S(1)}, u32[]{:S(2)}, u32[]{:S(2)}) collective-permute-start(bf16[24,1024]{1,0:T(8,128)(2,1)S(1)} %get-tuple-element.58), channel_id=1, source_target_pairs={{0,2},{2,0},{4,6},{6,4},{8,10},{10,8},{12,14},{14,12},{16,18},{18,... | collective-permute-start | bytes 147464 | tf_op jit(solution)/shard_map/ppermute | solution.py:392
  45.1 2.1 %collective-permute-done.5 = bf16[24,1024]{1,0:T(8,128)(2,1)S(1)} collective-permute-done((bf16[24,1024]{1,0:T(8,128)(2,1)S(1)}, bf16[24,1024]{1,0:T(8,128)(2,1)S(1)}, u32[]{:S(2)}, u32[]{:S(2)}) %collective-permute-start.5) | collective-permute-done | bytes 49184 | tf_op jit(solution)/shard_map/ppermute | solution.py:392
  47.2 2.7 %collective-permute-start.6 = (bf16[40,1024]{1,0:T(8,128)(2,1)S(1)}, bf16[40,1024]{1,0:T(8,128)(2,1)S(1)}, u32[]{:S(2)}, u32[]{:S(2)}) collective-permute-start(bf16[40,1024]{1,0:T(8,128)(2,1)S(1)} %pad_maximum_fusion), channel_id=1, source_target_pairs={{0,16},{2,18},{4,20},{6,22},{8,24},{10,26},{12,28},{14,30},{16,0},... | collective-permute-start | bytes 245768 | tf_op jit(solution)/shard_map/ppermute | solution.py:392
  49.8 2.8 %collective-permute-done.6 = bf16[40,1024]{1,0:T(8,128)(2,1)S(1)} collective-permute-done((bf16[40,1024]{1,0:T(8,128)(2,1)S(1)}, bf16[40,1024]{1,0:T(8,128)(2,1)S(1)}, u32[]{:S(2)}, u32[]{:S(2)}) %collective-permute-start.6) | collective-permute-done | bytes 81952 | tf_op jit(solution)/shard_map/ppermute | solution.py:392
  52.7 1.6 %collective-permute-start.7 = (bf16[40,1024]{1,0:T(8,128)(2,1)S(1)}, bf16[40,1024]{1,0:T(8,128)(2,1)S(1)}, u32[]{:S(2)}, u32[]{:S(2)}) collective-permute-start(bf16[40,1024]{1,0:T(8,128)(2,1)S(1)} %fusion.1), channel_id=1, source_target_pairs={{0,8},{2,10},{4,12},{6,14},{8,0},{10,2},{12,4},{14,6},{16,24},{18,... | collective-permute-start | bytes 245768 | tf_op jit(solution)/shard_map/ppermute | solution.py:392
  54.2 2.9 %collective-permute-done.7 = bf16[40,1024]{1,0:T(8,128)(2,1)S(1)} collective-permute-done((bf16[40,1024]{1,0:T(8,128)(2,1)S(1)}, bf16[40,1024]{1,0:T(8,128)(2,1)S(1)}, u32[]{:S(2)}, u32[]{:S(2)}) %collective-permute-start.7) | collective-permute-done | bytes 81952 | tf_op jit(solution)/shard_map/ppermute | solution.py:392
  57.2 9.5 %collective-permute-start.8 = (bf16[40,1024]{1,0:T(8,128)(2,1)S(1)}, bf16[40,1024]{1,0:T(8,128)(2,1)S(1)}, u32[]{:S(2)}, u32[]{:S(2)}) collective-permute-start(bf16[40,1024]{1,0:T(8,128)(2,1)S(1)} %fusion), channel_id=1, source_target_pairs={{0,4},{2,6},{4,0},{6,2},{8,12},{10,14},{12,8},{14,10},{16,20},{18,... | collective-permute-start | bytes 245768 | tf_op jit(solution)/shard_map/ppermute | solution.py:392
  66.7 3.5 %fourth.1 = (bf16[192,2048]{1,0:T(8,128)(2,1)}, bf16[192,2048]{1,0:T(8,128)(2,1)}, bf16[192,2048]{1,0:T(8,128)(2,1)}) custom-call(bf16[208,2048]{1,0:T(8,128)(2,1)S(1)} %get-tuple-element.47.gk, bf16[208,2048]{1,0:T(8,128)(2,1)S(1)} %get-tuple-element.48.gv, f32[16,2048]{1,0:T(8,128)S(1)} %get-tuple-element.40.near.following, ...), custom_call_target="tpu_custom_call", output_to_operand_aliasing={{2}: (5, {})} | custom-call | flops 4000000000 | bytes 10000000 | tf_op jit(solution)/shard_map/fourth/pallas_call | solution.py:550
  70.1 0.0 collective-permute-done.8
  70.2 0.4 collective-permute-start.9
  70.6 2.2 %sixth.1 = bf16[192,2048]{1,0:T(8,128)(2,1)} custom-call(bf16[128,2048]{1,0:T(8,128)(2,1)S(1)} %get-tuple-element.39.grad, f32[16,2048]{1,0:T(8,128)S(1)} %get-tuple-element.40.near.following, f32[3,7,2048]{2,1,0:T(8,128)} %w.11, bf16[192,2048]{1,0:T(8,128)(2,1)} %get-tuple-element.51.gq_in), custom_call_target="tpu_custom_call", output_to_operand_aliasing={{}: (3, {})} | custom-call | flops 2000000000 | bytes 3000000 | tf_op jit(solution)/shard_map/sixth/pallas_call | solution.py:594
  72.8 1.9 %collective-permute-done.9.other = bf16[40,1024]{1,0:T(8,128)(2,1)S(1)} collective-permute-done((bf16[40,1024]{1,0:T(8,128)(2,1)S(1)}, bf16[40,1024]{1,0:T(8,128)(2,1)S(1)}, u32[]{:S(2)}, u32[]{:S(2)}) %collective-permute-start.9) | collective-permute-done | bytes 81952 | tf_op jit(solution)/shard_map/ppermute | solution.py:392
  74.7 0.7 finish.1
  (9 shorter events, 0.2 us)
Async XLA Ops:
  0.6 6.9 %copy-start = (f32[128,128]{1,0:T(8,128)S(1)}, f32[128,128]{1,0:T(8,128)}, u32[]{:S(2)}) copy-start(f32[128,128]{1,0:T(8,128)} %own_taps.1) | copy-start | bytes 196612
  2.6 7.1 %collective-permute-start = (bf16[24,2048]{1,0:T(8,128)(2,1)S(1)}, bf16[24,2048]{1,0:T(8,128)(2,1)S(1)}, u32[]{:S(2)}, u32[]{:S(2)}) collective-permute-start(bf16[24,2048]{1,0:T(8,128)(2,1)S(1)} %get-tuple-element.34.ends), channel_id=1, source_target_pairs={{0,2},{2,4},{4,6},{6,8},{8,10},{10,12},{12,14},{14,16},{16,18},{18... | collective-permute-start | bytes 294920 | tf_op jit(solution)/shard_map/ppermute | solution.py:379
  7.5 11.0 %collective-permute-start.1 = (bf16[128,128]{1,0:T(8,128)(2,1)S(1)}, bf16[128,128]{1,0:T(8,128)(2,1)S(1)}, u32[]{:S(2)}, u32[]{:S(2)}) collective-permute-start(bf16[128,128]{1,0:T(8,128)(2,1)S(1)} %convert_element_type.27), channel_id=1, source_target_pairs={{0,1},{1,0},{2,3},{3,2},{4,5},{5,4},{6,7},{7,6},{8,9},{9,8},{10,11... | collective-permute-start | bytes 98312 | tf_op jit(solution)/shard_map/ppermute | solution.py:385
  7.6 19.5 %collective-permute-start.3 = (bf16[160,2048]{1,0:T(8,128)(2,1)S(1)}, bf16[160,2048]{1,0:T(8,128)(2,1)S(1)}, u32[]{:S(2)}, u32[]{:S(2)}) collective-permute-start(bf16[160,2048]{1,0:T(8,128)(2,1)S(1)} %get-tuple-element.41), channel_id=1, source_target_pairs={{2,0},{4,2},{6,4},{8,6},{10,8},{12,10},{14,12},{16,14},{18,16},{20... | collective-permute-start | bytes 1966088 | tf_op jit(solution)/shard_map/ppermute | solution.py:379
  14.2 24.5 %collective-permute-start.2 = (bf16[128,2048]{1,0:T(8,128)(2,1)S(1)}, bf16[128,2048]{1,0:T(8,128)(2,1)S(1)}, u32[]{:S(2)}, u32[]{:S(2)}) collective-permute-start(bf16[128,2048]{1,0:T(8,128)(2,1)S(1)} %get-tuple-element.37), channel_id=1, source_target_pairs={{0,2},{2,4},{4,6},{6,8},{8,10},{10,12},{12,14},{14,16},{16,18},{18... | collective-permute-start | bytes 1572872 | tf_op jit(solution)/shard_map/ppermute | solution.py:379
  34.9 7.6 %collective-permute-start.4 = (bf16[128,128]{1,0:T(8,128)(2,1)S(1)}, bf16[128,128]{1,0:T(8,128)(2,1)S(1)}, u32[]{:S(2)}, u32[]{:S(2)}) collective-permute-start(bf16[128,128]{1,0:T(8,128)(2,1)S(1)} %get-tuple-element.56), channel_id=1, source_target_pairs={{0,1},{1,0},{2,3},{3,2},{4,5},{5,4},{6,7},{7,6},{8,9},{9,8},{10,11... | collective-permute-start | bytes 98312 | tf_op jit(solution)/shard_map/ppermute | solution.py:385
  42.5 4.6 %collective-permute-start.5 = (bf16[24,1024]{1,0:T(8,128)(2,1)S(1)}, bf16[24,1024]{1,0:T(8,128)(2,1)S(1)}, u32[]{:S(2)}, u32[]{:S(2)}) collective-permute-start(bf16[24,1024]{1,0:T(8,128)(2,1)S(1)} %get-tuple-element.58), channel_id=1, source_target_pairs={{0,2},{2,0},{4,6},{6,4},{8,10},{10,8},{12,14},{14,12},{16,18},{18,... | collective-permute-start | bytes 147464 | tf_op jit(solution)/shard_map/ppermute | solution.py:392
  47.2 5.5 %collective-permute-start.6 = (bf16[40,1024]{1,0:T(8,128)(2,1)S(1)}, bf16[40,1024]{1,0:T(8,128)(2,1)S(1)}, u32[]{:S(2)}, u32[]{:S(2)}) collective-permute-start(bf16[40,1024]{1,0:T(8,128)(2,1)S(1)} %pad_maximum_fusion), channel_id=1, source_target_pairs={{0,16},{2,18},{4,20},{6,22},{8,24},{10,26},{12,28},{14,30},{16,0},... | collective-permute-start | bytes 245768 | tf_op jit(solution)/shard_map/ppermute | solution.py:392
  52.7 4.5 %collective-permute-start.7 = (bf16[40,1024]{1,0:T(8,128)(2,1)S(1)}, bf16[40,1024]{1,0:T(8,128)(2,1)S(1)}, u32[]{:S(2)}, u32[]{:S(2)}) collective-permute-start(bf16[40,1024]{1,0:T(8,128)(2,1)S(1)} %fusion.1), channel_id=1, source_target_pairs={{0,8},{2,10},{4,12},{6,14},{8,0},{10,2},{12,4},{14,6},{16,24},{18,... | collective-permute-start | bytes 245768 | tf_op jit(solution)/shard_map/ppermute | solution.py:392
  57.2 12.9 %collective-permute-start.8 = (bf16[40,1024]{1,0:T(8,128)(2,1)S(1)}, bf16[40,1024]{1,0:T(8,128)(2,1)S(1)}, u32[]{:S(2)}, u32[]{:S(2)}) collective-permute-start(bf16[40,1024]{1,0:T(8,128)(2,1)S(1)} %fusion), channel_id=1, source_target_pairs={{0,4},{2,6},{4,0},{6,2},{8,12},{10,14},{12,8},{14,10},{16,20},{18,... | collective-permute-start | bytes 245768 | tf_op jit(solution)/shard_map/ppermute | solution.py:392
  70.2 4.5 %collective-permute-start.9 = (bf16[40,1024]{1,0:T(8,128)(2,1)S(1)}, bf16[40,1024]{1,0:T(8,128)(2,1)S(1)}, u32[]{:S(2)}, u32[]{:S(2)}) collective-permute-start(bf16[40,1024]{1,0:T(8,128)(2,1)S(1)} %get-tuple-element.63), channel_id=1, source_target_pairs={{0,2},{2,0},{4,6},{6,4},{8,10},{10,8},{12,14},{14,12},{16,18},{18,... | collective-permute-start | bytes 245768 | tf_op jit(solution)/shard_map/ppermute | solution.py:392
